TPU v7x, 32 devices: a whole 2x2x4 slice. The times are simulated.
32 devices in a mesh: dp: 8 (over y, x, core), mp: 4 (over z).
Axes of the slice: x: 2, y: 2, z: 4, core: 2. Of those that a mesh axis runs over, the one named last changes fastest.
Arguments:
- points: bfloat16 [8192, 1024], P(('dp', 'mp')), may hold values from -6 to 6
- members: int32 [32, 256], P(('dp', 'mp')), may hold values from -1 to 255, as said below
- cotangent: bfloat16 [8192, 1024], P(('dp', 'mp')), may hold values from -6 to 6
- project_weight: bfloat16 [1024, 3, 1024], P(None, None, 'mp'), may hold values from -0.1875 to 0.1875
- output_weight: bfloat16 [1024, 1024], P('mp'), may hold values from -1.5 to 1.5
- upward_weight: bfloat16 [1024, 4096], P(None, 'mp'), may hold values from -0.1875 to 0.1875
- downward_weight: bfloat16 [4096, 1024], P('mp'), may hold values from -0.09375 to 0.09375
- layer_norms: float32 [4, 1024], replicated, may hold values from -0.9 to 1.75
- project_master: float32 [1024, 3, 1024], P('dp', None, 'mp'), may hold values from -0.1875 to 0.1875
- project_first: float32 [1024, 3, 1024], P('dp', None, 'mp'), may hold values from -96 to 96
- project_second: float32 [1024, 3, 1024], P('dp', None, 'mp'), may hold values from 966.656 to 3874.816
- output_master: float32 [1024, 1024], P('mp', 'dp'), may hold values from -1.5 to 1.5
- output_first: float32 [1024, 1024], P('mp', 'dp'), may hold values from -6 to 6
- output_second: float32 [1024, 1024], P('mp', 'dp'), may hold values from 6.22592 to 24.82176
- upward_master: float32 [1024, 4096], P('dp', 'mp'), may hold values from -0.1875 to 0.1875
- upward_first: float32 [1024, 4096], P('dp', 'mp'), may hold values from -16 to 16
- upward_second: float32 [1024, 4096], P('dp', 'mp'), may hold values from 38.5024 to 155.648
- downward_master: float32 [4096, 1024], P('mp', 'dp'), may hold values from -0.09375 to 0.09375
- downward_first: float32 [4096, 1024], P('mp', 'dp'), may hold values from -28 to 28
- downward_second: float32 [4096, 1024], P('mp', 'dp'), may hold values from 87.6544 to 352.256
- norm_first: float32 [4, 1024], P(None, 'dp'), may hold values from -64 to 64
- norm_second: float32 [4, 1024], P(None, 'dp'), may hold values from 430.8992 to 1720.32
Outputs:
- latents: float32 [8192, 1024], P(('dp', 'mp'))
- point_gradient: float32 [8192, 1024], P(('dp', 'mp'))
- project_gradient: float32 [1024, 3, 1024], P('dp', None, 'mp')
- project_updated: float32 [1024, 3, 1024], P('dp', None, 'mp')
- project_moment_one: float32 [1024, 3, 1024], P('dp', None, 'mp')
- project_moment_two: float32 [1024, 3, 1024], P('dp', None, 'mp')
- project_copy: bfloat16 [1024, 3, 1024], P('dp', None, 'mp')
- output_gradient: float32 [1024, 1024], P('mp', 'dp')
- output_updated: float32 [1024, 1024], P('mp', 'dp')
- output_moment_one: float32 [1024, 1024], P('mp', 'dp')
- output_moment_two: float32 [1024, 1024], P('mp', 'dp')
- output_copy: bfloat16 [1024, 1024], P('mp', 'dp')
- upward_gradient: float32 [1024, 4096], P('dp', 'mp')
- upward_updated: float32 [1024, 4096], P('dp', 'mp')
- upward_moment_one: float32 [1024, 4096], P('dp', 'mp')
- upward_moment_two: float32 [1024, 4096], P('dp', 'mp')
- upward_copy: bfloat16 [1024, 4096], P('dp', 'mp')
- downward_gradient: float32 [4096, 1024], P('mp', 'dp')
- downward_updated: float32 [4096, 1024], P('mp', 'dp')
- downward_moment_one: float32 [4096, 1024], P('mp', 'dp')
- downward_moment_two: float32 [4096, 1024], P('mp', 'dp')
- downward_copy: bfloat16 [4096, 1024], P('mp', 'dp')
- norm_gradient: float32 [4, 1024], P(None, 'dp')
- norm_updated: float32 [4, 1024], P(None, 'dp')
- norm_moment_one: float32 [4, 1024], P(None, 'dp')
- norm_moment_two: float32 [4, 1024], P(None, 'dp')
Inputs may be any that keep to these rules, and one draw needn't show every extreme that they name: members[g, j] names row g * 256 + members[g, j] of points, or is -1 for a padded slot; in each row every value of 0 to 255 stands at most once, and at most 64 entries are -1.
All inputs are finite; a program needn't handle non-finite values.
Results may differ from a plain program's by a relative error of at most 0.014.
The roundings to bfloat16 on the way count: a program that leaves them out, or rounds other values in their place, can miss the bound.
Values may be sent and summed in bfloat16 or wider, within the bound.
A program may use at most 128 MiB of HBM per device.

v0:
```python
import functools

import jax
import jax.numpy as jnp
from jax import lax
from jax.experimental import pallas as pl
from jax.experimental.pallas import tpu as pltpu
from jax.sharding import PartitionSpec as P

D = 1024
HEAD_DIM = 128
FF = 4096
LAT = 256
ADAM_STEP = 10


norm_epsilon = 1e-05
beta_one = 0.9
beta_two = 0.95
adam_epsilon = 1e-08
weight_decay = 0.1
masked_score = -1e30


def layer_norm(values, norm_gain, norm_shift):
    center = values - jnp.mean(values, axis=-1, keepdims=True)
    spread = jnp.mean(center * center, axis=-1, keepdims=True)
    return center * lax.rsqrt(spread + norm_epsilon) * norm_gain + norm_shift


def pick_rows(source_rows, row_index):
    return source_rows[row_index]


def adamw_step(weight, gradient, moment_one, moment_two, step_rate):
    one_new = beta_one * moment_one + (1.0 - beta_one) * gradient
    two_new = beta_two * moment_two + (1.0 - beta_two) * gradient * gradient
    corrected_one = one_new / (1.0 - beta_one**ADAM_STEP)
    corrected_two = two_new / (1.0 - beta_two**ADAM_STEP)
    updated = weight - step_rate * (
        corrected_one / (jnp.sqrt(corrected_two) + adam_epsilon) + weight_decay * weight
    )
    return (updated, one_new, two_new)


def masked_scores(queries, keys_all, key_mask, score_scale):
    raw_scores = (
        jnp.einsum("gqhe,gkhe->ghqk", queries, keys_all, preferred_element_type=jnp.float32)
        * score_scale
    )
    return jnp.where(key_mask, raw_scores, masked_score)


def on_device_any(
    points,
    members,
    cotangent,
    project_weight,
    output_weight,
    upward_weight,
    downward_weight,
    layer_norms,
    project_master,
    project_first,
    project_second,
    output_master,
    output_first,
    output_second,
    upward_master,
    upward_first,
    upward_second,
    downward_master,
    downward_first,
    downward_second,
    norm_first,
    norm_second,
):
    groups_here = members.shape[0]
    shard_rows = points.shape[0]
    model_width = points.shape[1]
    heads_here = project_weight.shape[2] // HEAD_DIM
    score_scale = HEAD_DIM ** (-0.5)
    grouped = points.reshape(groups_here, LAT, model_width)
    slot_index = jnp.maximum(members, 0)
    key_live = members >= 0
    picked = jax.vmap(pick_rows)(grouped, slot_index)
    inputs = jnp.where(key_live[:, :, None], picked.astype(jnp.float32), 0.0).reshape(
        shard_rows, model_width
    )
    normed, norm_back_one = jax.vjp(layer_norm, inputs, layer_norms[0], layer_norms[1])
    gathered, live_all = (
        lax.all_gather(normed.astype(jnp.bfloat16), "mp", axis=0, tiled=True),
        lax.all_gather(key_live.astype(jnp.bfloat16), "mp", axis=0, tiled=True),
    )
    total_rows = gathered.shape[0]
    total_groups = live_all.shape[0]
    key_mask = (live_all > 0)[:, None, None, :]
    projected = jnp.einsum(
        "rd,dcf->rcf", gathered, project_weight, preferred_element_type=jnp.float32
    ).astype(jnp.bfloat16)
    heads_view = projected.reshape(total_groups, LAT, 3, heads_here, HEAD_DIM)
    queries = heads_view[:, :, 0]
    keys_all = heads_view[:, :, 1]
    values_all = heads_view[:, :, 2]
    scores = masked_scores(queries, keys_all, key_mask, score_scale)
    row_top = jnp.max(scores, axis=-1, keepdims=True)
    exponent = jnp.exp(scores - row_top)
    row_total = jnp.sum(exponent, axis=-1, keepdims=True)
    attention_weights = exponent / row_total
    log_total = row_top + jnp.log(row_total)
    weights_low = attention_weights.astype(jnp.bfloat16)
    attended = jnp.einsum(
        "ghqk,gkhe->gqhe", weights_low, values_all, preferred_element_type=jnp.float32
    ).astype(jnp.bfloat16)
    attended = attended.reshape(total_rows, heads_here * HEAD_DIM)
    branch = lax.psum_scatter(
        jnp.dot(attended, output_weight, preferred_element_type=jnp.float32),
        "mp",
        scatter_dimension=0,
        tiled=True,
    )
    residual = inputs + branch
    normed_two, norm_back_two = jax.vjp(layer_norm, residual, layer_norms[2], layer_norms[3])
    gathered_two = lax.all_gather(normed_two.astype(jnp.bfloat16), "mp", axis=0, tiled=True)
    upward = jnp.dot(gathered_two, upward_weight, preferred_element_type=jnp.float32)
    activated_float, gelu_back = jax.vjp(jax.nn.gelu, upward)
    activated = activated_float.astype(jnp.bfloat16)
    latents = residual + lax.psum_scatter(
        jnp.dot(activated, downward_weight, preferred_element_type=jnp.float32).astype(
            jnp.bfloat16
        ),
        "mp",
        scatter_dimension=0,
        tiled=True,
    ).astype(jnp.float32)
    cotangent_all = lax.all_gather(cotangent, "mp", axis=0, tiled=True)
    downward_local = jnp.einsum(
        "rf,rd->fd", activated, cotangent_all, preferred_element_type=jnp.float32
    )
    activated_grad = jnp.einsum(
        "rd,fd->rf", cotangent_all, downward_weight, preferred_element_type=jnp.float32
    )
    upward_grad = gelu_back(activated_grad)[0].astype(jnp.bfloat16)
    upward_local = jnp.einsum(
        "rd,rf->df", gathered_two, upward_grad, preferred_element_type=jnp.float32
    )
    normed_two_grad = lax.psum_scatter(
        jnp.einsum("rf,df->rd", upward_grad, upward_weight, preferred_element_type=jnp.float32),
        "mp",
        scatter_dimension=0,
        tiled=True,
    )
    residual_part, gain_two_grad, shift_two_grad = norm_back_two(normed_two_grad)
    residual_grad = residual_part + cotangent.astype(jnp.float32)
    norm_two_local = jnp.stack([gain_two_grad, shift_two_grad])
    branch_grad = lax.all_gather(residual_grad.astype(jnp.bfloat16), "mp", axis=0, tiled=True)
    output_local = jnp.einsum(
        "rh,rd->hd", attended, branch_grad, preferred_element_type=jnp.float32
    )
    attended_grad = jnp.einsum(
        "rd,hd->rh", branch_grad, output_weight, preferred_element_type=jnp.float32
    ).astype(jnp.bfloat16)
    attended_grad = attended_grad.reshape(total_groups, LAT, heads_here, HEAD_DIM)
    scores_again = masked_scores(queries, keys_all, key_mask, score_scale)
    weights_again = jnp.exp(scores_again - log_total)
    weights_again_low = weights_again.astype(jnp.bfloat16)
    value_grad = jnp.einsum(
        "ghqk,gqhe->gkhe", weights_again_low, attended_grad, preferred_element_type=jnp.float32
    ).astype(jnp.bfloat16)
    weight_grad = jnp.einsum(
        "gqhe,gkhe->ghqk", attended_grad, values_all, preferred_element_type=jnp.float32
    )
    score_grad = (
        weights_again * (weight_grad - jnp.sum(weights_again * weight_grad, axis=-1, keepdims=True))
    ).astype(jnp.bfloat16)
    query_grad = (
        jnp.einsum("ghqk,gkhe->gqhe", score_grad, keys_all, preferred_element_type=jnp.float32)
        * score_scale
    ).astype(jnp.bfloat16)
    key_grad = (
        jnp.einsum("ghqk,gqhe->gkhe", score_grad, queries, preferred_element_type=jnp.float32)
        * score_scale
    ).astype(jnp.bfloat16)
    projected_grad = jnp.stack([query_grad, key_grad, value_grad], axis=2).reshape(
        total_rows, 3, heads_here * HEAD_DIM
    )
    project_local = jnp.einsum(
        "rd,rcf->dcf", gathered, projected_grad, preferred_element_type=jnp.float32
    )
    normed_grad = lax.psum_scatter(
        jnp.einsum(
            "rcf,dcf->rd", projected_grad, project_weight, preferred_element_type=jnp.float32
        ).astype(jnp.bfloat16),
        "mp",
        scatter_dimension=0,
        tiled=True,
    ).astype(jnp.float32)
    input_part, gain_one_grad, shift_one_grad = norm_back_one(normed_grad)
    input_grad = input_part + residual_grad
    norm_one_local = jnp.stack([gain_one_grad, shift_one_grad])
    matches = members[:, :, None] == jnp.arange(LAT, dtype=jnp.int32)[None, None, :]
    slot_of = jnp.argmax(matches, axis=1)
    point_used = jnp.any(matches, axis=1)
    grouped_grad = input_grad.reshape(groups_here, LAT, model_width)
    point_gradient = jnp.where(
        point_used[:, :, None], jax.vmap(pick_rows)(grouped_grad, slot_of), 0.0
    ).reshape(shard_rows, model_width)
    (
        project_summed,
        output_summed,
        upward_summed,
        downward_summed,
        norm_one_summed,
        norm_two_summed,
    ) = (
        lax.psum_scatter(project_local, "dp", scatter_dimension=0, tiled=True),
        lax.psum_scatter(output_local, "dp", scatter_dimension=1, tiled=True),
        lax.psum_scatter(upward_local, "dp", scatter_dimension=0, tiled=True),
        lax.psum_scatter(downward_local, "dp", scatter_dimension=1, tiled=True),
        lax.psum_scatter(norm_one_local, "dp", scatter_dimension=1, tiled=True),
        lax.psum_scatter(norm_two_local, "dp", scatter_dimension=1, tiled=True),
    )
    norm_gradient = lax.psum(jnp.concatenate([norm_one_summed, norm_two_summed], axis=0), "mp")
    data_index = lax.axis_index("dp")
    norm_columns = norm_first.shape[1]
    norm_current = lax.dynamic_slice_in_dim(layer_norms, data_index * norm_columns, norm_columns, 1)
    project_new = adamw_step(
        project_master, project_summed, project_first, project_second, D ** (-0.5)
    )
    output_new = adamw_step(
        output_master, output_summed, output_first, output_second, max(1, D * 4 // LAT) ** (-0.5)
    )
    upward_new = adamw_step(upward_master, upward_summed, upward_first, upward_second, D ** (-0.5))
    downward_new = adamw_step(
        downward_master, downward_summed, downward_first, downward_second, FF ** (-0.5)
    )
    norm_new = adamw_step(norm_current, norm_gradient, norm_first, norm_second, 0.2)
    return (
        latents,
        point_gradient,
        project_summed,
        project_new[0],
        project_new[1],
        project_new[2],
        project_new[0].astype(jnp.bfloat16),
        output_summed,
        output_new[0],
        output_new[1],
        output_new[2],
        output_new[0].astype(jnp.bfloat16),
        upward_summed,
        upward_new[0],
        upward_new[1],
        upward_new[2],
        upward_new[0].astype(jnp.bfloat16),
        downward_summed,
        downward_new[0],
        downward_new[1],
        downward_new[2],
        downward_new[0].astype(jnp.bfloat16),
        norm_gradient,
        norm_new[0],
        norm_new[1],
        norm_new[2],
    )


MESH = pl.DeviceIdType.MESH
PLANES = 4
OWNERS = 8
ROWS = LAT
HALVES = (0, 1)
SHARDS = ((3, D, 256), (256, D), (D, D), (D, D))


def place():
    dp = lax.axis_index("dp")
    return dp // 4, (dp // 2) % 2, dp % 2, lax.axis_index("mp")


def device(y, x, c, z):
    return (y * 4 + x * 2 + c, z)


def greet(y, x, c, z):
    barrier = pltpu.get_barrier_semaphore()
    partners = [device(1 - y, x, c, z), device(y, 1 - x, c, z), device(y, x, 1 - c, z)]
    partners += [device(y, x, c, (z + d) % PLANES) for d in (1, 2, 3)]
    for partner in partners:
        pl.semaphore_signal(barrier, inc=1, device_id=partner, device_id_type=MESH)
    pl.semaphore_wait(barrier, len(partners))


def arrival(z, k):
    return (z + 1 - 2 * (z % 2), 2 - z // 2, 3 - 3 * (z // 2))[k]


def dot(a, b, contract):
    return lax.dot_general(a, b, (contract, ((), ())), preferred_element_type=jnp.float32)


NN = ((1,), (0,))
NT = ((1,), (1,))
TN = ((0,), (0,))


def tiles(count, size, body):
    def step(n, carry):
        body(pl.ds(pl.multiple_of(n * size, size), size))
        return carry

    lax.fori_loop(0, count, step, 0)


def norm_rows(source, target, gain, shift, strip=64):
    def step(n, carry):
        rows = pl.ds(pl.multiple_of(n * strip, strip), strip)
        target[rows, :] = layer_norm(source[rows, :], gain, shift).astype(target.dtype)
        return carry

    lax.fori_loop(0, ROWS // strip, step, 0)


def forward_kernel(*refs):
    shards, (points, members, norms) = refs[0:4], refs[4:7]
    fulls_out, saved_out, latents_out = refs[7:11], refs[11:19], refs[19]
    fulls, saved, latents = refs[20:24], refs[24:32], refs[32]
    inputs, entering_one, projected, attended, residual, entering_two, activated, slope = saved
    own_sem, z_send, z_recv, a_send, a_recv, b_send, b_recv, c_send, c_recv = refs[33:42]
    weight_sem, saved_sem, latents_sem = refs[42:45]
    y, x, c, z = place()
    greet(y, x, c, z)
    is_mid = jnp.logical_or(z == 1, z == 2)
    sibling = device(y, x, 1 - c, z)
    over_x, over_y = device(y, 1 - x, c, z), device(1 - y, x, c, z)
    beside, across = device(y, x, c, arrival(z, 0)), device(y, x, c, 3 - z)

    def view(w, plane, rows):
        return fulls[w].at[plane, :, rows, :] if w == 0 else fulls[w].at[plane, rows, :]

    def block(w, half, first, count):
        height = SHARDS[w][-2]
        start = pl.multiple_of(half * (height // 2) + first * (height // 16), height // 16)
        return pl.ds(start, count * (height // 16))

    spot = (c * 4 + y * 2 + x, c * 4 + x * 2 + y)
    pair = (c * 4 + y * 2, c * 4 + x * 2)

    def remote(w, plane, rows, send, recv, target):
        return pltpu.make_async_remote_copy(
            src_ref=view(w, plane, rows),
            dst_ref=view(w, plane, rows),
            send_sem=send,
            recv_sem=recv,
            device_id=target,
            device_id_type=MESH,
        )

    def z_copy(w, plane, half, lane, k, target):
        rows = block(w, half, spot[half], 1)
        return remote(w, plane, rows, z_send.at[w, lane, half], z_recv.at[w, k, half], target)

    def z_own(w, half):
        return z_copy(w, z, half, 0, 0, beside)

    def z_own_across(w, half):
        return z_copy(w, z, half, 1, 1, across)

    def z_pass(w, k, half):
        lane, target, slot = ((2, across, 2), (3, beside, 1), (4, beside, 2))[k]
        return z_copy(w, arrival(z, k), half, lane, slot, target)

    def z_arrived(w, k, half):
        return z_copy(w, arrival(z, k), half, 0, k, beside)

    def a_copy(w, k, half):
        rows = block(w, half, spot[half], 1)
        return remote(
            w, arrival(z, k), rows, a_send.at[w, k, half], a_recv.at[w, k, half], (over_x, over_y)[half]
        )

    def b_copy(w, k, half):
        rows = block(w, half, pair[half], 2)
        return remote(
            w, arrival(z, k), rows, b_send.at[w, k, half], b_recv.at[w, k, half], (over_y, over_x)[half]
        )

    def c_copy(w, k, half):
        rows = block(w, half, c * 4, 4)
        return remote(w, arrival(z, k), rows, c_send.at[w, k, half], c_recv.at[w, k, half], sibling)

    def own_load(w):
        return pltpu.make_async_copy(shards[w], fulls[w].at[z], own_sem.at[w])

    def keep_weight(w, k):
        plane = z if k is None else arrival(z, k)
        slot = 3 if k is None else k
        return pltpu.make_async_copy(fulls[w].at[plane], fulls_out[w].at[plane], weight_sem.at[w, slot])

    def keep(n):
        return pltpu.make_async_copy(saved[n], saved_out[n], saved_sem.at[n])

    def enter():
        slot_of = lax.broadcasted_iota(jnp.int32, (ROWS, ROWS), 0) == members[...]
        chosen = slot_of.astype(jnp.float32).astype(jnp.bfloat16)

        def pick(columns):
            inputs[:, columns] = dot(chosen, points[:, columns], TN)

        tiles(4, 256, pick)
        norm_rows(inputs, entering_one, norms[0:1, :], norms[1:2, :])
        residual[...] = inputs[...]

    def project(plane):
        for part in range(3):
            projected[plane, part] = dot(entering_one[...], fulls[0][plane, part], NN).astype(jnp.bfloat16)

    def attend(plane):
        live = members[...] >= 0
        for head in range(2):
            span = slice(head * HEAD_DIM, (head + 1) * HEAD_DIM)
            queries, keys_all, values_all = (projected[plane, part, :, span] for part in range(3))
            scores = jnp.where(live, dot(queries, keys_all, NT) * HEAD_DIM ** (-0.5), masked_score)
            exponent = jnp.exp(scores - jnp.max(scores, axis=-1, keepdims=True))
            probs = exponent * (1.0 / jnp.sum(exponent, axis=-1, keepdims=True))
            attended[plane, :, span] = dot(probs.astype(jnp.bfloat16), values_all, NN).astype(jnp.bfloat16)

    def branch(plane):
        def body(columns):
            residual[:, columns] += dot(attended[plane], fulls[1][plane, :, columns], NN)

        tiles(4, 256, body)

    def enter_two():
        norm_rows(residual, entering_two, norms[2:3, :], norms[3:4, :])
        latents[...] = residual[...]

    def widen(plane):
        def body(columns):
            u = dot(entering_two[...], fulls[2][plane, :, columns], NN)
            square = u * u
            bend = jnp.tanh(0.7978845608028654 * u * (1.0 + 0.044715 * square))
            activated[plane, :, columns] = (0.5 * u * (1.0 + bend)).astype(jnp.bfloat16)
            slope[plane, :, columns] = 0.5 * (1.0 + bend) + 0.5 * u * (1.0 - bend * bend) * (
                0.7978845608028654 * (1.0 + 3.0 * 0.044715 * square)
            )

        tiles(4, 256, body)

    def narrow(plane):
        def body(columns):
            latents[:, columns] += dot(activated[plane], fulls[3][plane, :, columns], NN)

        tiles(4, 256, body)

    def compute(w, k):
        plane = z if k is None else arrival(z, k)
        if w == 0:
            project(plane)
            attend(plane)
        elif w == 1:
            branch(plane)
        elif w == 2:
            widen(plane)
        else:
            narrow(plane)

    chunks = [(w, k) for w in range(4) for k in range(3)]
    lag = (1, 3, 5, 7)

    for w in range(4):
        own_load(w).start()
    for step in range(len(chunks) + lag[3]):
        for w in range(4):
            if step == max(0, 3 * w - 3):
                own_load(w).wait()
                keep_weight(w, None).start()
                for half in HALVES:
                    z_own(w, half).start()

                @pl.when(is_mid)
                def _():
                    for half in HALVES:
                        z_own_across(w, half).start()

        if 0 <= step - lag[0] < len(chunks):
            w, k = chunks[step - lag[0]]
            for half in HALVES:
                z_arrived(w, k, half).wait_recv()
                a_copy(w, k, half).start()

            @pl.when(is_mid)
            def _():
                for half in HALVES:
                    z_pass(w, k, half).start()

        if 0 <= step - lag[1] < len(chunks):
            w, k = chunks[step - lag[1]]
            for half in HALVES:
                a_copy(w, k, half).wait_recv()
                b_copy(w, k, half).start()
        if 0 <= step - lag[2] < len(chunks):
            w, k = chunks[step - lag[2]]
            for half in HALVES:
                b_copy(w, k, half).wait_recv()
                c_copy(w, k, half).start()
        if step == 0:
            enter()
            keep(0).start()
            keep(1).start()
            compute(0, None)
        if 0 <= step - lag[3] < len(chunks):
            w, k = chunks[step - lag[3]]
            for half in HALVES:
                c_copy(w, k, half).wait_recv()
            keep_weight(w, k).start()
            if k == 0 and w > 0:
                compute(w, None)
            compute(w, k)
            if k == 2:
                if w == 0:
                    keep(2).start()
                    keep(3).start()
                elif w == 1:
                    keep(4).start()
                    enter_two()
                    keep(5).start()
                elif w == 2:
                    keep(6).start()
                    keep(7).start()
    out = pltpu.make_async_copy(latents, latents_out, latents_sem)
    out.start()
    for w in range(4):
        for half in HALVES:
            z_own(w, half).wait_send()
            for k in range(3):
                a_copy(w, k, half).wait_send()
                b_copy(w, k, half).wait_send()
                c_copy(w, k, half).wait_send()

    @pl.when(is_mid)
    def _():
        for w in range(4):
            for half in HALVES:
                z_own_across(w, half).wait_send()
                for k in range(3):
                    z_pass(w, k, half).wait_send()

    for w in range(4):
        for k in (None, 0, 1, 2):
            keep_weight(w, k).wait()
    for n in range(8):
        keep(n).wait()
    out.wait()


def run_forward(shards, points, members, layer_norms):
    f32, bf16 = jnp.float32, jnp.bfloat16
    saved = [
        ((ROWS, D), f32),
        ((ROWS, D), bf16),
        ((PLANES, 3, ROWS, 256), bf16),
        ((PLANES, ROWS, 256), bf16),
        ((ROWS, D), f32),
        ((ROWS, D), bf16),
        ((PLANES, ROWS, D), bf16),
        ((PLANES, ROWS, D), f32),
    ]
    anywhere, vmem = pl.BlockSpec(memory_space=pl.ANY), pl.BlockSpec(memory_space=pltpu.VMEM)
    fulls = [((PLANES,) + s, bf16) for s in SHARDS]
    dma = pltpu.SemaphoreType.DMA
    result = pl.pallas_call(
        forward_kernel,
        out_shape=[jax.ShapeDtypeStruct(*a) for a in fulls + saved + [((ROWS, D), f32)]],
        in_specs=[anywhere] * 4 + [vmem] * 3,
        out_specs=[anywhere] * 13,
        scratch_shapes=[pltpu.VMEM(*a) for a in fulls + saved + [((ROWS, D), f32)]]
        + [dma((4,)), dma((4, 5, 2))]
        + [dma((4, 3, 2))] * 7
        + [dma((4, 4)), dma((8,)), dma],
        name="forward",
        compiler_params=pltpu.CompilerParams(
            collective_id=0, has_side_effects=True, vmem_limit_bytes=52 << 20
        ),
    )(*shards, points, members, layer_norms)
    return result[:4], result[4:12], result[12]


BLOCKS = ((1024, 128), (128, 1024), (256, 128), (384, 256))
STRIPS = (128, 16, 128, 64)


def owner_view(ref, w, plane, owner):
    if w in (0, 2):
        return ref.at[plane, :, pl.ds(pl.multiple_of(owner * 128, 128), 128)]
    return ref.at[plane, pl.ds(pl.multiple_of(owner * BLOCKS[w][0], BLOCKS[w][0]), BLOCKS[w][0]), :]


def reduce_kernel(*refs):
    grads, norm_part = refs[0:4], refs[4]
    outs, norm_out = refs[5:9], refs[9]
    own, pair_in, one_in, two_in, z_in = (refs[10 + 4 * k : 14 + 4 * k] for k in range(5))
    norm_own, norm_in, norm_planes = refs[30:33]
    load_sem, c_send, c_recv, one_send, one_recv, two_send, two_recv, z_send, z_recv = refs[33:42]
    norm_send, norm_recv = refs[42:44]
    y, x, c, z = place()
    greet(y, x, c, z)
    sibling = device(y, x, 1 - c, z)
    over_x, over_y = device(y, 1 - x, c, z), device(1 - y, x, c, z)

    def plane_of(i):
        return (z + 1 + i) % PLANES

    def remote(src, dst, send, recv, target):
        return pltpu.make_async_remote_copy(
            src_ref=src, dst_ref=dst, send_sem=send, recv_sem=recv, device_id=target, device_id_type=MESH
        )

    def load(w, i, k):
        return pltpu.make_async_copy(
            owner_view(grads[w], w, plane_of(i), k * 2 + c), own[w].at[i, k // 2, k % 2], load_sem.at[w, i, k]
        )

    def pair_copy(w, i, k):
        return remote(
            owner_view(grads[w], w, plane_of(i), k * 2 + 1 - c),
            pair_in[w].at[i, k // 2, k % 2],
            c_send.at[w, i, k],
            c_recv.at[w, i, k],
            sibling,
        )

    def half_rows(w, half):
        size = BLOCKS[w][0] // 2
        return pl.ds(half * size, size)

    def one_copy(w, i, half):
        rows = half_rows(w, half)
        src = own[w].at[i, 1 - y, :, rows] if half == 0 else own[w].at[i, :, 1 - x, rows]
        return remote(
            src, one_in[w].at[i, half], one_send.at[w, i, half], one_recv.at[w, i, half], (over_y, over_x)[half]
        )

    def two_copy(w, i, half):
        rows = half_rows(w, half)
        src = own[w].at[i, y, 1 - x, rows] if half == 0 else own[w].at[i, 1 - y, x, rows]
        return remote(
            src, two_in[w].at[i, half], two_send.at[w, i, half], two_recv.at[w, i, half], (over_x, over_y)[half]
        )

    def z_copy(w, i):
        return remote(
            own[w].at[i, y, x], z_in[w].at[i], z_send.at[w, i], z_recv.at[w, i], device(y, x, c, plane_of(i))
        )

    def add_rows(target, source, count, strip):
        def body(r, carry):
            rows = pl.ds(pl.multiple_of(r * strip, strip), strip)
            total = target[rows].astype(jnp.float32) + source[rows].astype(jnp.float32)
            target[rows] = total.astype(target.dtype)
            return carry

        lax.fori_loop(0, count // strip, body, 0)

    def start_unit(w, i):
        for k in range(4):
            pair_copy(w, i, k).start()
            load(w, i, k).start()

    def after_pair(w, i):
        for k in range(4):
            load(w, i, k).wait()
            pair_copy(w, i, k).wait_recv()
            add_rows(own[w].at[i, k // 2, k % 2], pair_in[w].at[i, k // 2, k % 2], BLOCKS[w][0], STRIPS[w])
        for half in (0, 1):
            one_copy(w, i, half).start()

    def after_one(w, i):
        size = BLOCKS[w][0] // 2
        for half in (0, 1):
            one_copy(w, i, half).wait()
            rows = half_rows(w, half)
            for k in (0, 1):
                target = own[w].at[i, y, k, rows] if half == 0 else own[w].at[i, k, x, rows]
                add_rows(target, one_in[w].at[i, half, k], size, min(size, STRIPS[w]))
            two_copy(w, i, half).start()

    def after_two(w, i):
        size = BLOCKS[w][0] // 2
        for half in (0, 1):
            two_copy(w, i, half).wait()
            add_rows(own[w].at[i, y, x, half_rows(w, half)], two_in[w].at[i, half], size, min(size, STRIPS[w]))
        if i < PLANES - 1:
            z_copy(w, i).start()

    def finish(w):
        for i in range(PLANES - 1):
            z_copy(w, i).wait()

        def body(r, carry):
            rows = pl.ds(pl.multiple_of(r * STRIPS[w], STRIPS[w]), STRIPS[w])
            total = own[w].at[PLANES - 1, y, x][rows].astype(jnp.float32)
            for i in range(PLANES - 1):
                total = total + z_in[w].at[i][rows].astype(jnp.float32)
            outs[w][rows] = total
            return carry

        lax.fori_loop(0, BLOCKS[w][0] // STRIPS[w], body, 0)

    def norm_step(k):
        return remote(
            norm_own.at[k], norm_in.at[k], norm_send.at[k], norm_recv.at[k], (sibling, over_x, over_y)[k]
        )

    def norm_plane(d):
        return remote(
            norm_own.at[3],
            norm_planes.at[z],
            norm_send.at[2 + d],
            norm_recv.at[2 + d],
            device(y, x, c, (z + d) % PLANES),
        )

    norm_own[0] = norm_part[...]
    norm_step(0).start()

    units = [(w, i) for w in range(4) for i in range(PLANES)]
    ahead = 2
    for unit in units[:ahead]:
        start_unit(*unit)
    for step in range(len(units) + 4):
        if step + ahead < len(units):
            start_unit(*units[step + ahead])
        if step < len(units):
            after_pair(*units[step])
        if 0 <= step - 1 < len(units):
            after_one(*units[step - 1])
        if 0 <= step - 2 < len(units):
            after_two(*units[step - 2])
        if step < 3:
            norm_step(step).wait()
            norm_own[step + 1] = norm_own[step] + norm_in[step]
            if step < 2:
                norm_step(step + 1).start()
            else:
                norm_planes[z] = norm_own[3]
                for d in (1, 2, 3):
                    norm_plane(d).start()
        if step >= 4 and (step - 4) % PLANES == PLANES - 1:
            finish((step - 4) // PLANES)
    for d in (1, 2, 3):
        norm_plane(d).wait()
    norm_out[...] = (norm_planes[0] + norm_planes[1]) + (norm_planes[2] + norm_planes[3])
    for w, i in units:
        for k in range(4):
            pair_copy(w, i, k).wait_send()


def reduce_gradients(grads, norm_part):
    bf16 = jnp.bfloat16
    halves = [(b[0] // 2, b[1]) for b in BLOCKS]
    scratch = [pltpu.VMEM((4, 2, 2) + b, bf16) for b in BLOCKS]
    scratch += [pltpu.VMEM((4, 2, 2) + b, bf16) for b in BLOCKS]
    scratch += [pltpu.VMEM((4, 2, 2) + h, bf16) for h in halves]
    scratch += [pltpu.VMEM((4, 2) + h, bf16) for h in halves]
    scratch += [pltpu.VMEM((3,) + b, bf16) for b in BLOCKS]
    scratch += [
        pltpu.VMEM((4,) + norm_part.shape, jnp.float32),
        pltpu.VMEM((3,) + norm_part.shape, jnp.float32),
        pltpu.VMEM((4,) + norm_part.shape, jnp.float32),
    ]
    dma = pltpu.SemaphoreType.DMA
    scratch += [dma((4, 4, 4)), dma((4, 4, 4)), dma((4, 4, 4)), dma((4, 4, 2)), dma((4, 4, 2))]
    scratch += [dma((4, 4, 2)), dma((4, 4, 2)), dma((4, 3)), dma((4, 3)), dma((6,)), dma((6,))]
    vmem = pl.BlockSpec(memory_space=pltpu.VMEM)
    result = pl.pallas_call(
        reduce_kernel,
        out_shape=[jax.ShapeDtypeStruct(b, jnp.float32) for b in BLOCKS]
        + [jax.ShapeDtypeStruct(norm_part.shape, jnp.float32)],
        in_specs=[pl.BlockSpec(memory_space=pl.ANY)] * 4 + [vmem],
        out_specs=[vmem] * 5,
        scratch_shapes=scratch,
        name="reduce_gradients",
        compiler_params=pltpu.CompilerParams(
            collective_id=1, has_side_effects=True, vmem_limit_bytes=48 << 20
        ),
    )(*grads, norm_part)
    return result[:4], result[4]


def on_device_cube(
    points,
    members,
    cotangent,
    project_weight,
    output_weight,
    upward_weight,
    downward_weight,
    layer_norms,
    project_master,
    project_first,
    project_second,
    output_master,
    output_first,
    output_second,
    upward_master,
    upward_first,
    upward_second,
    downward_master,
    downward_first,
    downward_second,
    norm_first,
    norm_second,
):
    f32, bf16 = jnp.float32, jnp.bfloat16
    score_scale = HEAD_DIM ** (-0.5)
    fulls, saved, latents = run_forward(
        (jnp.transpose(project_weight, (1, 0, 2)), output_weight, upward_weight, downward_weight),
        points,
        members,
        layer_norms,
    )
    project_full, output_full, upward_full, downward_full = fulls
    inputs, entering_one, projected, attended, residual, entering_two, activated, slope = saved
    rows = points.shape[0]
    slots = members[0]
    live = slots >= 0
    norm_back_one = jax.vjp(layer_norm, inputs, layer_norms[0], layer_norms[1])[1]
    norm_back_two = jax.vjp(layer_norm, residual, layer_norms[2], layer_norms[3])[1]
    heads_view = projected.reshape(PLANES, 3, rows, 2, HEAD_DIM)
    queries, keys_all, values_all = heads_view[:, 0], heads_view[:, 1], heads_view[:, 2]
    scores = jnp.einsum("sqhe,skhe->shqk", queries, keys_all, preferred_element_type=f32) * score_scale
    scores = jnp.where(live[None, None, None, :], scores, masked_score)
    probs = jax.nn.softmax(scores, axis=-1)
    probs_low = probs.astype(bf16)
    downward_part = jnp.einsum("srf,rd->sfd", activated, cotangent, preferred_element_type=f32).astype(bf16)
    activated_grad = jnp.einsum("rd,sfd->srf", cotangent, downward_full, preferred_element_type=f32)
    upward_grad = (activated_grad * slope).astype(bf16)
    upward_part = jnp.einsum("rd,srf->sdf", entering_two, upward_grad, preferred_element_type=f32).astype(bf16)
    normed_two_grad = jnp.einsum("srf,sdf->rd", upward_grad, upward_full, preferred_element_type=f32)
    residual_part, gain_two_grad, shift_two_grad = norm_back_two(normed_two_grad)
    residual_grad = residual_part + cotangent.astype(f32)
    branch_grad = residual_grad.astype(bf16)
    output_part = jnp.einsum("srh,rd->shd", attended, branch_grad, preferred_element_type=f32).astype(bf16)
    attended_grad = jnp.einsum("rd,shd->srh", branch_grad, output_full, preferred_element_type=f32).astype(bf16)
    attended_grad = attended_grad.reshape(PLANES, rows, 2, HEAD_DIM)
    value_grad = jnp.einsum("shqk,sqhe->skhe", probs_low, attended_grad, preferred_element_type=f32).astype(bf16)
    prob_grad = jnp.einsum("sqhe,skhe->shqk", attended_grad, values_all, preferred_element_type=f32)
    score_grad = (probs * (prob_grad - jnp.sum(probs * prob_grad, axis=-1, keepdims=True))).astype(bf16)
    query_grad = jnp.einsum("shqk,skhe->sqhe", score_grad, keys_all, preferred_element_type=f32) * score_scale
    key_grad = jnp.einsum("shqk,sqhe->skhe", score_grad, queries, preferred_element_type=f32) * score_scale
    projected_grad = jnp.stack([query_grad.astype(bf16), key_grad.astype(bf16), value_grad], axis=1)
    projected_grad = projected_grad.reshape(PLANES, 3, rows, 2 * HEAD_DIM)
    project_part = jnp.einsum(
        "rod,sjrf->sojdf",
        entering_one.reshape(rows, OWNERS, D // OWNERS),
        projected_grad,
        preferred_element_type=f32,
    ).astype(bf16)
    normed_grad = jnp.einsum("sjrf,sjdf->rd", projected_grad, project_full, preferred_element_type=f32)
    input_part, gain_one_grad, shift_one_grad = norm_back_one(normed_grad)
    input_grad = input_part + residual_grad
    norm_part = jnp.stack([gain_one_grad, shift_one_grad, gain_two_grad, shift_two_grad])
    matches = slots[:, None] == jnp.arange(LAT, dtype=jnp.int32)[None, :]
    slot_of = jnp.argmax(matches, axis=0)
    point_gradient = jnp.where(jnp.any(matches, axis=0)[:, None], input_grad[slot_of], 0.0)
    (downward_summed, upward_summed, output_summed, project_blocks), norm_summed = reduce_gradients(
        (downward_part, upward_part, output_part, project_part.reshape(PLANES, OWNERS * 384, 256)), norm_part
    )
    project_summed = jnp.transpose(project_blocks.reshape(3, D // OWNERS, 256), (1, 0, 2))
    data_index = lax.axis_index("dp")
    norm_columns = norm_first.shape[1]
    norm_gradient = lax.dynamic_slice_in_dim(norm_summed, data_index * norm_columns, norm_columns, 1)
    norm_current = lax.dynamic_slice_in_dim(layer_norms, data_index * norm_columns, norm_columns, 1)
    results = [latents, point_gradient]
    for master, summed, first, second, rate in (
        (project_master, project_summed, project_first, project_second, D ** (-0.5)),
        (output_master, output_summed, output_first, output_second, max(1, D * 4 // LAT) ** (-0.5)),
        (upward_master, upward_summed, upward_first, upward_second, D ** (-0.5)),
        (downward_master, downward_summed, downward_first, downward_second, FF ** (-0.5)),
    ):
        updated, one_new, two_new = adamw_step(master, summed, first, second, rate)
        results += [summed, updated, one_new, two_new, updated.astype(bf16)]
    norm_new = adamw_step(norm_current, norm_gradient, norm_first, norm_second, 0.2)
    results += [norm_gradient, *norm_new]
    return tuple(results)


def solution(mesh):
    return jax.shard_map(
        on_device_cube if dict(mesh.shape) == {"dp": 8, "mp": 4} else on_device_any,
        mesh=mesh,
        in_specs=(
            P(("dp", "mp"), None),
            P(("dp", "mp"), None),
            P(("dp", "mp"), None),
            P(None, None, "mp"),
            P("mp", None),
            P(None, "mp"),
            P("mp", None),
            P(),
            P("dp", None, "mp"),
            P("dp", None, "mp"),
            P("dp", None, "mp"),
            P("mp", "dp"),
            P("mp", "dp"),
            P("mp", "dp"),
            P("dp", "mp"),
            P("dp", "mp"),
            P("dp", "mp"),
            P("mp", "dp"),
            P("mp", "dp"),
            P("mp", "dp"),
            P(None, "dp"),
            P(None, "dp"),
        ),
        out_specs=(
            P(("dp", "mp"), None),
            P(("dp", "mp"), None),
            P("dp", None, "mp"),
            P("dp", None, "mp"),
            P("dp", None, "mp"),
            P("dp", None, "mp"),
            P("dp", None, "mp"),
            P("mp", "dp"),
            P("mp", "dp"),
            P("mp", "dp"),
            P("mp", "dp"),
            P("mp", "dp"),
            P("dp", "mp"),
            P("dp", "mp"),
            P("dp", "mp"),
            P("dp", "mp"),
            P("dp", "mp"),
            P("mp", "dp"),
            P("mp", "dp"),
            P("mp", "dp"),
            P("mp", "dp"),
            P("mp", "dp"),
            P(None, "dp"),
            P(None, "dp"),
            P(None, "dp"),
            P(None, "dp"),
        ),
        check_vma=False,
    )
```

profile of v0, /device:TPU:0, one launch (start us, length us, event | category | flops | bytes accessed | tf_op | source)
XLA Modules:
  0.0 317.7 jit_solution(10830303568285109498)
XLA Ops:
  0.7 0.7 copy-done
  1.4 0.7 copy-done.2
  2.1 108.3 %forward.1 = (bf16[4,3,1024,256]{3,2,1,0:T(8,128)(2,1)}, bf16[4,256,1024]{2,1,0:T(8,128)(2,1)}, bf16[4,1024,1024]{2,1,0:T(8,128)(2,1)}, bf16[4,1024,1024]{2,1,0:...) custom-call(bf16[3,1024,256]{2,1,0:T(8,128)(2,1)} %bitcast.110, ...), custom_call_target="tpu_custom_call" | custom-call | tf_op jit(solution)/shard_map/forward/pallas_call | solution.py:572
  110.4 1.5 reduce_sum.133
  111.8 1.4 reduce_sum.125
  113.2 1.7 multiply_reduce_fusion.4
  115.0 7.1 %fusion.3 = bf16[4,256,1024]{2,1,0:T(8,128)(2,1)S(1)} fusion(f32[4,256,1024]{2,1,0:T(8,128)} %get-tuple-element.49, bf16[4,1024,1024]{2,1,0:T(8,128)(2,1)} %get-tuple-element.48, bf16[256,1024]{1,0:T(8,128)(2,1)S(1)} %copy-done.12), kind=kOutput, calls=%fused_computation.8 | convolution fusion | flops 2149580800 | bytes 15204352 | tf_op jit(solution)/shard_map/rd,sfd->srf/dot_general | solution.py:837
  122.2 2.7 multiply_reduce_fusion.1
  124.9 0.4 fusion.44
  125.5 1.5 copy-done.32
  127.0 1.5 convolution_convert_fusion.3
  128.5 3.7 %reshape.152 = bf16[4,3,256,2,128]{4,3,2,1,0:T(2,128)(2,1)} reshape(bf16[4,3,256,256]{3,2,1,0:T(8,128)(2,1)} %get-tuple-element.46) | data formatting | bytes 3145728 | tf_op jit(solution)/shard_map/reshape | solution.py:830
  132.2 3.4 %fusion.45 = (bf16[4,1,256,2,128]{4,3,2,1,0:T(2,128)(2,1)}, bf16[4,1,256,2,128]{4,3,2,1,0:T(2,128)(2,1)}, bf16[4,1,256,2,128]{4,3,2,1,0:T(2,128)(2,1)}) fusion(bf16[4,3,256,2,128]{4,3,2,1,0:T(2,128)(2,1)} %reshape.152), kind=kLoop, calls=%fused_computation.99 | loop fusion | bytes 3145728 | tf_op jit(solution)/shard_map/slice | solution.py:831
  135.7 3.4 %fusion.47 = (f32[4,2,256]{2,1,0:T(2,128)S(1)}, f32[4,2,256,256]{2,3,1,0:T(8,128)}) fusion(pred[256]{0:T(512)(128)(4,1)S(1)} %broadcast_compare_fusion, bf16[4,1,256,2,128]{4,3,2,1,0:T(2,128)(2,1)} %get-tuple-element.96, bf16[4,1,256,2,128]{4,3,2,1,0:T(2,128)(2,1)} %get-tuple-element.95), kind=kOutput, calls=%fused_computation.101 | convolution fusion | flops 136315136 | bytes 3154176 | tf_op jit(solution)/shard_map/sub | solution.py:834
  139.1 2.5 multiply_reduce_fusion
  141.6 0.4 multiply_convert_fusion
  142.0 1.0 copy-done.10
  143.0 1.1 fusion.9
  144.1 2.0 copy.79
  146.1 2.7 fusion.10
  148.8 2.0 copy.80
  150.8 3.1 convolution_convert_fusion.2
  153.9 2.0 copy.81
  155.9 6.2 %multiply_reduce_fusion.2 = (f32[1024]{0:T(1024)S(1)}, f32[256]{0:T(256)S(1)}, f32[1024]{0:T(1024)S(1)}, f32[256,1024]{1,0:T(8,128)}) fusion(f32[256,1024]{1,0:T(8,128)S(1)} %copy-done.6, f32[256]{0:T(256)S(1)} %fusion.30, f32[256]{0:T(256)S(1)} %broadcast_multiply_fusion, f32[1024]{0:T(1024)S(1)} %bitcast.113, ...), kind=kOutput, calls=%fused_computation.28 | convolution fusion | flops 1614280448 | bytes 9976832 | tf_op jit(solution)/shard_map/sjrf,sjdf->rd/dot_general | solution.py:860
  162.2 1.0 copy.106
  163.2 3.3 %convert_bitcast_fusion.1 = bf16[4,8,3,128,256]{4,3,1,2,0:T(8,128)(2,1)S(1)} fusion(bf16[256,8,128,1,1]{0,2,1,4,3:T(8,128)(2,1)} %bitcast.111, bf16[4,1,256,256]{3,2,0,1:T(8,128)(2,1)} %copy.81, bf16[4,1,256,256]{3,2,0,1:T(8,128)(2,1)} %copy.80, bf16[4,1,256,256]{3,2,0,1:T(8,128)(2,1)} %copy.79), kind=kOutput, calls=%fused_computation.6 | convolution fusion | flops 1615331328 | bytes 8388608 | tf_op jit(solution)/shard_map/rod,sjrf->sojdf/dot_general | solution.py:854
  166.5 3.1 copy.89
  169.6 0.7 convolution_convert_fusion.1.refs_2_
  170.3 0.8 copy-done.5
  171.2 5.9 %convert_bitcast_fusion.refs_1_ = bf16[4,1024,1024]{2,1,0:T(8,128)(2,1)} fusion(bf16[4,256,1024]{2,1,0:T(8,128)(2,1)S(1)} %copy-done.5, bf16[256,1024]{1,0:T(8,128)(2,1)S(1)} %get-tuple-element.56), kind=kOutput, calls=%fused_computation.2 | convolution fusion | flops 2151677952 | bytes 11010048 | tf_op jit(solution)/shard_map/rd,srf->sdf/dot_general | solution.py:839
  177.1 5.9 %convolution_convert_fusion.refs_0_ = bf16[4,1024,1024]{2,1,0:T(8,128)(2,1)} fusion(bf16[4,256,1024]{2,1,0:T(8,128)(2,1)S(1)} %copy-done.11, bf16[256,1024]{1,0:T(8,128)(2,1)S(1)} %copy-done.12), kind=kOutput, calls=%fused_computation.3 | convolution fusion | flops 2151677952 | bytes 11010048 | tf_op jit(solution)/shard_map/srf,rd->sfd/dot_general | solution.py:836
  183.0 117.0 %reduce_gradients.1 = (f32[1024,128]{1,0:T(8,128)S(1)}, f32[128,1024]{1,0:T(8,128)S(1)}, f32[256,128]{1,0:T(8,128)S(1)}, f32[384,256]{1,0:T(8,128)S(1)}, f32[4,1024]{1,0:T(4,128)S(1)}) custom-call(bf16[4,1024,1024]{2,1,0:T(8,128)(2,1)} %convolution_convert_fusion.refs_0_, bf16[4,1024,1024]{2,1,0:T(8,128)(2,1)} %convert_bitcast_fusion.refs_1_, ...), custom_call_target="tpu_custom_call" | custom-call | tf_op jit(solution)/shard_map/reduce_gradients/pallas_call | solution.py:776
  300.1 1.5 fusion.37
  301.7 0.3 copy-done.23
  301.9 1.5 fusion.35
  303.5 1.3 fusion.41
  304.7 0.8 fusion.39
  305.6 0.6 multiply_subtract_fusion.4
  306.2 1.6 fusion.43
  307.8 0.3 add_add_fusion.2
  308.1 0.7 iota_reduce_fusion
  308.8 2.0 gather_fusion
  310.9 2.4 broadcast_select_fusion
  313.3 1.0 copy.149
  314.3 0.7 copy.150
  315.0 0.7 copy.151
  315.7 0.8 copy.152
  316.5 0.8 copy.153
  (80 shorter events, 0.6 us)
Async XLA Ops:
  0.7 0.7 copy-start
  1.4 0.7 copy-start.2
  110.3 2.9 copy-start.6
  110.3 4.6 %copy-start.12 = (bf16[256,1024]{1,0:T(8,128)(2,1)S(1)}, bf16[256,1024]{1,0:T(8,128)(2,1)}, u32[]{:S(2)}) copy-start(bf16[256,1024]{1,0:T(8,128)(2,1)} %param.24) | copy-start | bytes 1572868
  113.2 8.9 %slice-start = ((s8[8388608]{0:T(1024)(128)(4,1)}), s8[4194304]{0:T(1024)(128)(4,1)S(1)}, s32[]{:S(2)}) async-start(s8[8388608]{0:T(1024)(128)(4,1)} %bitcast.121), calls=%async_computation | async-start | bytes 8388608
  115.0 7.1 %copy-start.1 = (f32[4,1024]{1,0:T(4,128)S(1)}, f32[4,1024]{1,0:T(4,128)}, u32[]{:S(2)}) copy-start(f32[4,1024]{1,0:T(4,128)} %refs_6_.1) | copy-start | bytes 49156
  115.0 7.2 %copy-start.9 = (f32[256,1024]{1,0:T(8,128)S(1)}, f32[256,1024]{1,0:T(8,128)}, u32[]{:S(2)}) copy-start(f32[256,1024]{1,0:T(8,128)} %get-tuple-element.51) | copy-start | bytes 3145732
  115.0 7.2 %slice-start.1 = ((s8[8388608]{0:T(1024)(128)(4,1)}), s8[4194304]{0:T(1024)(128)(4,1)S(1)}, s32[]{:S(2)}) async-start(s8[8388608]{0:T(1024)(128)(4,1)} %bitcast.121), calls=%async_computation.1 | async-start | bytes 8388608
  122.1 2.7 copy-start.4
  124.9 2.1 copy-start.32
  125.3 3.3 %copy-start.7 = (f32[256,1024]{1,0:T(8,128)}, f32[256,1024]{1,0:T(8,128)S(1)}, u32[]{:S(2)}) copy-start(f32[256,1024]{1,0:T(8,128)S(1)} %get-tuple-element.93) | copy-start | bytes 3145732
  125.5 3.1 copy-start.14
  132.2 3.4 %copy-start.3 = (s32[1,256]{1,0:T(1,128)S(1)}, s32[1,256]{1,0:T(1,128)}, u32[]{:S(2)}) copy-start(s32[1,256]{1,0:T(1,128)} %refs_5_.1) | copy-start | bytes 3076
  139.1 2.5 copy-start.13
  141.6 1.4 copy-start.16
  142.0 1.0 copy-start.10
  166.5 3.1 copy-start.15
  169.6 1.6 copy-start.5
  171.2 5.9 %copy-start.11 = (bf16[4,256,1024]{2,1,0:T(8,128)(2,1)S(1)}, bf16[4,256,1024]{2,1,0:T(8,128)(2,1)}, u32[]{:S(2)}) copy-start(bf16[4,256,1024]{2,1,0:T(8,128)(2,1)} %get-tuple-element.55) | copy-start | bytes 6291460
  183.0 117.1 %copy-start.18 = (f32[128,1024]{1,0:T(8,128)S(1)}, f32[128,1024]{1,0:T(8,128)}, u32[]{:S(2)}) copy-start(f32[128,1024]{1,0:T(8,128)} %param.36) | copy-start | bytes 1572868
  183.0 117.1 %copy-start.19 = (f32[128,1024]{1,0:T(8,128)S(1)}, f32[128,1024]{1,0:T(8,128)}, u32[]{:S(2)}) copy-start(f32[128,1024]{1,0:T(8,128)} %param.37) | copy-start | bytes 1572868
  183.0 117.1 %copy-start.20 = (f32[128,1024]{1,0:T(8,128)S(1)}, f32[128,1024]{1,0:T(8,128)}, u32[]{:S(2)}) copy-start(f32[128,1024]{1,0:T(8,128)} %param.38) | copy-start | bytes 1572868
  300.1 1.6 copy-start.21
  300.1 1.6 copy-start.22
  300.1 1.8 copy-start.23
  301.6 1.8 copy-start.24
  301.6 1.8 copy-start.25
  301.6 1.8 copy-start.26
  303.4 1.3 copy-start.27
  303.4 1.3 copy-start.28
  303.4 1.3 copy-start.29
  303.4 2.1 copy-start.30
  303.4 2.1 copy-start.31
  305.6 2.3 copy-start.8
  310.8 2.5 copy-start.17
where the time goes:
time: 324 us; the launch traced here: 318 us
  Pallas kernels  225 us (69%)
  matrix products  46.1 us (14%)
  local copies, waits for them, and re-layouts  28.4 us (9%)
  other arithmetic  16.4 us (5%)
    pallas_call x1, Pallas kernels, reduce_gradients(): pl.pallas_call(reduce_kernel, out_shape=[jax.ShapeDtypeStruct(b, jnp.floa...  117 us
    pallas_call x1, Pallas kernels, run_forward(): pl.pallas_call(forward_kernel, out_shape=[jax.ShapeDtypeStruct(*a) for a...  108 us
    unnamed x75, local copies, waits for them, and re-layouts  9.09 us
    dot_general x1, matrix products, on_device_cube(): jnp.einsum('rd,sfd->srf', cotangent, downward_full, preferred_element_typ...  7.09 us

commit v1 on v0

--- a/solution.py
+++ b/solution.py
@@ -1,5 +1,3 @@
-import functools
-
 import jax
 import jax.numpy as jnp
 from jax import lax
@@ -586,206 +584,400 @@
     return result[:4], result[4:12], result[12]
 
 
-BLOCKS = ((1024, 128), (128, 1024), (256, 128), (384, 256))
-STRIPS = (128, 16, 128, 64)
-
-
-def owner_view(ref, w, plane, owner):
-    if w in (0, 2):
-        return ref.at[plane, :, pl.ds(pl.multiple_of(owner * 128, 128), 128)]
-    return ref.at[plane, pl.ds(pl.multiple_of(owner * BLOCKS[w][0], BLOCKS[w][0]), BLOCKS[w][0]), :]
-
-
-def reduce_kernel(*refs):
-    grads, norm_part = refs[0:4], refs[4]
-    outs, norm_out = refs[5:9], refs[9]
-    own, pair_in, one_in, two_in, z_in = (refs[10 + 4 * k : 14 + 4 * k] for k in range(5))
-    norm_own, norm_in, norm_planes = refs[30:33]
-    load_sem, c_send, c_recv, one_send, one_recv, two_send, two_recv, z_send, z_recv = refs[33:42]
-    norm_send, norm_recv = refs[42:44]
+WIDTHS = (D, D, 256, 3 * 256)
+BLOCK = D // OWNERS
+HALF = BLOCK // 2
+RING = 3
+UNITS = [(w, i) for w in (0, 1, 3, 2) for i in range(PLANES)]
+
+
+def backward_kernel(*refs):
+    fulls, saved_in = refs[0:4], refs[4:12]
+    cotangent_in, members, norms = refs[12:15]
+    outs, norm_out, points_out = refs[15:19], refs[19], refs[20]
+    saved, cotangent = refs[21:29], refs[29]
+    inputs, entering_one, projected, attended, residual, entering_two, activated, slope = saved
+    down_ring, up_ring, output_full, project_ring = refs[30:34]
+    turned, upward_grad, residual_grad, branch_grad, projected_grad, normed_grad = refs[34:40]
+    ring = refs[40]
+    acc, one_in, two_in, z_in = refs[41:45], refs[45:49], refs[49:53], refs[53:57]
+    norm_own, norm_in, norm_planes = refs[57:60]
+    saved_sem, cotangent_sem, weight_sem = refs[60:63]
+    c_send, c_recv, one_send, one_recv, two_send, two_recv, z_send, z_recv = refs[63:71]
+    norm_send, norm_recv = refs[71:73]
+    f32, bf16 = jnp.float32, jnp.bfloat16
     y, x, c, z = place()
+
+    def load(n):
+        return pltpu.make_async_copy(saved_in[n], saved[n], saved_sem.at[n])
+
+    cotangent_load = pltpu.make_async_copy(cotangent_in, cotangent, cotangent_sem)
+    cotangent_load.start()
+    for n in (6, 5, 7, 4, 2, 3, 1, 0):
+        load(n).start()
+
+    def plane_of(i):
+        return (z + 1 + i) % PLANES
+
+    def weight_load(w, i):
+        plane = plane_of(i)
+        if w == 2:
+            return pltpu.make_async_copy(fulls[1], output_full, weight_sem.at[2, 0])
+        target = (down_ring, up_ring, None, project_ring.at[i % 2])[w]
+        return pltpu.make_async_copy(fulls[(3, 2, 1, 0)[w]].at[plane], target, weight_sem.at[w, i])
+
+    weight_load(0, 0).start()
+    weight_load(1, 0).start()
+    weight_load(2, 0).start()
+    weight_load(3, 0).start()
     greet(y, x, c, z)
     sibling = device(y, x, 1 - c, z)
     over_x, over_y = device(y, 1 - x, c, z), device(1 - y, x, c, z)
-
-    def plane_of(i):
-        return (z + 1 + i) % PLANES
 
     def remote(src, dst, send, recv, target):
         return pltpu.make_async_remote_copy(
             src_ref=src, dst_ref=dst, send_sem=send, recv_sem=recv, device_id=target, device_id_type=MESH
         )
 
-    def load(w, i, k):
-        return pltpu.make_async_copy(
-            owner_view(grads[w], w, plane_of(i), k * 2 + c), own[w].at[i, k // 2, k % 2], load_sem.at[w, i, k]
+    def pair_copy(t):
+        w, i = UNITS[t]
+        return remote(
+            ring.at[t % RING, :, :, :, 0 : WIDTHS[w]], acc[w].at[i], c_send.at[t], c_recv.at[t], sibling
         )
 
-    def pair_copy(w, i, k):
+    def half_rows(half):
+        return pl.ds(half * HALF, HALF)
+
+    def one_copy(t, half):
+        w, i = UNITS[t]
+        rows = half_rows(half)
+        src = acc[w].at[i, 1 - y, :, rows] if half == 0 else acc[w].at[i, :, 1 - x, rows]
         return remote(
-            owner_view(grads[w], w, plane_of(i), k * 2 + 1 - c),
-            pair_in[w].at[i, k // 2, k % 2],
-            c_send.at[w, i, k],
-            c_recv.at[w, i, k],
-            sibling,
+            src, one_in[w].at[i, half], one_send.at[t, half], one_recv.at[t, half], (over_y, over_x)[half]
         )
 
-    def half_rows(w, half):
-        size = BLOCKS[w][0] // 2
-        return pl.ds(half * size, size)
-
-    def one_copy(w, i, half):
-        rows = half_rows(w, half)
-        src = own[w].at[i, 1 - y, :, rows] if half == 0 else own[w].at[i, :, 1 - x, rows]
+    def two_copy(t, half):
+        w, i = UNITS[t]
+        rows = half_rows(half)
+        src = acc[w].at[i, y, 1 - x, rows] if half == 0 else acc[w].at[i, 1 - y, x, rows]
         return remote(
-            src, one_in[w].at[i, half], one_send.at[w, i, half], one_recv.at[w, i, half], (over_y, over_x)[half]
+            src, two_in[w].at[i, half], two_send.at[t, half], two_recv.at[t, half], (over_x, over_y)[half]
         )
 
-    def two_copy(w, i, half):
-        rows = half_rows(w, half)
-        src = own[w].at[i, y, 1 - x, rows] if half == 0 else own[w].at[i, 1 - y, x, rows]
-        return remote(
-            src, two_in[w].at[i, half], two_send.at[w, i, half], two_recv.at[w, i, half], (over_x, over_y)[half]
-        )
-
-    def z_copy(w, i):
-        return remote(
-            own[w].at[i, y, x], z_in[w].at[i], z_send.at[w, i], z_recv.at[w, i], device(y, x, c, plane_of(i))
-        )
-
-    def add_rows(target, source, count, strip):
+    def z_copy(t):
+        w, i = UNITS[t]
+        return remote(acc[w].at[i, y, x], z_in[w].at[i], z_send.at[t], z_recv.at[t], device(y, x, c, plane_of(i)))
+
+    def add_rows(target, source):
         def body(r, carry):
-            rows = pl.ds(pl.multiple_of(r * strip, strip), strip)
-            total = target[rows].astype(jnp.float32) + source[rows].astype(jnp.float32)
-            target[rows] = total.astype(target.dtype)
+            rows = pl.ds(pl.multiple_of(r * 16, 16), 16)
+            target[rows] = (target[rows].astype(f32) + source[rows].astype(f32)).astype(bf16)
             return carry
 
-        lax.fori_loop(0, count // strip, body, 0)
-
-    def start_unit(w, i):
-        for k in range(4):
-            pair_copy(w, i, k).start()
-            load(w, i, k).start()
-
-    def after_pair(w, i):
-        for k in range(4):
-            load(w, i, k).wait()
-            pair_copy(w, i, k).wait_recv()
-            add_rows(own[w].at[i, k // 2, k % 2], pair_in[w].at[i, k // 2, k % 2], BLOCKS[w][0], STRIPS[w])
-        for half in (0, 1):
-            one_copy(w, i, half).start()
-
-    def after_one(w, i):
-        size = BLOCKS[w][0] // 2
-        for half in (0, 1):
-            one_copy(w, i, half).wait()
-            rows = half_rows(w, half)
+        lax.fori_loop(0, HALF // 16, body, 0)
+
+    def partial(w, i, parity, columns, n):
+        plane = plane_of(i)
+        if w == 3:
+            right = projected_grad[plane, n]
+        else:
+            right = (activated, upward_grad, attended)[w][plane, :, columns]
+        return dot(turned[w, parity], right, NN)
+
+    def over_tiles(w, body):
+        if w == 2:
+            body(pl.ds(0, 256), 0)
+            return
+
+        def step(n, carry):
+            body(pl.ds(pl.multiple_of(n * 256, 256), 256), n)
+            return carry
+
+        lax.fori_loop(0, WIDTHS[w] // 256, step, 0)
+
+    def produce(t):
+        w, i = UNITS[t]
+        if t >= RING:
+            pair_copy(t - RING).wait_send()
+
+        def body(columns, n):
+            product = partial(w, i, 1 - c, columns, n).astype(bf16)
+            for k in range(4):
+                ring[t % RING, k // 2, k % 2, :, columns] = product[k * BLOCK : (k + 1) * BLOCK]
+
+        over_tiles(w, body)
+        pair_copy(t).start()
+
+    def join(t):
+        w, i = UNITS[t]
+        pair_copy(t).wait_recv()
+
+        def body(columns, n):
+            product = partial(w, i, c, columns, n)
+            for k in range(4):
+                came = acc[w][i, k // 2, k % 2, :, columns].astype(f32)
+                acc[w][i, k // 2, k % 2, :, columns] = (product[k * BLOCK : (k + 1) * BLOCK] + came).astype(bf16)
+
+        over_tiles(w, body)
+        for half in HALVES:
+            one_copy(t, half).start()
+
+    def after_one(t):
+        w, i = UNITS[t]
+        for half in HALVES:
+            one_copy(t, half).wait()
+            rows = half_rows(half)
             for k in (0, 1):
-                target = own[w].at[i, y, k, rows] if half == 0 else own[w].at[i, k, x, rows]
-                add_rows(target, one_in[w].at[i, half, k], size, min(size, STRIPS[w]))
-            two_copy(w, i, half).start()
-
-    def after_two(w, i):
-        size = BLOCKS[w][0] // 2
-        for half in (0, 1):
-            two_copy(w, i, half).wait()
-            add_rows(own[w].at[i, y, x, half_rows(w, half)], two_in[w].at[i, half], size, min(size, STRIPS[w]))
+                target = acc[w].at[i, y, k, rows] if half == 0 else acc[w].at[i, k, x, rows]
+                add_rows(target, one_in[w].at[i, half, k])
+            two_copy(t, half).start()
+
+    def after_two(t):
+        w, i = UNITS[t]
+        for half in HALVES:
+            two_copy(t, half).wait()
+            add_rows(acc[w].at[i, y, x, half_rows(half)], two_in[w].at[i, half])
         if i < PLANES - 1:
-            z_copy(w, i).start()
+            z_copy(t).start()
 
     def finish(w):
-        for i in range(PLANES - 1):
-            z_copy(w, i).wait()
-
-        def body(r, carry):
-            rows = pl.ds(pl.multiple_of(r * STRIPS[w], STRIPS[w]), STRIPS[w])
-            total = own[w].at[PLANES - 1, y, x][rows].astype(jnp.float32)
+        for t, unit in enumerate(UNITS):
+            if unit[0] == w and unit[1] < PLANES - 1:
+                z_copy(t).wait()
+
+        def body(n, carry):
+            columns = pl.ds(pl.multiple_of(n * 128, 128), 128)
+            total = acc[w].at[PLANES - 1, y, x][:, columns].astype(f32)
             for i in range(PLANES - 1):
-                total = total + z_in[w].at[i][rows].astype(jnp.float32)
-            outs[w][rows] = total
+                total = total + z_in[w].at[i][:, columns].astype(f32)
+            if w in (0, 2):
+                outs[w][columns, :] = total.T
+            else:
+                outs[w][:, columns] = total
             return carry
 
-        lax.fori_loop(0, BLOCKS[w][0] // STRIPS[w], body, 0)
+        lax.fori_loop(0, WIDTHS[w] // 128, body, 0)
+
+    def turn(source, w):
+        for owner in range(OWNERS):
+            columns = slice(owner * BLOCK, (owner + 1) * BLOCK)
+            place_at = slice((owner // 2) * BLOCK, (owner // 2 + 1) * BLOCK)
+            turned[w, owner % 2, place_at, :] = source[:, columns].T
+
+    def hidden_back(i):
+        plane = plane_of(i)
+        weight_load(0, i).wait()
+
+        def grad(columns):
+            product = dot(cotangent[...], down_ring[columns, :], NT)
+            upward_grad[plane, :, columns] = (product * slope[plane, :, columns]).astype(bf16)
+
+        tiles(4, 256, grad)
+        if i < PLANES - 1:
+            weight_load(0, i + 1).start()
+        weight_load(1, i).wait()
+
+        def normed(columns):
+            product = dot(upward_grad[plane], up_ring[columns, :], NT)
+            if i == 0:
+                normed_grad[:, columns] = product
+            else:
+                normed_grad[:, columns] += product
+
+        tiles(4, 256, normed)
+        if i < PLANES - 1:
+            weight_load(1, i + 1).start()
+
+    def norm_back(source, gain, row, store):
+        norm_own[0, row : row + 2, :] = jnp.zeros((2, D), f32)
+
+        def strip(n, carry):
+            rows = pl.ds(pl.multiple_of(n * 32, 32), 32)
+            values = source[rows, :]
+            center = values - jnp.mean(values, axis=-1, keepdims=True)
+            scale = lax.rsqrt(jnp.mean(center * center, axis=-1, keepdims=True) + norm_epsilon)
+            hat = center * scale
+            grad = normed_grad[rows, :]
+            norm_own[0, row : row + 1, :] += jnp.sum(grad * hat, axis=0, keepdims=True)
+            norm_own[0, row + 1 : row + 2, :] += jnp.sum(grad, axis=0, keepdims=True)
+            grad = grad * gain
+            inner = jnp.mean(grad * hat, axis=-1, keepdims=True)
+            store(rows, scale * (grad - jnp.mean(grad, axis=-1, keepdims=True) - hat * inner))
+            return carry
+
+        lax.fori_loop(0, ROWS // 32, strip, 0)
+
+    def residual_back():
+        def store(rows, part):
+            total = part + cotangent[rows, :].astype(f32)
+            residual_grad[rows, :] = total
+            branch_grad[rows, :] = total.astype(bf16)
+
+        norm_back(residual, norms[2:3, :], 2, store)
+
+    def attend_back(i):
+        plane = plane_of(i)
+        live = members[...] >= 0
+        attended_grad = dot(branch_grad[...], output_full[plane], NT).astype(bf16)
+        scale = HEAD_DIM ** (-0.5)
+        for head in range(2):
+            span = slice(head * HEAD_DIM, (head + 1) * HEAD_DIM)
+            queries, keys_all, values_all = (projected[plane, part, :, span] for part in range(3))
+            scores = jnp.where(live, dot(queries, keys_all, NT) * scale, masked_score)
+            exponent = jnp.exp(scores - jnp.max(scores, axis=-1, keepdims=True))
+            probs = exponent * (1.0 / jnp.sum(exponent, axis=-1, keepdims=True))
+            grad = attended_grad[:, span]
+            projected_grad[plane, 2, :, span] = dot(probs.astype(bf16), grad, TN).astype(bf16)
+            prob_grad = dot(grad, values_all, NT)
+            inner = jnp.sum(probs * prob_grad, axis=-1, keepdims=True)
+            score_grad = (probs * (prob_grad - inner)).astype(bf16)
+            projected_grad[plane, 0, :, span] = (dot(score_grad, keys_all, NN) * scale).astype(bf16)
+            projected_grad[plane, 1, :, span] = (dot(score_grad, queries, TN) * scale).astype(bf16)
+
+    def project_back(i):
+        plane = plane_of(i)
+        weight_load(3, i).wait()
+        if i < PLANES - 1:
+            weight_load(3, i + 1).start()
+
+        def normed(columns):
+            total = dot(projected_grad[plane, 0], project_ring[i % 2, 0, columns, :], NT)
+            for part in (1, 2):
+                total += dot(projected_grad[plane, part], project_ring[i % 2, part, columns, :], NT)
+            if i == 0:
+                normed_grad[:, columns] = total
+            else:
+                normed_grad[:, columns] += total
+
+        tiles(4, 256, normed)
+
+    def input_back():
+        def store(rows, part):
+            residual_grad[rows, :] += part
+
+        norm_back(inputs, norms[0:1, :], 0, store)
+
+    def points_back():
+        slot_of = lax.broadcasted_iota(jnp.int32, (ROWS, ROWS), 0) == members[...]
+        chosen = slot_of.astype(f32).astype(bf16)
+
+        def pick(columns):
+            rest = residual_grad[:, columns]
+            total = jnp.zeros((ROWS, 256), f32)
+            for _ in range(3):
+                low = rest.astype(bf16)
+                total += dot(chosen, low, NN)
+                rest = rest - low.astype(f32)
+            points_out[:, columns] = total
+
+        tiles(4, 256, pick)
 
     def norm_step(k):
-        return remote(
-            norm_own.at[k], norm_in.at[k], norm_send.at[k], norm_recv.at[k], (sibling, over_x, over_y)[k]
-        )
+        return remote(norm_own.at[k], norm_in.at[k], norm_send.at[k], norm_recv.at[k], (sibling, over_x, over_y)[k])
 
     def norm_plane(d):
-        return remote(
-            norm_own.at[3],
-            norm_planes.at[z],
-            norm_send.at[2 + d],
-            norm_recv.at[2 + d],
-            device(y, x, c, (z + d) % PLANES),
-        )
-
-    norm_own[0] = norm_part[...]
-    norm_step(0).start()
-
-    units = [(w, i) for w in range(4) for i in range(PLANES)]
-    ahead = 2
-    for unit in units[:ahead]:
-        start_unit(*unit)
-    for step in range(len(units) + 4):
-        if step + ahead < len(units):
-            start_unit(*units[step + ahead])
-        if step < len(units):
-            after_pair(*units[step])
-        if 0 <= step - 1 < len(units):
-            after_one(*units[step - 1])
-        if 0 <= step - 2 < len(units):
-            after_two(*units[step - 2])
-        if step < 3:
-            norm_step(step).wait()
-            norm_own[step + 1] = norm_own[step] + norm_in[step]
-            if step < 2:
-                norm_step(step + 1).start()
+        target = device(y, x, c, (z + d) % PLANES)
+        return remote(norm_own.at[3], norm_planes.at[z], norm_send.at[2 + d], norm_recv.at[2 + d], target)
+
+    def before(t):
+        w, i = UNITS[t]
+        if (w, i) == (0, 0):
+            cotangent_load.wait()
+            turn(cotangent, 0)
+            load(6).wait()
+        elif w == 1:
+            if i == 0:
+                load(5).wait()
+                turn(entering_two, 1)
+                load(7).wait()
+            hidden_back(i)
+        elif w == 3:
+            if i == 0:
+                load(4).wait()
+                residual_back()
+                load(2).wait()
+                load(1).wait()
+                turn(entering_one, 3)
+                weight_load(2, 0).wait()
+            attend_back(i)
+            project_back(i)
+        elif i == 0:
+            load(3).wait()
+            turn(branch_grad, 2)
+
+    count = len(UNITS)
+    lag = (2, 3, 4)
+    before(0)
+    produce(0)
+    input_at = 1 + [t for t, unit in enumerate(UNITS) if unit == (3, 3)][0]
+    last = {w: max(t for t, unit in enumerate(UNITS) if unit[0] == w) for w in range(4)}
+    for step in range(count + lag[2]):
+        if step + 1 < count:
+            before(step + 1)
+            produce(step + 1)
+        if step < count:
+            join(step)
+        if 0 <= step - lag[0] < count:
+            after_one(step - lag[0])
+        if 0 <= step - lag[1] < count:
+            after_two(step - lag[1])
+        if step == input_at:
+            load(0).wait()
+            input_back()
+            norm_step(0).start()
+        if step == count:
+            points_back()
+        at = step - input_at - 1
+        if 0 <= at < 3:
+            norm_step(at).wait()
+            norm_own[at + 1] = norm_own[at] + norm_in[at]
+            if at < 2:
+                norm_step(at + 1).start()
             else:
                 norm_planes[z] = norm_own[3]
                 for d in (1, 2, 3):
                     norm_plane(d).start()
-        if step >= 4 and (step - 4) % PLANES == PLANES - 1:
-            finish((step - 4) // PLANES)
+        for w in range(4):
+            if step - lag[2] == last[w]:
+                finish(w)
     for d in (1, 2, 3):
         norm_plane(d).wait()
     norm_out[...] = (norm_planes[0] + norm_planes[1]) + (norm_planes[2] + norm_planes[3])
-    for w, i in units:
-        for k in range(4):
-            pair_copy(w, i, k).wait_send()
-
-
-def reduce_gradients(grads, norm_part):
-    bf16 = jnp.bfloat16
-    halves = [(b[0] // 2, b[1]) for b in BLOCKS]
-    scratch = [pltpu.VMEM((4, 2, 2) + b, bf16) for b in BLOCKS]
-    scratch += [pltpu.VMEM((4, 2, 2) + b, bf16) for b in BLOCKS]
-    scratch += [pltpu.VMEM((4, 2, 2) + h, bf16) for h in halves]
-    scratch += [pltpu.VMEM((4, 2) + h, bf16) for h in halves]
-    scratch += [pltpu.VMEM((3,) + b, bf16) for b in BLOCKS]
-    scratch += [
-        pltpu.VMEM((4,) + norm_part.shape, jnp.float32),
-        pltpu.VMEM((3,) + norm_part.shape, jnp.float32),
-        pltpu.VMEM((4,) + norm_part.shape, jnp.float32),
-    ]
+    for t in range(count - RING, count):
+        pair_copy(t).wait_send()
+
+
+def run_backward(fulls, saved, cotangent, members, layer_norms):
+    f32, bf16 = jnp.float32, jnp.bfloat16
+    rows_f32, rows_bf16 = pltpu.VMEM((ROWS, D), f32), pltpu.VMEM((ROWS, D), bf16)
+    scratch = [pltpu.VMEM(a.shape, a.dtype) for a in saved] + [rows_bf16]
+    scratch += [pltpu.VMEM((D, D), bf16)] * 2
+    scratch += [pltpu.VMEM((PLANES, 256, D), bf16), pltpu.VMEM((2, 3, D, 256), bf16)]
+    scratch += [pltpu.VMEM((4, 2, D // 2, ROWS), bf16), pltpu.VMEM((PLANES, ROWS, D), bf16)]
+    scratch += [rows_f32, rows_bf16, pltpu.VMEM((PLANES, 3, ROWS, 256), bf16), rows_f32]
+    scratch += [pltpu.VMEM((RING, 2, 2, BLOCK, D), bf16)]
+    scratch += [pltpu.VMEM((4, 2, 2, BLOCK, n), bf16) for n in WIDTHS]
+    scratch += [pltpu.VMEM((4, 2, 2, HALF, n), bf16) for n in WIDTHS]
+    scratch += [pltpu.VMEM((4, 2, HALF, n), bf16) for n in WIDTHS]
+    scratch += [pltpu.VMEM((3, BLOCK, n), bf16) for n in WIDTHS]
+    scratch += [pltpu.VMEM((n, 4, D), f32) for n in (4, 3, 4)]
     dma = pltpu.SemaphoreType.DMA
-    scratch += [dma((4, 4, 4)), dma((4, 4, 4)), dma((4, 4, 4)), dma((4, 4, 2)), dma((4, 4, 2))]
-    scratch += [dma((4, 4, 2)), dma((4, 4, 2)), dma((4, 3)), dma((4, 3)), dma((6,)), dma((6,))]
-    vmem = pl.BlockSpec(memory_space=pltpu.VMEM)
+    scratch += [dma((8,)), dma, dma((4, 4)), dma((16,)), dma((16,))]
+    scratch += [dma((16, 2))] * 4 + [dma((16,))] * 2 + [dma((6,))] * 2
+    anywhere, vmem = pl.BlockSpec(memory_space=pl.ANY), pl.BlockSpec(memory_space=pltpu.VMEM)
+    blocks = [(WIDTHS[0], BLOCK), (BLOCK, WIDTHS[1]), (WIDTHS[2], BLOCK), (BLOCK, WIDTHS[3])]
     result = pl.pallas_call(
-        reduce_kernel,
-        out_shape=[jax.ShapeDtypeStruct(b, jnp.float32) for b in BLOCKS]
-        + [jax.ShapeDtypeStruct(norm_part.shape, jnp.float32)],
-        in_specs=[pl.BlockSpec(memory_space=pl.ANY)] * 4 + [vmem],
-        out_specs=[vmem] * 5,
+        backward_kernel,
+        out_shape=[jax.ShapeDtypeStruct(s, f32) for s in blocks + [(4, D), (ROWS, D)]],
+        in_specs=[anywhere] * 13 + [vmem] * 2,
+        out_specs=[vmem] * 6,
         scratch_shapes=scratch,
-        name="reduce_gradients",
+        name="backward",
         compiler_params=pltpu.CompilerParams(
-            collective_id=1, has_side_effects=True, vmem_limit_bytes=48 << 20
+            collective_id=1, has_side_effects=True, vmem_limit_bytes=60 << 20
         ),
-    )(*grads, norm_part)
-    return result[:4], result[4]
+    )(*fulls, *saved, cotangent, members, layer_norms)
+    return result[:4], result[4], result[5]
 
 
 def on_device_cube(
@@ -812,62 +1004,16 @@
     norm_first,
     norm_second,
 ):
-    f32, bf16 = jnp.float32, jnp.bfloat16
-    score_scale = HEAD_DIM ** (-0.5)
+    bf16 = jnp.bfloat16
     fulls, saved, latents = run_forward(
         (jnp.transpose(project_weight, (1, 0, 2)), output_weight, upward_weight, downward_weight),
         points,
         members,
         layer_norms,
     )
-    project_full, output_full, upward_full, downward_full = fulls
-    inputs, entering_one, projected, attended, residual, entering_two, activated, slope = saved
-    rows = points.shape[0]
-    slots = members[0]
-    live = slots >= 0
-    norm_back_one = jax.vjp(layer_norm, inputs, layer_norms[0], layer_norms[1])[1]
-    norm_back_two = jax.vjp(layer_norm, residual, layer_norms[2], layer_norms[3])[1]
-    heads_view = projected.reshape(PLANES, 3, rows, 2, HEAD_DIM)
-    queries, keys_all, values_all = heads_view[:, 0], heads_view[:, 1], heads_view[:, 2]
-    scores = jnp.einsum("sqhe,skhe->shqk", queries, keys_all, preferred_element_type=f32) * score_scale
-    scores = jnp.where(live[None, None, None, :], scores, masked_score)
-    probs = jax.nn.softmax(scores, axis=-1)
-    probs_low = probs.astype(bf16)
-    downward_part = jnp.einsum("srf,rd->sfd", activated, cotangent, preferred_element_type=f32).astype(bf16)
-    activated_grad = jnp.einsum("rd,sfd->srf", cotangent, downward_full, preferred_element_type=f32)
-    upward_grad = (activated_grad * slope).astype(bf16)
-    upward_part = jnp.einsum("rd,srf->sdf", entering_two, upward_grad, preferred_element_type=f32).astype(bf16)
-    normed_two_grad = jnp.einsum("srf,sdf->rd", upward_grad, upward_full, preferred_element_type=f32)
-    residual_part, gain_two_grad, shift_two_grad = norm_back_two(normed_two_grad)
-    residual_grad = residual_part + cotangent.astype(f32)
-    branch_grad = residual_grad.astype(bf16)
-    output_part = jnp.einsum("srh,rd->shd", attended, branch_grad, preferred_element_type=f32).astype(bf16)
-    attended_grad = jnp.einsum("rd,shd->srh", branch_grad, output_full, preferred_element_type=f32).astype(bf16)
-    attended_grad = attended_grad.reshape(PLANES, rows, 2, HEAD_DIM)
-    value_grad = jnp.einsum("shqk,sqhe->skhe", probs_low, attended_grad, preferred_element_type=f32).astype(bf16)
-    prob_grad = jnp.einsum("sqhe,skhe->shqk", attended_grad, values_all, preferred_element_type=f32)
-    score_grad = (probs * (prob_grad - jnp.sum(probs * prob_grad, axis=-1, keepdims=True))).astype(bf16)
-    query_grad = jnp.einsum("shqk,skhe->sqhe", score_grad, keys_all, preferred_element_type=f32) * score_scale
-    key_grad = jnp.einsum("shqk,sqhe->skhe", score_grad, queries, preferred_element_type=f32) * score_scale
-    projected_grad = jnp.stack([query_grad.astype(bf16), key_grad.astype(bf16), value_grad], axis=1)
-    projected_grad = projected_grad.reshape(PLANES, 3, rows, 2 * HEAD_DIM)
-    project_part = jnp.einsum(
-        "rod,sjrf->sojdf",
-        entering_one.reshape(rows, OWNERS, D // OWNERS),
-        projected_grad,
-        preferred_element_type=f32,
-    ).astype(bf16)
-    normed_grad = jnp.einsum("sjrf,sjdf->rd", projected_grad, project_full, preferred_element_type=f32)
-    input_part, gain_one_grad, shift_one_grad = norm_back_one(normed_grad)
-    input_grad = input_part + residual_grad
-    norm_part = jnp.stack([gain_one_grad, shift_one_grad, gain_two_grad, shift_two_grad])
-    matches = slots[:, None] == jnp.arange(LAT, dtype=jnp.int32)[None, :]
-    slot_of = jnp.argmax(matches, axis=0)
-    point_gradient = jnp.where(jnp.any(matches, axis=0)[:, None], input_grad[slot_of], 0.0)
-    (downward_summed, upward_summed, output_summed, project_blocks), norm_summed = reduce_gradients(
-        (downward_part, upward_part, output_part, project_part.reshape(PLANES, OWNERS * 384, 256)), norm_part
-    )
-    project_summed = jnp.transpose(project_blocks.reshape(3, D // OWNERS, 256), (1, 0, 2))
+    summed_blocks, norm_summed, point_gradient = run_backward(fulls, saved, cotangent, members, layer_norms)
+    downward_summed, upward_summed, output_summed, project_block = summed_blocks
+    project_summed = project_block.reshape(BLOCK, 3, 256)
     data_index = lax.axis_index("dp")
     norm_columns = norm_first.shape[1]
     norm_gradient = lax.dynamic_slice_in_dim(norm_summed, data_index * norm_columns, norm_columns, 1)

time: 324 us -> 254 us (0.78); the launches traced: 318 us -> 253 us
  matrix products: 46.1 us -> 0 us
  local copies, waits for them, and re-layouts: 28.4 us -> 14.2 us
  other arithmetic: 16.4 us -> 6.63 us
  Pallas kernels: 225 us -> 232 us
    dot_general x12 -> x0, matrix products: 42.7 us -> none  [the longest x1 7.09 us: on_device_cube(): jnp.einsum('rd,sfd->srf', cotangent, downward_full, preferred_element_typ...]
    reduce_sum x5 -> x0, other arithmetic: 6.55 us -> none  [the longest x4 4.84 us: layer_norm(): center = values - jnp.mean(values, axis=-1, keepdims=True)]
    pallas_call x1, Pallas kernels: 117 us -> 123 us  [run_backward(): pl.pallas_call(backward_kernel, out_shape=[jax.ShapeDtypeStruct(s, f32) f...]
    another operation x3 -> x0, local copies, waits for them, and re-layouts: 6.12 us -> none  [on_device_cube(): jnp.stack([query_grad.astype(bf16), key_grad.astype(bf16), value_grad], a...]
    reshape x2 -> x0, local copies, waits for them, and re-layouts: 4.68 us -> none  [the longest x1 3.68 us: on_device_cube(): heads_view = projected.reshape(PLANES, 3, rows, 2, HEAD_DIM)]
    unnamed x75 -> x59, local copies, waits for them, and re-layouts: 9.09 us -> 13 us
    slice x2 -> x0, local copies, waits for them, and re-layouts: 3.42 us -> none  [the longest x1 3.41 us: on_device_cube(): heads_view[:, 2]]
    sub x1 -> x0, matrix products: 3.4 us -> none  [on_device_cube(): probs = jax.nn.softmax(scores, axis=-1)]
where the time goes in v1:
time: 254 us; the launch traced here: 253 us
  Pallas kernels  232 us (91%)
  local copies, waits for them, and re-layouts  14.2 us (6%)
  other arithmetic  6.63 us (3%)
    pallas_call x1, Pallas kernels, run_backward(): pl.pallas_call(backward_kernel, out_shape=[jax.ShapeDtypeStruct(s, f32) f...  123 us
    pallas_call x1, Pallas kernels, run_forward(): pl.pallas_call(forward_kernel, out_shape=[jax.ShapeDtypeStruct(*a) for a...  108 us
    unnamed x59, local copies, waits for them, and re-layouts  13 us
    convert_element_type x4, other arithmetic, on_device_cube(): results += [summed, updated, one_new, two_new, updated.astype(bf16)]  5.33 us

profile of v1, /device:TPU:0, one launch (start us, length us, event | category | flops | bytes accessed | tf_op | source)
XLA Modules:
  0.0 253.3 jit_solution(6783373487311909793)
XLA Ops:
  0.7 0.0 copy-start.3
  0.7 0.7 copy-done.3
  1.4 0.7 copy-done.4
  2.1 108.1 %forward.1 = (bf16[4,3,1024,256]{3,2,1,0:T(8,128)(2,1)}, bf16[4,256,1024]{2,1,0:T(8,128)(2,1)}, bf16[4,1024,1024]{2,1,0:T(8,128)(2,1)}, bf16[4,1024,1024]{2,1,0:...) custom-call(bf16[3,1024,256]{2,1,0:T(8,128)(2,1)} %bitcast.4, ...), custom_call_target="tpu_custom_call" | custom-call | tf_op jit(solution)/shard_map/forward/pallas_call | solution.py:570
  110.1 0.0 copy-start
  110.2 0.8 copy-done
  110.9 0.8 copy-done.1
  111.7 0.8 copy-done.2
  112.5 123.5 %backward.1 = (f32[1024,128]{1,0:T(8,128)}, f32[128,1024]{1,0:T(8,128)}, f32[256,128]{1,0:T(8,128)}, f32[128,768]{1,0:T(8,128)}, f32[4,1024]{1,0:T(4,128)}, /*index=5*/f32[256,1024]{1,0:T(8,128)}) custom-call(bf16[4,3,1024,256]{3,2,1,0:T(8,128)(2,1)} %get-tuple-element.46.refs_0_, bf16[4,256,1024]{2,1,0:T(8,128)(2,1)} %get-tuple-element.47.refs_1_, ...), custom_call_target="tpu_custom_call" | custom-call | tf_op jit(solution)/shard_map/backward/pallas_call | solution.py:969
  236.0 0.0 copy-start.16
  236.0 0.0 copy-start.17
  236.0 1.2 copy.52
  237.3 0.9 copy.57
  238.2 0.0 copy-done.15
  238.2 0.2 copy.56
  238.4 0.0 copy-done.16
  238.4 0.2 copy.53
  238.5 0.0 copy-done.17
  238.5 0.2 copy.54
  238.7 0.3 fusion.12
  239.0 0.0 copy-start.14
  239.0 0.0 copy-start.18
  239.1 0.0 copy-start.19
  239.1 0.0 copy-start.20
  239.1 0.0 copy-start.6
  239.1 0.0 copy-start.9
  239.1 0.0 copy-start.10
  239.1 0.9 copy.58
  240.0 0.9 copy.59
  240.9 0.9 copy.60
  241.9 0.8 copy.61
  242.7 0.0 copy-done.14
  242.7 0.0 copy-done.18
  242.7 0.0 copy-done.19
  242.7 0.0 copy-done.20
  242.7 0.8 fusion.10
  243.5 0.0 copy-done.6
  243.5 0.0 copy-done.9
  243.5 0.0 copy-done.10
  243.6 2.7 %fusion.8 = (bf16[128,1024]{1,0:T(8,128)(2,1)}, f32[128,1024]{1,0:T(8,128)}, f32[128,1024]{1,0:T(8,128)}, f32[128,1024]{1,0:T(8,128)}) fusion(f32[128,1024]{1,0:T(8,128)S(1)} %copy-done.9, f32[128,1024]{1,0:T(8,128)S(1)} %copy-done.6, f32[128,1024]{1,0:T(8,128)S(1)} %copy-done.10, f32[128,1024]{1,0:T(8,128)} %param.38), kind=kLoop, calls=%fused_computation.22 | loop fusion | flops 2097152 | bytes 3932160 | tf_op jit(solution)/shard_map/convert_element_type | solution.py:1029
  246.2 0.0 copy-done.5
  246.3 1.5 fusion.6
  247.8 1.3 multiply_subtract_fusion.4
  249.1 1.0 copy.67
  250.1 1.0 copy.68
  251.0 0.7 copy.69
  251.7 0.8 copy.70
  252.5 0.8 copy.71
  (19 shorter events, 0.0 us)
Async XLA Ops:
  0.7 0.7 copy-start.3
  1.4 0.7 copy-start.4
  110.1 0.8 copy-start
  110.9 0.8 copy-start.1
  111.7 0.8 copy-start.2
  112.5 125.7 %copy-start.15 = (f32[128,3,256]{2,0,1:T(8,128)S(1)}, f32[128,3,256]{2,0,1:T(8,128)}, u32[]{:S(2)}) copy-start(f32[128,3,256]{2,0,1:T(8,128)} %param.30) | copy-start | bytes 1179652
  236.0 2.3 copy-start.16
  236.0 2.5 copy-start.17
  239.0 3.6 %copy-start.14 = (f32[256,128]{1,0:T(8,128)S(1)}, f32[256,128]{1,0:T(8,128)}, u32[]{:S(2)}) copy-start(f32[256,128]{1,0:T(8,128)} %get-tuple-element.169) | copy-start | bytes 393220
  239.0 3.6 %copy-start.18 = (f32[256,128]{1,0:T(8,128)S(1)}, f32[256,128]{1,0:T(8,128)}, u32[]{:S(2)}) copy-start(f32[256,128]{1,0:T(8,128)} %param.33) | copy-start | bytes 393220
  239.1 3.6 %copy-start.19 = (f32[256,128]{1,0:T(8,128)S(1)}, f32[256,128]{1,0:T(8,128)}, u32[]{:S(2)}) copy-start(f32[256,128]{1,0:T(8,128)} %param.34) | copy-start | bytes 393220
  239.1 3.6 %copy-start.20 = (f32[256,128]{1,0:T(8,128)S(1)}, f32[256,128]{1,0:T(8,128)}, u32[]{:S(2)}) copy-start(f32[256,128]{1,0:T(8,128)} %param.35) | copy-start | bytes 393220
  239.1 4.5 %copy-start.6 = (f32[128,1024]{1,0:T(8,128)S(1)}, f32[128,1024]{1,0:T(8,128)}, u32[]{:S(2)}) copy-start(f32[128,1024]{1,0:T(8,128)} %get-tuple-element.174) | copy-start | bytes 1572868
  239.1 4.5 %copy-start.9 = (f32[128,1024]{1,0:T(8,128)S(1)}, f32[128,1024]{1,0:T(8,128)}, u32[]{:S(2)}) copy-start(f32[128,1024]{1,0:T(8,128)} %param.36) | copy-start | bytes 1572868
  239.1 4.5 %copy-start.10 = (f32[128,1024]{1,0:T(8,128)S(1)}, f32[128,1024]{1,0:T(8,128)}, u32[]{:S(2)}) copy-start(f32[128,1024]{1,0:T(8,128)} %param.37) | copy-start | bytes 1572868
  243.5 2.7 %copy-start.5 = (f32[1024,128]{1,0:T(8,128)S(1)}, f32[1024,128]{1,0:T(8,128)}, u32[]{:S(2)}) copy-start(f32[1024,128]{1,0:T(8,128)} %get-tuple-element.179) | copy-start | bytes 1572868
  243.5 2.7 %copy-start.11 = (f32[1024,128]{1,0:T(8,128)S(1)}, f32[1024,128]{1,0:T(8,128)}, u32[]{:S(2)}) copy-start(f32[1024,128]{1,0:T(8,128)} %param.39) | copy-start | bytes 1572868
  243.5 2.7 %copy-start.12 = (f32[1024,128]{1,0:T(8,128)S(1)}, f32[1024,128]{1,0:T(8,128)}, u32[]{:S(2)}) copy-start(f32[1024,128]{1,0:T(8,128)} %param.40) | copy-start | bytes 1572868
  243.5 2.8 %copy-start.13 = (f32[1024,128]{1,0:T(8,128)S(1)}, f32[1024,128]{1,0:T(8,128)}, u32[]{:S(2)}) copy-start(f32[1024,128]{1,0:T(8,128)} %param.41) | copy-start | bytes 1572868
  246.2 1.6 copy-start.21
  246.2 1.6 copy-start.22
  246.2 2.9 %copy-start.7 = (f32[256,1024]{1,0:T(8,128)S(1)}, f32[256,1024]{1,0:T(8,128)}, u32[]{:S(2)}) copy-start(f32[256,1024]{1,0:T(8,128)} %get-tuple-element.162) | copy-start | bytes 3145732
  246.3 3.8 %copy-start.8 = (f32[256,1024]{1,0:T(8,128)S(1)}, f32[256,1024]{1,0:T(8,128)}, u32[]{:S(2)}) copy-start(f32[256,1024]{1,0:T(8,128)} %get-tuple-element.163) | copy-start | bytes 3145732

commit v2 on v1

--- a/solution.py
+++ b/solution.py
@@ -271,6 +271,9 @@
 SHARDS = ((3, D, 256), (256, D), (D, D), (D, D))
 
 
+SHORT = (3,)
+
+
 def place():
     dp = lax.axis_index("dp")
     return dp // 4, (dp // 2) % 2, dp % 2, lax.axis_index("mp")
@@ -355,7 +358,7 @@
         )
 
     def z_copy(w, plane, half, lane, k, target):
-        rows = block(w, half, spot[half], 1)
+        rows = block(w, half, pair[half], 2) if w in SHORT else block(w, half, spot[half], 1)
         return remote(w, plane, rows, z_send.at[w, lane, half], z_recv.at[w, k, half], target)
 
     def z_own(w, half):
@@ -463,76 +466,89 @@
         else:
             narrow(plane)
 
-    chunks = [(w, k) for w in range(4) for k in range(3)]
-    lag = (1, 3, 5, 7)
-
-    for w in range(4):
+    def send_own(w):
+        own_load(w).wait()
+        for half in HALVES:
+            z_own(w, half).start()
+
+        @pl.when(is_mid)
+        def _():
+            for half in HALVES:
+                z_own_across(w, half).start()
+
+        keep_weight(w, None).start()
+
+    def take(w, k):
+        for half in HALVES:
+            z_arrived(w, k, half).wait_recv()
+            (b_copy if w in SHORT else a_copy)(w, k, half).start()
+
+        @pl.when(is_mid)
+        def _():
+            for half in HALVES:
+                z_pass(w, k, half).start()
+
+    def finished(w, k):
+        if w == 1:
+            return
+        compute(w, k)
+        if k == 2:
+            if w == 0:
+                keep(2).start()
+                keep(3).start()
+                for at in (None, 0, 1, 2):
+                    compute(1, at)
+                keep(4).start()
+                enter_two()
+                keep(5).start()
+                compute(2, None)
+            elif w == 2:
+                keep(6).start()
+                keep(7).start()
+                compute(3, None)
+
+    order = (1, 0, 2, 3)
+    chunks = [(w, k) for w in order for k in range(3)]
+    for w in order:
         own_load(w).start()
-    for step in range(len(chunks) + lag[3]):
-        for w in range(4):
-            if step == max(0, 3 * w - 3):
-                own_load(w).wait()
-                keep_weight(w, None).start()
+    send_own(order[0])
+    taken = 0
+    for step in range(len(chunks) + 3):
+        while taken < min(len(chunks), step + 1):
+            if taken % 3 == 0 and taken // 3 + 1 < 4:
+                send_own(order[taken // 3 + 1])
+            take(*chunks[taken])
+            taken += 1
+        if 0 <= step - 1 < len(chunks):
+            w, k = chunks[step - 1]
+            if w not in SHORT:
                 for half in HALVES:
-                    z_own(w, half).start()
-
-                @pl.when(is_mid)
-                def _():
-                    for half in HALVES:
-                        z_own_across(w, half).start()
-
-        if 0 <= step - lag[0] < len(chunks):
-            w, k = chunks[step - lag[0]]
-            for half in HALVES:
-                z_arrived(w, k, half).wait_recv()
-                a_copy(w, k, half).start()
-
-            @pl.when(is_mid)
-            def _():
-                for half in HALVES:
-                    z_pass(w, k, half).start()
-
-        if 0 <= step - lag[1] < len(chunks):
-            w, k = chunks[step - lag[1]]
-            for half in HALVES:
-                a_copy(w, k, half).wait_recv()
-                b_copy(w, k, half).start()
-        if 0 <= step - lag[2] < len(chunks):
-            w, k = chunks[step - lag[2]]
+                    a_copy(w, k, half).wait_recv()
+                    b_copy(w, k, half).start()
+        if 0 <= step - 2 < len(chunks):
+            w, k = chunks[step - 2]
             for half in HALVES:
                 b_copy(w, k, half).wait_recv()
                 c_copy(w, k, half).start()
-        if step == 0:
+        if step == 1:
             enter()
             keep(0).start()
             keep(1).start()
             compute(0, None)
-        if 0 <= step - lag[3] < len(chunks):
-            w, k = chunks[step - lag[3]]
+        if 0 <= step - 3 < len(chunks):
+            w, k = chunks[step - 3]
             for half in HALVES:
                 c_copy(w, k, half).wait_recv()
             keep_weight(w, k).start()
-            if k == 0 and w > 0:
-                compute(w, None)
-            compute(w, k)
-            if k == 2:
-                if w == 0:
-                    keep(2).start()
-                    keep(3).start()
-                elif w == 1:
-                    keep(4).start()
-                    enter_two()
-                    keep(5).start()
-                elif w == 2:
-                    keep(6).start()
-                    keep(7).start()
+            finished(w, k)
     out = pltpu.make_async_copy(latents, latents_out, latents_sem)
     out.start()
     for w in range(4):
         for half in HALVES:
             z_own(w, half).wait_send()
             for k in range(3):
-                a_copy(w, k, half).wait_send()
+                if w not in SHORT:
+                    a_copy(w, k, half).wait_send()
                 b_copy(w, k, half).wait_send()
                 c_copy(w, k, half).wait_send()
 
@@ -578,7 +594,7 @@
         + [dma((4, 4)), dma((8,)), dma],
         name="forward",
         compiler_params=pltpu.CompilerParams(
-            collective_id=0, has_side_effects=True, vmem_limit_bytes=52 << 20
+            collective_id=0, has_side_effects=True, vmem_limit_bytes=60 << 20
         ),
     )(*shards, points, members, layer_norms)
     return result[:4], result[4:12], result[12]
@@ -587,24 +603,29 @@
 WIDTHS = (D, D, 256, 3 * 256)
 BLOCK = D // OWNERS
 HALF = BLOCK // 2
-RING = 3
+RING = 2
 UNITS = [(w, i) for w in (0, 1, 3, 2) for i in range(PLANES)]
+EARLY_Z = (0, 1)
+OWN = PLANES - 1
+LAG_ONE, LAG_TWO, LAG_Z, TAIL = 2, 4, 6, 7
+OWN_AT = {0: 13, 1: 17}
+FINISH_AT = {0: 15, 1: 20, 3: 19, 2: 22}
 
 
 def backward_kernel(*refs):
     fulls, saved_in = refs[0:4], refs[4:12]
     cotangent_in, members, norms = refs[12:15]
-    outs, norm_out, points_out = refs[15:19], refs[19], refs[20]
-    saved, cotangent = refs[21:29], refs[29]
+    outs, norm_out, points_out = refs[15:23], refs[23], refs[24]
+    saved, cotangent = refs[25:33], refs[33]
     inputs, entering_one, projected, attended, residual, entering_two, activated, slope = saved
-    down_ring, up_ring, output_full, project_ring = refs[30:34]
-    turned, upward_grad, residual_grad, branch_grad, projected_grad, normed_grad = refs[34:40]
-    ring = refs[40]
-    acc, one_in, two_in, z_in = refs[41:45], refs[45:49], refs[49:53], refs[53:57]
-    norm_own, norm_in, norm_planes = refs[57:60]
-    saved_sem, cotangent_sem, weight_sem = refs[60:63]
-    c_send, c_recv, one_send, one_recv, two_send, two_recv, z_send, z_recv = refs[63:71]
-    norm_send, norm_recv = refs[71:73]
+    down_ring, up_ring, output_full, project_ring = refs[34:38]
+    turned, upward_grad, residual_grad, branch_grad, projected_grad, normed_grad = refs[38:44]
+    ring = refs[44]
+    acc, one_in, two_in, z_in = refs[45:49], refs[49:53], refs[53:57], refs[57:61]
+    norm_own, norm_in, norm_planes = refs[61:64]
+    saved_sem, cotangent_sem, weight_sem, points_sem = refs[64:68]
+    c_send, c_recv, one_send, one_recv, two_send, two_recv, z_send, z_recv = refs[68:76]
+    norm_send, norm_recv = refs[76:78]
     f32, bf16 = jnp.float32, jnp.bfloat16
     y, x, c, z = place()
 
@@ -616,8 +637,11 @@
     for n in (6, 5, 7, 4, 2, 3, 1, 0):
         load(n).start()
 
+    is_mid = jnp.logical_or(z == 1, z == 2)
+    is_end = jnp.logical_not(is_mid)
+
     def plane_of(i):
-        return (z + 1 + i) % PLANES
+        return z if i == OWN else arrival(z, 2 - i)
 
     def weight_load(w, i):
         plane = plane_of(i)
@@ -633,6 +657,7 @@
     greet(y, x, c, z)
     sibling = device(y, x, 1 - c, z)
     over_x, over_y = device(y, 1 - x, c, z), device(1 - y, x, c, z)
+    beside, across = device(y, x, c, arrival(z, 0)), device(y, x, c, 3 - z)
 
     def remote(src, dst, send, recv, target):
         return pltpu.make_async_remote_copy(
@@ -660,13 +685,50 @@
         w, i = UNITS[t]
         rows = half_rows(half)
         src = acc[w].at[i, y, 1 - x, rows] if half == 0 else acc[w].at[i, 1 - y, x, rows]
+        slot = 0 if w in EARLY_Z else i
         return remote(
-            src, two_in[w].at[i, half], two_send.at[t, half], two_recv.at[t, half], (over_x, over_y)[half]
+            src, two_in[w].at[slot, half], two_send.at[t, half], two_recv.at[t, half], (over_x, over_y)[half]
         )
 
-    def z_copy(t):
+    def z_piece(t, half):
         w, i = UNITS[t]
-        return remote(acc[w].at[i, y, x], z_in[w].at[i], z_send.at[t], z_recv.at[t], device(y, x, c, plane_of(i)))
+        if w in EARLY_Z:
+            return acc[w].at[i, y, :, half_rows(half)] if half == 0 else acc[w].at[i, :, x, half_rows(half)]
+        return acc[w].at[i, y, x, half_rows(half)]
+
+    def z_copy(t, half, slot, target):
+        w = UNITS[t][0]
+        return remote(
+            z_piece(t, half), z_in[w].at[slot, half], z_send.at[t, half], z_recv.at[w, slot, half], target
+        )
+
+    def z_add(t, slot):
+        w = UNITS[t][0]
+        for half in HALVES:
+            z_copy(t, half, slot, beside).wait_recv()
+            piece = z_piece(t, half)
+            if w in EARLY_Z:
+                for k in (0, 1):
+                    add_rows(piece.at[k], z_in[w].at[slot, half, k])
+            else:
+                add_rows(piece, z_in[w].at[slot, half])
+
+    def z_send_end(t):
+        i = UNITS[t][1]
+
+        @pl.when(is_end)
+        def _():
+            for half in HALVES:
+                z_copy(t, half, 2 - i, beside).start()
+
+    def z_send_mid(t):
+        i = UNITS[t][1]
+
+        @pl.when(is_mid)
+        def _():
+            z_add(t, (2, 1, 3)[i])
+            for half in HALVES:
+                z_copy(t, half, (3, 4, 0)[i], (across, across, beside)[i]).start()
 
     def add_rows(target, source):
         def body(r, carry):
@@ -730,30 +792,65 @@
             for k in (0, 1):
                 target = acc[w].at[i, y, k, rows] if half == 0 else acc[w].at[i, k, x, rows]
                 add_rows(target, one_in[w].at[i, half, k])
-            two_copy(t, half).start()
+            if w not in EARLY_Z:
+                two_copy(t, half).start()
+        if w in EARLY_Z and i < OWN:
+            z_send_end(t)
 
     def after_two(t):
         w, i = UNITS[t]
+        if w in EARLY_Z:
+            return
         for half in HALVES:
             two_copy(t, half).wait()
             add_rows(acc[w].at[i, y, x, half_rows(half)], two_in[w].at[i, half])
-        if i < PLANES - 1:
-            z_copy(t).start()
+        if i < OWN:
+            z_send_end(t)
+
+    def own_hop(w):
+        t = UNITS.index((w, OWN))
+        z_add(t, 0)
+
+        @pl.when(is_mid)
+        def _():
+            z_add(t, 4)
+
+        for half in HALVES:
+            two_copy(t, half).start()
 
     def finish(w):
-        for t, unit in enumerate(UNITS):
-            if unit[0] == w and unit[1] < PLANES - 1:
-                z_copy(t).wait()
+        t = UNITS.index((w, OWN))
+        mine = acc[w].at[OWN, y, x]
+        if w in EARLY_Z:
+            for half in HALVES:
+                two_copy(t, half).wait()
+        else:
+            for half in HALVES:
+                z_copy(t, half, 0, beside).wait_recv()
+
+            @pl.when(is_mid)
+            def _():
+                for half in HALVES:
+                    z_copy(t, half, 4, across).wait_recv()
 
         def body(n, carry):
             columns = pl.ds(pl.multiple_of(n * 128, 128), 128)
-            total = acc[w].at[PLANES - 1, y, x][:, columns].astype(f32)
-            for i in range(PLANES - 1):
-                total = total + z_in[w].at[i][:, columns].astype(f32)
-            if w in (0, 2):
-                outs[w][columns, :] = total.T
+            first = mine[:, columns].astype(f32)
+            if w in EARLY_Z:
+                second = [two_in[w][0, half, :, columns] for half in HALVES]
             else:
-                outs[w][:, columns] = total
+                second = [z_in[w][0, half, :, columns] for half in HALVES]
+                third = [z_in[w][4, half, :, columns] for half in HALVES]
+                first += jnp.where(is_mid, jnp.concatenate(third, axis=0).astype(f32), 0.0)
+            second = jnp.concatenate(second, axis=0).astype(f32)
+            for n_out, value in ((w, first), (4 + w, second)):
+                if w in (0, 2):
+                    outs[n_out][columns, :] = value.T.astype(outs[n_out].dtype)
+                elif w == 1:
+                    outs[n_out][:, columns] = value.astype(outs[n_out].dtype)
+                else:
+                    part_columns = pl.ds(pl.multiple_of((n % 2) * 128, 128), 128)
+                    outs[n_out][n // 2, :, part_columns] = value.astype(outs[n_out].dtype)
             return carry
 
         lax.fori_loop(0, WIDTHS[w] // 128, body, 0)
@@ -857,6 +954,8 @@
 
         norm_back(inputs, norms[0:1, :], 0, store)
 
+    points_copy = pltpu.make_async_copy(inputs, points_out, points_sem)
+
     def points_back():
         slot_of = lax.broadcasted_iota(jnp.int32, (ROWS, ROWS), 0) == members[...]
         chosen = slot_of.astype(f32).astype(bf16)
@@ -868,9 +967,10 @@
                 low = rest.astype(bf16)
                 total += dot(chosen, low, NN)
                 rest = rest - low.astype(f32)
-            points_out[:, columns] = total
+            inputs[:, columns] = total
 
         tiles(4, 256, pick)
+        points_copy.start()
 
     def norm_step(k):
         return remote(norm_own.at[k], norm_in.at[k], norm_send.at[k], norm_recv.at[k], (sibling, over_x, over_y)[k])
@@ -906,21 +1006,21 @@
             turn(branch_grad, 2)
 
     count = len(UNITS)
-    lag = (2, 3, 4)
     before(0)
     produce(0)
-    input_at = 1 + [t for t, unit in enumerate(UNITS) if unit == (3, 3)][0]
-    last = {w: max(t for t, unit in enumerate(UNITS) if unit[0] == w) for w in range(4)}
-    for step in range(count + lag[2]):
+    input_at = 1 + UNITS.index((3, OWN))
+    for step in range(count + TAIL):
         if step + 1 < count:
             before(step + 1)
             produce(step + 1)
         if step < count:
             join(step)
-        if 0 <= step - lag[0] < count:
-            after_one(step - lag[0])
-        if 0 <= step - lag[1] < count:
-            after_two(step - lag[1])
+        if 0 <= step - LAG_ONE < count:
+            after_one(step - LAG_ONE)
+        if 0 <= step - LAG_TWO < count:
+            after_two(step - LAG_TWO)
+        if 0 <= step - LAG_Z < count and UNITS[step - LAG_Z][1] < OWN:
+            z_send_mid(step - LAG_Z)
         if step == input_at:
             load(0).wait()
             input_back()
@@ -938,13 +1038,20 @@
                 for d in (1, 2, 3):
                     norm_plane(d).start()
         for w in range(4):
-            if step - lag[2] == last[w]:
+            if w in EARLY_Z and step == OWN_AT[w]:
+                own_hop(w)
+            if step == FINISH_AT[w]:
                 finish(w)
     for d in (1, 2, 3):
         norm_plane(d).wait()
     norm_out[...] = (norm_planes[0] + norm_planes[1]) + (norm_planes[2] + norm_planes[3])
     for t in range(count - RING, count):
         pair_copy(t).wait_send()
+    for t in range(count):
+        if UNITS[t][1] < OWN:
+            for half in HALVES:
+                z_copy(t, half, 0, beside).wait_send()
+    points_copy.wait()
 
 
 def run_backward(fulls, saved, cotangent, members, layer_norms):
@@ -958,26 +1065,28 @@
     scratch += [pltpu.VMEM((RING, 2, 2, BLOCK, D), bf16)]
     scratch += [pltpu.VMEM((4, 2, 2, BLOCK, n), bf16) for n in WIDTHS]
     scratch += [pltpu.VMEM((4, 2, 2, HALF, n), bf16) for n in WIDTHS]
-    scratch += [pltpu.VMEM((4, 2, HALF, n), bf16) for n in WIDTHS]
-    scratch += [pltpu.VMEM((3, BLOCK, n), bf16) for n in WIDTHS]
+    scratch += [pltpu.VMEM((1 if w in EARLY_Z else 4, 2, HALF, WIDTHS[w]), bf16) for w in range(4)]
+    scratch += [pltpu.VMEM((5, 2) + ((2,) if w in EARLY_Z else ()) + (HALF, WIDTHS[w]), bf16) for w in range(4)]
     scratch += [pltpu.VMEM((n, 4, D), f32) for n in (4, 3, 4)]
     dma = pltpu.SemaphoreType.DMA
-    scratch += [dma((8,)), dma, dma((4, 4)), dma((16,)), dma((16,))]
-    scratch += [dma((16, 2))] * 4 + [dma((16,))] * 2 + [dma((6,))] * 2
+    scratch += [dma((8,)), dma, dma((4, 4)), dma, dma((16,)), dma((16,))]
+    scratch += [dma((16, 2))] * 5 + [dma((4, 5, 2))] + [dma((6,))] * 2
     anywhere, vmem = pl.BlockSpec(memory_space=pl.ANY), pl.BlockSpec(memory_space=pltpu.VMEM)
-    blocks = [(WIDTHS[0], BLOCK), (BLOCK, WIDTHS[1]), (WIDTHS[2], BLOCK), (BLOCK, WIDTHS[3])]
+    blocks = [(WIDTHS[0], BLOCK), (BLOCK, WIDTHS[1]), (WIDTHS[2], BLOCK), (3, BLOCK, 256)]
     result = pl.pallas_call(
         backward_kernel,
-        out_shape=[jax.ShapeDtypeStruct(s, f32) for s in blocks + [(4, D), (ROWS, D)]],
+        out_shape=[jax.ShapeDtypeStruct(blocks[w], bf16 if w in EARLY_Z else f32) for w in range(4)]
+        + [jax.ShapeDtypeStruct(s, bf16) for s in blocks]
+        + [jax.ShapeDtypeStruct((4, D), f32), jax.ShapeDtypeStruct((ROWS, D), f32)],
         in_specs=[anywhere] * 13 + [vmem] * 2,
-        out_specs=[vmem] * 6,
+        out_specs=[vmem] * 9 + [anywhere],
         scratch_shapes=scratch,
         name="backward",
         compiler_params=pltpu.CompilerParams(
             collective_id=1, has_side_effects=True, vmem_limit_bytes=60 << 20
         ),
     )(*fulls, *saved, cotangent, members, layer_norms)
-    return result[:4], result[4], result[5]
+    return result[:4], result[4:8], result[8], result[9]
 
 
 def on_device_cube(
@@ -1011,22 +1120,24 @@
         members,
         layer_norms,
     )
-    summed_blocks, norm_summed, point_gradient = run_backward(fulls, saved, cotangent, members, layer_norms)
-    downward_summed, upward_summed, output_summed, project_block = summed_blocks
-    project_summed = project_block.reshape(BLOCK, 3, 256)
+    firsts, seconds, norm_summed, point_gradient = run_backward(fulls, saved, cotangent, members, layer_norms)
     data_index = lax.axis_index("dp")
     norm_columns = norm_first.shape[1]
     norm_gradient = lax.dynamic_slice_in_dim(norm_summed, data_index * norm_columns, norm_columns, 1)
     norm_current = lax.dynamic_slice_in_dim(layer_norms, data_index * norm_columns, norm_columns, 1)
     results = [latents, point_gradient]
-    for master, summed, first, second, rate in (
-        (project_master, project_summed, project_first, project_second, D ** (-0.5)),
-        (output_master, output_summed, output_first, output_second, max(1, D * 4 // LAT) ** (-0.5)),
-        (upward_master, upward_summed, upward_first, upward_second, D ** (-0.5)),
-        (downward_master, downward_summed, downward_first, downward_second, FF ** (-0.5)),
+    swap = lambda array: jnp.transpose(array, (1, 0, 2))
+    for w, states, rate in (
+        (3, [swap(a) for a in (project_master, project_first, project_second)], D ** (-0.5)),
+        (2, [output_master, output_first, output_second], max(1, D * 4 // LAT) ** (-0.5)),
+        (1, [upward_master, upward_first, upward_second], D ** (-0.5)),
+        (0, [downward_master, downward_first, downward_second], FF ** (-0.5)),
     ):
+        master, first, second = states
+        summed = firsts[w].astype(jnp.float32) + seconds[w].astype(jnp.float32)
         updated, one_new, two_new = adamw_step(master, summed, first, second, rate)
-        results += [summed, updated, one_new, two_new, updated.astype(bf16)]
+        new = [summed, updated, one_new, two_new, updated.astype(bf16)]
+        results += [swap(a) for a in new] if w == 3 else new
     norm_new = adamw_step(norm_current, norm_gradient, norm_first, norm_second, 0.2)
     results += [norm_gradient, *norm_new]
     return tuple(results)

time: 254 us -> 222 us (0.87)
  Pallas kernels: 232 us -> 210 us
  local copies, waits for them, and re-layouts: 14.2 us -> 2.79 us
    pallas_call x1, Pallas kernels: 108 us -> 97 us  [run_forward(): pl.pallas_call(forward_kernel, out_shape=[jax.ShapeDtypeStruct(*a) for a...]
    pallas_call x1, Pallas kernels: 123 us -> 113 us  [run_backward(): pl.pallas_call(backward_kernel, out_shape=[jax.ShapeDtypeStruct(blocks[w]...]
    unnamed x59 -> x46, local copies, waits for them, and re-layouts: 13 us -> 2.79 us
    transpose x0 -> x1, other arithmetic: none -> 2.73 us  [on_device_cube(): swap = lambda array: jnp.transpose(array, (1, 0, 2))]
    convert_element_type x4 -> x3, other arithmetic: 5.33 us -> 3.91 us  [on_device_cube(): new = [summed, updated, one_new, two_new, updated.astype(bf16)]]
where the time goes in v2:
time: 222 us
  Pallas kernels  210 us (95%)
  other arithmetic  8.03 us (4%)
  local copies, waits for them, and re-layouts  2.79 us (1%)
    pallas_call x1, Pallas kernels, run_backward(): pl.pallas_call(backward_kernel, out_shape=[jax.ShapeDtypeStruct(blocks[w]...  113 us
    pallas_call x1, Pallas kernels, run_forward(): pl.pallas_call(forward_kernel, out_shape=[jax.ShapeDtypeStruct(*a) for a...  97 us

profile of v2, /device:TPU:0, one launch (start us, length us, event | category | flops | bytes accessed | tf_op | source)
XLA Modules:
  0.0 221.5 jit_solution(3987156029058160980)
XLA Ops:
  0.7 97.0 %forward.1 = (bf16[4,3,1024,256]{3,2,1,0:T(8,128)(2,1)}, bf16[4,256,1024]{2,1,0:T(8,128)(2,1)}, bf16[4,1024,1024]{2,1,0:T(8,128)(2,1)}, bf16[4,1024,1024]{2,1,0:...) custom-call(bf16[3,1024,256]{2,1,0:T(8,128)(2,1)} %bitcast.34, ...), custom_call_target="tpu_custom_call" | custom-call | tf_op jit(solution)/shard_map/forward/pallas_call | solution.py:586
  97.7 0.0 copy-start.8
  97.7 0.0 copy-start.9
  97.7 0.0 copy-start.10
  97.7 112.8 %backward.1 = (bf16[1024,128]{1,0:T(8,128)(2,1)}, bf16[128,1024]{1,0:T(8,128)(2,1)}, f32[256,128]{1,0:T(8,128)}, f32[3,128,256]{2,1,0:T(8,128)}, bf16[1024,128]{...) custom-call(bf16[4,3,1024,256]{3,2,1,0:T(8,128)(2,1)} %get-tuple-ele, ...), custom_call_target="tpu_custom_call" | custom-call | tf_op jit(solution)/shard_map/backward/pallas_call | solution.py:1076
  210.5 0.0 copy-start.15
  210.6 0.0 copy-start.16
  210.6 0.0 copy-start.17
  210.6 0.0 copy-start.18
  210.6 0.0 copy-start.19
  210.6 0.0 copy-done.8
  210.6 0.0 copy-done.9
  210.6 0.0 copy-done.10
  210.6 0.0 copy-start.2
  210.6 0.0 copy-start.3
  210.7 0.0 copy-start.4
  210.7 0.0 copy-start.13
  210.7 0.0 copy-start.14
  210.7 2.7 %convert_bitcast_fusion = (bf16[128,3,256]{2,0,1:T(8,128)(2,1)}, f32[3,128,256]{2,1,0:T(8,128)}, f32[128,3,256]{2,0,1:T(8,128)}, f32[128,3,256]{2,0,1:T(8,128)}, f32[128,3,256]{2,0,1:T(8,128)}) fusion(f32[128,3,256]{2,0,1:T(8,128)S(1)} %copy-done.8, f32[3,128,256]{2,1,0:T(8,128)} %get-tuple-element.63, bf16[3,128,256]{2,1,0:T(8,128)(2,1)} %get-tuple-element.64, ...), kind=kLoop, calls=%fused_computation.19 | loop fusion | flops 1769472 | bytes 3538944 | tf_op jit(solution)/shard_map/transpose | solution.py:1129
  213.4 0.0 copy-done.15
  213.4 0.0 copy-done.16
  213.4 0.0 copy-done.17
  213.4 0.0 copy-done.18
  213.4 0.0 copy-done.19
  213.4 0.8 fusion.15
  214.3 0.0 copy-done.2
  214.3 0.0 copy-done.3
  214.3 0.0 copy-done.4
  214.3 0.0 copy-done.13
  214.3 0.0 copy-done.14
  214.3 0.0 copy-start.5
  214.3 0.0 copy-start.6
  214.3 0.0 copy-start.7
  214.4 0.0 copy-start.11
  214.4 0.0 copy-start.12
  214.4 1.6 fusion.13
  215.9 0.0 copy-done.5
  215.9 0.0 copy-done.6
  215.9 0.3 copy-done.7
  216.3 0.3 copy-done.11
  216.5 0.1 copy-done.12
  216.7 1.5 fusion.11
  218.2 0.0 copy-done.20
  218.2 0.0 copy-done.21
  218.2 1.4 multiply_subtract_fusion.3
  219.6 0.0 copy-done
  219.6 1.0 copy.50
  220.6 1.0 copy.51
  (5 shorter events, 0.0 us)
Async XLA Ops:
  97.7 112.9 %copy-start.8 = (f32[128,3,256]{2,0,1:T(8,128)S(1)}, f32[128,3,256]{2,0,1:T(8,128)}, u32[]{:S(2)}) copy-start(f32[128,3,256]{2,0,1:T(8,128)} %param.32) | copy-start | bytes 1179652
  97.7 112.9 %copy-start.9 = (f32[128,3,256]{2,0,1:T(8,128)S(1)}, f32[128,3,256]{2,0,1:T(8,128)}, u32[]{:S(2)}) copy-start(f32[128,3,256]{2,0,1:T(8,128)} %param.31) | copy-start | bytes 1179652
  97.7 112.9 %copy-start.10 = (f32[128,3,256]{2,0,1:T(8,128)S(1)}, f32[128,3,256]{2,0,1:T(8,128)}, u32[]{:S(2)}) copy-start(f32[128,3,256]{2,0,1:T(8,128)} %param.30) | copy-start | bytes 1179652
  210.5 2.9 %copy-start.15 = (f32[256,128]{1,0:T(8,128)S(1)}, f32[256,128]{1,0:T(8,128)}, u32[]{:S(2)}) copy-start(f32[256,128]{1,0:T(8,128)} %param.33) | copy-start | bytes 393220
  210.6 2.9 %copy-start.16 = (f32[256,128]{1,0:T(8,128)S(1)}, f32[256,128]{1,0:T(8,128)}, u32[]{:S(2)}) copy-start(f32[256,128]{1,0:T(8,128)} %param.34) | copy-start | bytes 393220
  210.6 2.9 %copy-start.17 = (f32[256,128]{1,0:T(8,128)S(1)}, f32[256,128]{1,0:T(8,128)}, u32[]{:S(2)}) copy-start(f32[256,128]{1,0:T(8,128)} %param.35) | copy-start | bytes 393220
  210.6 2.9 %copy-start.18 = (f32[256,128]{1,0:T(8,128)S(1)}, f32[256,128]{1,0:T(8,128)}, u32[]{:S(2)}) copy-start(f32[256,128]{1,0:T(8,128)} %get-tuple-element.65) | copy-start | bytes 393220
  210.6 2.9 %copy-start.19 = (bf16[256,128]{1,0:T(8,128)(2,1)S(1)}, bf16[256,128]{1,0:T(8,128)(2,1)}, u32[]{:S(2)}) copy-start(bf16[256,128]{1,0:T(8,128)(2,1)} %get-tuple-element.66) | copy-start | bytes 196612
  210.6 3.7 %copy-start.2 = (f32[128,1024]{1,0:T(8,128)S(1)}, f32[128,1024]{1,0:T(8,128)}, u32[]{:S(2)}) copy-start(f32[128,1024]{1,0:T(8,128)} %param.36) | copy-start | bytes 1572868
  210.6 3.6 %copy-start.3 = (f32[128,1024]{1,0:T(8,128)S(1)}, f32[128,1024]{1,0:T(8,128)}, u32[]{:S(2)}) copy-start(f32[128,1024]{1,0:T(8,128)} %param.37) | copy-start | bytes 1572868
  210.7 3.6 %copy-start.4 = (f32[128,1024]{1,0:T(8,128)S(1)}, f32[128,1024]{1,0:T(8,128)}, u32[]{:S(2)}) copy-start(f32[128,1024]{1,0:T(8,128)} %param.38) | copy-start | bytes 1572868
  210.7 3.6 %copy-start.13 = (bf16[128,1024]{1,0:T(8,128)(2,1)S(1)}, bf16[128,1024]{1,0:T(8,128)(2,1)}, u32[]{:S(2)}) copy-start(bf16[128,1024]{1,0:T(8,128)(2,1)} %get-tuple-element.67) | copy-start | bytes 786436
  210.7 3.6 %copy-start.14 = (bf16[128,1024]{1,0:T(8,128)(2,1)S(1)}, bf16[128,1024]{1,0:T(8,128)(2,1)}, u32[]{:S(2)}) copy-start(bf16[128,1024]{1,0:T(8,128)(2,1)} %get-tuple-element.68) | copy-start | bytes 786436
  214.3 1.6 copy-start.5
  214.3 1.6 copy-start.6
  214.3 1.9 copy-start.7
  214.4 2.2 copy-start.11
  214.4 2.3 %copy-start.12 = (bf16[1024,128]{1,0:T(8,128)(2,1)S(1)}, bf16[1024,128]{1,0:T(8,128)(2,1)}, u32[]{:S(2)}) copy-start(bf16[1024,128]{1,0:T(8,128)(2,1)} %get-tuple-element.70) | copy-start | bytes 786436
  216.7 1.5 copy-start.20
  216.7 1.5 copy-start.21
  216.7 2.9 %copy-start = (f32[256,1024]{1,0:T(8,128)S(1)}, f32[256,1024]{1,0:T(8,128)}, u32[]{:S(2)}) copy-start(f32[256,1024]{1,0:T(8,128)} %get-tuple-element.122) | copy-start | bytes 3145732
  218.2 2.4 %copy-start.1 = (f32[256,1024]{1,0:T(8,128)S(1)}, f32[256,1024]{1,0:T(8,128)}, u32[]{:S(2)}) copy-start(f32[256,1024]{1,0:T(8,128)} %get-tuple-element.123) | copy-start | bytes 3145732

commit v3 on v2

--- a/solution.py
+++ b/solution.py
@@ -269,9 +269,32 @@
 ROWS = LAT
 HALVES = (0, 1)
 SHARDS = ((3, D, 256), (256, D), (D, D), (D, D))
-
-
+GATHER_ORDER = (1, 0, 2, 3)
 SHORT = (3,)
+CHUNKS = [(w, k) for w in GATHER_ORDER for k in range(3)]
+SLOTS = 3
+LOADS = [(0, None), (0, 0), (0, 1), (0, 2)]
+LOADS += [(2, None), (2, 0), (2, 1), (2, 2)]
+LOADS += [(3, None), (3, 0), (3, 1), (3, 2)]
+LOADS += [(2, 2), (2, 1), (2, 0), (2, None)]
+LOADS += [(0, 2), (0, 1), (0, 0), (0, None)]
+
+WIDTHS = (D, D, 256, 3 * 256)
+BLOCK = D // OWNERS
+HALF = BLOCK // 2
+RING = 2
+OWN = PLANES - 1
+UNITS = [(w, i) for w in (0, 1, 3, 2) for i in range(PLANES)]
+EARLY_Z = (0, 1)
+TURNED_AT = (0, 1, 1, 0)
+LAG_ONE, LAG_TWO, LAG_Z, TAIL = 2, 4, 6, 7
+OWN_AT = {0: 13, 1: 17}
+FINISH_AT = {0: 15, 1: 20, 3: 19, 2: 22}
+JOIN_FROM = 13
+
+NN = ((1,), (0,))
+NT = ((1,), (1,))
+TN = ((0,), (0,))
 
 
 def place():
@@ -300,11 +323,6 @@
     return lax.dot_general(a, b, (contract, ((), ())), preferred_element_type=jnp.float32)
 
 
-NN = ((1,), (0,))
-NT = ((1,), (1,))
-TN = ((0,), (0,))
-
-
 def tiles(count, size, body):
     def step(n, carry):
         body(pl.ds(pl.multiple_of(n * size, size), size))
@@ -322,22 +340,43 @@
     lax.fori_loop(0, ROWS // strip, step, 0)
 
 
-def forward_kernel(*refs):
-    shards, (points, members, norms) = refs[0:4], refs[4:7]
-    fulls_out, saved_out, latents_out = refs[7:11], refs[11:19], refs[19]
-    fulls, saved, latents = refs[20:24], refs[24:32], refs[32]
-    inputs, entering_one, projected, attended, residual, entering_two, activated, slope = saved
-    own_sem, z_send, z_recv, a_send, a_recv, b_send, b_recv, c_send, c_recv = refs[33:42]
-    weight_sem, saved_sem, latents_sem = refs[42:45]
+def step_kernel(*refs):
+    f32, bf16 = jnp.float32, jnp.bfloat16
+    shards, (points, cotangent, members, norms) = refs[0:4], refs[4:8]
+    outs, norm_out, latents_out, points_out, fulls = refs[8:16], refs[16], refs[17], refs[18], refs[19:23]
+    inputs, entering_one, projected, attended, residual, entering_two, activated, slope, latents = refs[23:32]
+    turned, upward_grad, branch_grad, projected_grad, normed_grad = refs[32:37]
+    slots, output_full, ring = refs[37:40]
+    acc, one_in, two_in, z_in = refs[40:44], refs[44:48], refs[48:52], refs[52:56]
+    norm_own, norm_in, norm_planes = refs[56:59]
+    load_sem, output_sem, out_sem = refs[59:62]
+    gz_send, gz_recv, ga_send, ga_recv, gb_send, gb_recv, gc_send, gc_recv = refs[62:70]
+    c_send, c_recv, one_send, one_recv, two_send, two_recv, z_send, z_recv = refs[70:78]
+    norm_send, norm_recv = refs[78:80]
+    residual_grad = residual
     y, x, c, z = place()
-    greet(y, x, c, z)
     is_mid = jnp.logical_or(z == 1, z == 2)
+    is_end = jnp.logical_not(is_mid)
     sibling = device(y, x, 1 - c, z)
     over_x, over_y = device(y, 1 - x, c, z), device(1 - y, x, c, z)
     beside, across = device(y, x, c, arrival(z, 0)), device(y, x, c, 3 - z)
 
+    def plane_at(k):
+        return z if k is None else arrival(z, k)
+
+    def plane_of(i):
+        return z if i == OWN else arrival(z, 2 - i)
+
+    def remote(src, dst, send, recv, target):
+        return pltpu.make_async_remote_copy(
+            src_ref=src, dst_ref=dst, send_sem=send, recv_sem=recv, device_id=target, device_id_type=MESH
+        )
+
+    def rows_of(ref, w, rows):
+        return ref.at[:, rows, :] if w == 0 else ref.at[rows, :]
+
     def view(w, plane, rows):
-        return fulls[w].at[plane, :, rows, :] if w == 0 else fulls[w].at[plane, rows, :]
+        return rows_of(fulls[w].at[plane], w, rows)
 
     def block(w, half, first, count):
         height = SHARDS[w][-2]
@@ -347,63 +386,89 @@
     spot = (c * 4 + y * 2 + x, c * 4 + x * 2 + y)
     pair = (c * 4 + y * 2, c * 4 + x * 2)
 
-    def remote(w, plane, rows, send, recv, target):
-        return pltpu.make_async_remote_copy(
-            src_ref=view(w, plane, rows),
-            dst_ref=view(w, plane, rows),
-            send_sem=send,
-            recv_sem=recv,
-            device_id=target,
-            device_id_type=MESH,
-        )
-
-    def z_copy(w, plane, half, lane, k, target):
-        rows = block(w, half, pair[half], 2) if w in SHORT else block(w, half, spot[half], 1)
-        return remote(w, plane, rows, z_send.at[w, lane, half], z_recv.at[w, k, half], target)
-
-    def z_own(w, half):
-        return z_copy(w, z, half, 0, 0, beside)
-
-    def z_own_across(w, half):
-        return z_copy(w, z, half, 1, 1, across)
-
-    def z_pass(w, k, half):
+    def gz_rows(w, half):
+        return block(w, half, pair[half], 2) if w in SHORT else block(w, half, spot[half], 1)
+
+    def gz_own(w, half, lane, slot, target):
+        rows = gz_rows(w, half)
+        send, recv = gz_send.at[w, lane, half], gz_recv.at[w, slot, half]
+        return remote(rows_of(shards[w], w, rows), view(w, z, rows), send, recv, target)
+
+    def gz_beside(w, half):
+        return gz_own(w, half, 0, 0, beside)
+
+    def gz_across(w, half):
+        return gz_own(w, half, 1, 1, across)
+
+    def gz_foreign(w, k, half, lane, slot, target):
+        here = view(w, arrival(z, k), gz_rows(w, half))
+        return remote(here, here, gz_send.at[w, lane, half], gz_recv.at[w, slot, half], target)
+
+    def gz_pass(w, k, half):
         lane, target, slot = ((2, across, 2), (3, beside, 1), (4, beside, 2))[k]
-        return z_copy(w, arrival(z, k), half, lane, slot, target)
-
-    def z_arrived(w, k, half):
-        return z_copy(w, arrival(z, k), half, 0, k, beside)
-
-    def a_copy(w, k, half):
-        rows = block(w, half, spot[half], 1)
-        return remote(
-            w, arrival(z, k), rows, a_send.at[w, k, half], a_recv.at[w, k, half], (over_x, over_y)[half]
-        )
-
-    def b_copy(w, k, half):
-        rows = block(w, half, pair[half], 2)
-        return remote(
-            w, arrival(z, k), rows, b_send.at[w, k, half], b_recv.at[w, k, half], (over_y, over_x)[half]
-        )
-
-    def c_copy(w, k, half):
-        rows = block(w, half, c * 4, 4)
-        return remote(w, arrival(z, k), rows, c_send.at[w, k, half], c_recv.at[w, k, half], sibling)
-
-    def own_load(w):
-        return pltpu.make_async_copy(shards[w], fulls[w].at[z], own_sem.at[w])
-
-    def keep_weight(w, k):
-        plane = z if k is None else arrival(z, k)
-        slot = 3 if k is None else k
-        return pltpu.make_async_copy(fulls[w].at[plane], fulls_out[w].at[plane], weight_sem.at[w, slot])
-
-    def keep(n):
-        return pltpu.make_async_copy(saved[n], saved_out[n], saved_sem.at[n])
+        return gz_foreign(w, k, half, lane, slot, target)
+
+    def gz_arrived(w, k, half):
+        return gz_foreign(w, k, half, 0, k, beside)
+
+    def ga_copy(w, k, half):
+        here = view(w, arrival(z, k), block(w, half, spot[half], 1))
+        return remote(here, here, ga_send.at[w, k, half], ga_recv.at[w, k, half], (over_x, over_y)[half])
+
+    def gb_copy(w, k, half):
+        here = view(w, arrival(z, k), block(w, half, pair[half], 2))
+        return remote(here, here, gb_send.at[w, k, half], gb_recv.at[w, k, half], (over_y, over_x)[half])
+
+    def gc_copy(w, k, half):
+        here = view(w, arrival(z, k), block(w, half, c * 4, 4))
+        return remote(here, here, gc_send.at[w, k, half], gc_recv.at[w, k, half], sibling)
+
+    def send_own(w):
+        for half in HALVES:
+            gz_beside(w, half).start()
+
+        @pl.when(is_mid)
+        def _():
+            for half in HALVES:
+                gz_across(w, half).start()
+
+    def take(w, k):
+        for half in HALVES:
+            gz_arrived(w, k, half).wait_recv()
+            (gb_copy if w in SHORT else ga_copy)(w, k, half).start()
+
+        @pl.when(is_mid)
+        def _():
+            for half in HALVES:
+                gz_pass(w, k, half).start()
+
+    def loads(n):
+        w, k = LOADS[n]
+        source = shards[w] if k is None else fulls[w].at[arrival(z, k)]
+        if w != 0:
+            return [pltpu.make_async_copy(source, slots.at[n % SLOTS], load_sem.at[n, 0])]
+        return [
+            pltpu.make_async_copy(
+                source.at[part], slots.at[n % SLOTS, :, part * 256 : (part + 1) * 256], load_sem.at[n, part]
+            )
+            for part in range(3)
+        ]
+
+    def start_load(n):
+        for copy in loads(n):
+            copy.start()
+
+    def wait_load(n):
+        for copy in loads(n):
+            copy.wait()
+
+    def output_load(k):
+        source = shards[1] if k is None else fulls[1].at[arrival(z, k)]
+        return pltpu.make_async_copy(source, output_full.at[plane_at(k)], output_sem.at[3 if k is None else k])
 
     def enter():
         slot_of = lax.broadcasted_iota(jnp.int32, (ROWS, ROWS), 0) == members[...]
-        chosen = slot_of.astype(jnp.float32).astype(jnp.bfloat16)
+        chosen = slot_of.astype(f32).astype(bf16)
 
         def pick(columns):
             inputs[:, columns] = dot(chosen, points[:, columns], TN)
@@ -412,23 +477,29 @@
         norm_rows(inputs, entering_one, norms[0:1, :], norms[1:2, :])
         residual[...] = inputs[...]
 
-    def project(plane):
+    def softmax_parts(plane, span):
+        queries, keys_all = projected[plane, 0, :, span], projected[plane, 1, :, span]
+        scores = jnp.where(members[...] >= 0, dot(queries, keys_all, NT) * HEAD_DIM ** (-0.5), masked_score)
+        exponent = jnp.exp(scores - jnp.max(scores, axis=-1, keepdims=True))
+        return queries, keys_all, exponent * (1.0 / jnp.sum(exponent, axis=-1, keepdims=True))
+
+    def project_attend(n):
+        wait_load(n)
+        plane, slot = plane_at(LOADS[n][1]), n % SLOTS
         for part in range(3):
-            projected[plane, part] = dot(entering_one[...], fulls[0][plane, part], NN).astype(jnp.bfloat16)
-
-    def attend(plane):
-        live = members[...] >= 0
+            right = slots[slot, :, part * 256 : (part + 1) * 256]
+            projected[plane, part] = dot(entering_one[...], right, NN).astype(bf16)
         for head in range(2):
             span = slice(head * HEAD_DIM, (head + 1) * HEAD_DIM)
-            queries, keys_all, values_all = (projected[plane, part, :, span] for part in range(3))
-            scores = jnp.where(live, dot(queries, keys_all, NT) * HEAD_DIM ** (-0.5), masked_score)
-            exponent = jnp.exp(scores - jnp.max(scores, axis=-1, keepdims=True))
-            probs = exponent * (1.0 / jnp.sum(exponent, axis=-1, keepdims=True))
-            attended[plane, :, span] = dot(probs.astype(jnp.bfloat16), values_all, NN).astype(jnp.bfloat16)
-
-    def branch(plane):
+            probs = softmax_parts(plane, span)[2]
+            attended[plane, :, span] = dot(probs.astype(bf16), projected[plane, 2, :, span], NN).astype(bf16)
+
+    def branch(k):
+        plane = plane_at(k)
+        output_load(k).wait()
+
         def body(columns):
-            residual[:, columns] += dot(attended[plane], fulls[1][plane, :, columns], NN)
+            residual[:, columns] += dot(attended[plane], output_full[plane, :, columns], NN)
 
         tiles(4, 256, body)
 
@@ -436,233 +507,31 @@
         norm_rows(residual, entering_two, norms[2:3, :], norms[3:4, :])
         latents[...] = residual[...]
 
-    def widen(plane):
+    def widen(n):
+        wait_load(n)
+        plane, slot = plane_at(LOADS[n][1]), n % SLOTS
+
         def body(columns):
-            u = dot(entering_two[...], fulls[2][plane, :, columns], NN)
+            u = dot(entering_two[...], slots[slot, :, columns], NN)
             square = u * u
             bend = jnp.tanh(0.7978845608028654 * u * (1.0 + 0.044715 * square))
-            activated[plane, :, columns] = (0.5 * u * (1.0 + bend)).astype(jnp.bfloat16)
+            activated[plane, :, columns] = (0.5 * u * (1.0 + bend)).astype(bf16)
             slope[plane, :, columns] = 0.5 * (1.0 + bend) + 0.5 * u * (1.0 - bend * bend) * (
                 0.7978845608028654 * (1.0 + 3.0 * 0.044715 * square)
             )
 
         tiles(4, 256, body)
 
-    def narrow(plane):
+    def narrow(n):
+        wait_load(n)
+        plane, slot = plane_at(LOADS[n][1]), n % SLOTS
+
         def body(columns):
-            latents[:, columns] += dot(activated[plane], fulls[3][plane, :, columns], NN)
+            latents[:, columns] += dot(activated[plane], slots[slot, :, columns], NN)
+            product = dot(cotangent[...], slots[slot, columns, :], NT)
+            upward_grad[plane, :, columns] = (product * slope[plane, :, columns]).astype(bf16)
 
         tiles(4, 256, body)
-
-    def compute(w, k):
-        plane = z if k is None else arrival(z, k)
-        if w == 0:
-            project(plane)
-            attend(plane)
-        elif w == 1:
-            branch(plane)
-        elif w == 2:
-            widen(plane)
-        else:
-            narrow(plane)
-
-    def send_own(w):
-        own_load(w).wait()
-        for half in HALVES:
-            z_own(w, half).start()
-
-        @pl.when(is_mid)
-        def _():
-            for half in HALVES:
-                z_own_across(w, half).start()
-
-        keep_weight(w, None).start()
-
-    def take(w, k):
-        for half in HALVES:
-            z_arrived(w, k, half).wait_recv()
-            (b_copy if w in SHORT else a_copy)(w, k, half).start()
-
-        @pl.when(is_mid)
-        def _():
-            for half in HALVES:
-                z_pass(w, k, half).start()
-
-    def finished(w, k):
-        if w == 1:
-            return
-        compute(w, k)
-        if k == 2:
-            if w == 0:
-                keep(2).start()
-                keep(3).start()
-                for at in (None, 0, 1, 2):
-                    compute(1, at)
-                keep(4).start()
-                enter_two()
-                keep(5).start()
-                compute(2, None)
-            elif w == 2:
-                keep(6).start()
-                keep(7).start()
-                compute(3, None)
-
-    order = (1, 0, 2, 3)
-    chunks = [(w, k) for w in order for k in range(3)]
-    for w in order:
-        own_load(w).start()
-    send_own(order[0])
-    taken = 0
-    for step in range(len(chunks) + 3):
-        while taken < min(len(chunks), step + 1):
-            if taken % 3 == 0 and taken // 3 + 1 < 4:
-                send_own(order[taken // 3 + 1])
-            take(*chunks[taken])
-            taken += 1
-        if 0 <= step - 1 < len(chunks):
-            w, k = chunks[step - 1]
-            if w not in SHORT:
-                for half in HALVES:
-                    a_copy(w, k, half).wait_recv()
-                    b_copy(w, k, half).start()
-        if 0 <= step - 2 < len(chunks):
-            w, k = chunks[step - 2]
-            for half in HALVES:
-                b_copy(w, k, half).wait_recv()
-                c_copy(w, k, half).start()
-        if step == 1:
-            enter()
-            keep(0).start()
-            keep(1).start()
-            compute(0, None)
-        if 0 <= step - 3 < len(chunks):
-            w, k = chunks[step - 3]
-            for half in HALVES:
-                c_copy(w, k, half).wait_recv()
-            keep_weight(w, k).start()
-            finished(w, k)
-    out = pltpu.make_async_copy(latents, latents_out, latents_sem)
-    out.start()
-    for w in range(4):
-        for half in HALVES:
-            z_own(w, half).wait_send()
-            for k in range(3):
-                if w not in SHORT:
-                    a_copy(w, k, half).wait_send()
-                b_copy(w, k, half).wait_send()
-                c_copy(w, k, half).wait_send()
-
-    @pl.when(is_mid)
-    def _():
-        for w in range(4):
-            for half in HALVES:
-                z_own_across(w, half).wait_send()
-                for k in range(3):
-                    z_pass(w, k, half).wait_send()
-
-    for w in range(4):
-        for k in (None, 0, 1, 2):
-            keep_weight(w, k).wait()
-    for n in range(8):
-        keep(n).wait()
-    out.wait()
-
-
-def run_forward(shards, points, members, layer_norms):
-    f32, bf16 = jnp.float32, jnp.bfloat16
-    saved = [
-        ((ROWS, D), f32),
-        ((ROWS, D), bf16),
-        ((PLANES, 3, ROWS, 256), bf16),
-        ((PLANES, ROWS, 256), bf16),
-        ((ROWS, D), f32),
-        ((ROWS, D), bf16),
-        ((PLANES, ROWS, D), bf16),
-        ((PLANES, ROWS, D), f32),
-    ]
-    anywhere, vmem = pl.BlockSpec(memory_space=pl.ANY), pl.BlockSpec(memory_space=pltpu.VMEM)
-    fulls = [((PLANES,) + s, bf16) for s in SHARDS]
-    dma = pltpu.SemaphoreType.DMA
-    result = pl.pallas_call(
-        forward_kernel,
-        out_shape=[jax.ShapeDtypeStruct(*a) for a in fulls + saved + [((ROWS, D), f32)]],
-        in_specs=[anywhere] * 4 + [vmem] * 3,
-        out_specs=[anywhere] * 13,
-        scratch_shapes=[pltpu.VMEM(*a) for a in fulls + saved + [((ROWS, D), f32)]]
-        + [dma((4,)), dma((4, 5, 2))]
-        + [dma((4, 3, 2))] * 7
-        + [dma((4, 4)), dma((8,)), dma],
-        name="forward",
-        compiler_params=pltpu.CompilerParams(
-            collective_id=0, has_side_effects=True, vmem_limit_bytes=60 << 20
-        ),
-    )(*shards, points, members, layer_norms)
-    return result[:4], result[4:12], result[12]
-
-
-WIDTHS = (D, D, 256, 3 * 256)
-BLOCK = D // OWNERS
-HALF = BLOCK // 2
-RING = 2
-UNITS = [(w, i) for w in (0, 1, 3, 2) for i in range(PLANES)]
-EARLY_Z = (0, 1)
-OWN = PLANES - 1
-LAG_ONE, LAG_TWO, LAG_Z, TAIL = 2, 4, 6, 7
-OWN_AT = {0: 13, 1: 17}
-FINISH_AT = {0: 15, 1: 20, 3: 19, 2: 22}
-
-
-def backward_kernel(*refs):
-    fulls, saved_in = refs[0:4], refs[4:12]
-    cotangent_in, members, norms = refs[12:15]
-    outs, norm_out, points_out = refs[15:23], refs[23], refs[24]
-    saved, cotangent = refs[25:33], refs[33]
-    inputs, entering_one, projected, attended, residual, entering_two, activated, slope = saved
-    down_ring, up_ring, output_full, project_ring = refs[34:38]
-    turned, upward_grad, residual_grad, branch_grad, projected_grad, normed_grad = refs[38:44]
-    ring = refs[44]
-    acc, one_in, two_in, z_in = refs[45:49], refs[49:53], refs[53:57], refs[57:61]
-    norm_own, norm_in, norm_planes = refs[61:64]
-    saved_sem, cotangent_sem, weight_sem, points_sem = refs[64:68]
-    c_send, c_recv, one_send, one_recv, two_send, two_recv, z_send, z_recv = refs[68:76]
-    norm_send, norm_recv = refs[76:78]
-    f32, bf16 = jnp.float32, jnp.bfloat16
-    y, x, c, z = place()
-
-    def load(n):
-        return pltpu.make_async_copy(saved_in[n], saved[n], saved_sem.at[n])
-
-    cotangent_load = pltpu.make_async_copy(cotangent_in, cotangent, cotangent_sem)
-    cotangent_load.start()
-    for n in (6, 5, 7, 4, 2, 3, 1, 0):
-        load(n).start()
-
-    is_mid = jnp.logical_or(z == 1, z == 2)
-    is_end = jnp.logical_not(is_mid)
-
-    def plane_of(i):
-        return z if i == OWN else arrival(z, 2 - i)
-
-    def weight_load(w, i):
-        plane = plane_of(i)
-        if w == 2:
-            return pltpu.make_async_copy(fulls[1], output_full, weight_sem.at[2, 0])
-        target = (down_ring, up_ring, None, project_ring.at[i % 2])[w]
-        return pltpu.make_async_copy(fulls[(3, 2, 1, 0)[w]].at[plane], target, weight_sem.at[w, i])
-
-    weight_load(0, 0).start()
-    weight_load(1, 0).start()
-    weight_load(2, 0).start()
-    weight_load(3, 0).start()
-    greet(y, x, c, z)
-    sibling = device(y, x, 1 - c, z)
-    over_x, over_y = device(y, 1 - x, c, z), device(1 - y, x, c, z)
-    beside, across = device(y, x, c, arrival(z, 0)), device(y, x, c, 3 - z)
-
-    def remote(src, dst, send, recv, target):
-        return pltpu.make_async_remote_copy(
-            src_ref=src, dst_ref=dst, send_sem=send, recv_sem=recv, device_id=target, device_id_type=MESH
-        )
 
     def pair_copy(t):
         w, i = UNITS[t]
@@ -744,7 +613,7 @@
             right = projected_grad[plane, n]
         else:
             right = (activated, upward_grad, attended)[w][plane, :, columns]
-        return dot(turned[w, parity], right, NN)
+        return dot(turned[TURNED_AT[w], parity], right, NN)
 
     def over_tiles(w, body):
         if w == 2:
@@ -859,31 +728,22 @@
         for owner in range(OWNERS):
             columns = slice(owner * BLOCK, (owner + 1) * BLOCK)
             place_at = slice((owner // 2) * BLOCK, (owner // 2 + 1) * BLOCK)
-            turned[w, owner % 2, place_at, :] = source[:, columns].T
+            turned[TURNED_AT[w], owner % 2, place_at, :] = source[:, columns].T
 
     def hidden_back(i):
-        plane = plane_of(i)
-        weight_load(0, i).wait()
-
-        def grad(columns):
-            product = dot(cotangent[...], down_ring[columns, :], NT)
-            upward_grad[plane, :, columns] = (product * slope[plane, :, columns]).astype(bf16)
-
-        tiles(4, 256, grad)
-        if i < PLANES - 1:
-            weight_load(0, i + 1).start()
-        weight_load(1, i).wait()
+        n = 12 + i
+        wait_load(n)
+        plane, slot = plane_of(i), n % SLOTS
 
         def normed(columns):
-            product = dot(upward_grad[plane], up_ring[columns, :], NT)
+            product = dot(upward_grad[plane], slots[slot, columns, :], NT)
             if i == 0:
                 normed_grad[:, columns] = product
             else:
                 normed_grad[:, columns] += product
 
         tiles(4, 256, normed)
-        if i < PLANES - 1:
-            weight_load(1, i + 1).start()
+        start_load(n + SLOTS)
 
     def norm_back(source, gain, row, store):
         norm_own[0, row : row + 2, :] = jnp.zeros((2, D), f32)
@@ -914,39 +774,36 @@
 
     def attend_back(i):
         plane = plane_of(i)
-        live = members[...] >= 0
         attended_grad = dot(branch_grad[...], output_full[plane], NT).astype(bf16)
         scale = HEAD_DIM ** (-0.5)
         for head in range(2):
             span = slice(head * HEAD_DIM, (head + 1) * HEAD_DIM)
-            queries, keys_all, values_all = (projected[plane, part, :, span] for part in range(3))
-            scores = jnp.where(live, dot(queries, keys_all, NT) * scale, masked_score)
-            exponent = jnp.exp(scores - jnp.max(scores, axis=-1, keepdims=True))
-            probs = exponent * (1.0 / jnp.sum(exponent, axis=-1, keepdims=True))
+            queries, keys_all, probs = softmax_parts(plane, span)
             grad = attended_grad[:, span]
             projected_grad[plane, 2, :, span] = dot(probs.astype(bf16), grad, TN).astype(bf16)
-            prob_grad = dot(grad, values_all, NT)
+            prob_grad = dot(grad, projected[plane, 2, :, span], NT)
             inner = jnp.sum(probs * prob_grad, axis=-1, keepdims=True)
             score_grad = (probs * (prob_grad - inner)).astype(bf16)
             projected_grad[plane, 0, :, span] = (dot(score_grad, keys_all, NN) * scale).astype(bf16)
             projected_grad[plane, 1, :, span] = (dot(score_grad, queries, TN) * scale).astype(bf16)
 
     def project_back(i):
-        plane = plane_of(i)
-        weight_load(3, i).wait()
-        if i < PLANES - 1:
-            weight_load(3, i + 1).start()
+        n = 16 + i
+        wait_load(n)
+        plane, slot = plane_of(i), n % SLOTS
 
         def normed(columns):
-            total = dot(projected_grad[plane, 0], project_ring[i % 2, 0, columns, :], NT)
+            total = dot(projected_grad[plane, 0], slots[slot, columns, 0:256], NT)
             for part in (1, 2):
-                total += dot(projected_grad[plane, part], project_ring[i % 2, part, columns, :], NT)
+                total += dot(projected_grad[plane, part], slots[slot, columns, part * 256 : (part + 1) * 256], NT)
             if i == 0:
                 normed_grad[:, columns] = total
             else:
                 normed_grad[:, columns] += total
 
         tiles(4, 256, normed)
+        if n + SLOTS < len(LOADS):
+            start_load(n + SLOTS)
 
     def input_back():
         def store(rows, part):
@@ -954,7 +811,7 @@
 
         norm_back(inputs, norms[0:1, :], 0, store)
 
-    points_copy = pltpu.make_async_copy(inputs, points_out, points_sem)
+    points_copy = pltpu.make_async_copy(inputs, points_out, out_sem.at[1])
 
     def points_back():
         slot_of = lax.broadcasted_iota(jnp.int32, (ROWS, ROWS), 0) == members[...]
@@ -981,39 +838,29 @@
 
     def before(t):
         w, i = UNITS[t]
-        if (w, i) == (0, 0):
-            cotangent_load.wait()
+        if w == 0 and i == 0:
             turn(cotangent, 0)
-            load(6).wait()
         elif w == 1:
             if i == 0:
-                load(5).wait()
                 turn(entering_two, 1)
-                load(7).wait()
             hidden_back(i)
         elif w == 3:
             if i == 0:
-                load(4).wait()
                 residual_back()
-                load(2).wait()
-                load(1).wait()
                 turn(entering_one, 3)
-                weight_load(2, 0).wait()
             attend_back(i)
             project_back(i)
-        elif i == 0:
-            load(3).wait()
+        elif w == 2 and i == 0:
             turn(branch_grad, 2)
 
     count = len(UNITS)
-    before(0)
-    produce(0)
     input_at = 1 + UNITS.index((3, OWN))
-    for step in range(count + TAIL):
-        if step + 1 < count:
+
+    def reduce_step(step):
+        if 0 <= step + 1 < count:
             before(step + 1)
             produce(step + 1)
-        if step < count:
+        if 0 <= step < count:
             join(step)
         if 0 <= step - LAG_ONE < count:
             after_one(step - LAG_ONE)
@@ -1022,7 +869,6 @@
         if 0 <= step - LAG_Z < count and UNITS[step - LAG_Z][1] < OWN:
             z_send_mid(step - LAG_Z)
         if step == input_at:
-            load(0).wait()
             input_back()
             norm_step(0).start()
         if step == count:
@@ -1042,9 +888,78 @@
                 own_hop(w)
             if step == FINISH_AT[w]:
                 finish(w)
+
+    latents_copy = pltpu.make_async_copy(latents, latents_out, out_sem.at[0])
+    start_load(0)
+    output_load(None).start()
+    greet(y, x, c, z)
+    send_own(GATHER_ORDER[0])
+    starts = {6: (1,), 7: (2,), 8: (3, 4), 9: (5,), 10: (6,), 11: (7, 8), 12: (9,), 13: (10,), 14: (11, 12), 15: (13,)}
+    uses = {7: (1,), 8: (2,), 9: (3, 4), 10: (5,), 11: (6,), 12: (7, 8), 13: (9,), 14: (10,), 15: (11,)}
+    for step in range(JOIN_FROM + count + TAIL):
+        if step < len(CHUNKS):
+            if step % 3 == 0 and step // 3 + 1 < 4:
+                send_own(GATHER_ORDER[step // 3 + 1])
+            take(*CHUNKS[step])
+        if 0 <= step - 1 < len(CHUNKS):
+            w, k = CHUNKS[step - 1]
+            if w not in SHORT:
+                for half in HALVES:
+                    ga_copy(w, k, half).wait_recv()
+                    gb_copy(w, k, half).start()
+        if 0 <= step - 2 < len(CHUNKS):
+            w, k = CHUNKS[step - 2]
+            for half in HALVES:
+                gb_copy(w, k, half).wait_recv()
+                gc_copy(w, k, half).start()
+        if 0 <= step - 3 < len(CHUNKS):
+            w, k = CHUNKS[step - 3]
+            for half in HALVES:
+                gc_copy(w, k, half).wait_recv()
+            if w == 1:
+                output_load(k).start()
+        for n in starts.get(step, ()):
+            start_load(n)
+        if step == 1:
+            enter()
+            project_attend(0)
+        for n in uses.get(step, ()):
+            w, k = LOADS[n]
+            if w == 0:
+                project_attend(n)
+                if k == 2:
+                    for at in (None, 0, 1, 2):
+                        branch(at)
+                    enter_two()
+            elif w == 2:
+                widen(n)
+            else:
+                narrow(n)
+        if step == 15:
+            latents_copy.start()
+            start_load(14)
+        reduce_step(step - JOIN_FROM)
     for d in (1, 2, 3):
         norm_plane(d).wait()
     norm_out[...] = (norm_planes[0] + norm_planes[1]) + (norm_planes[2] + norm_planes[3])
+    for w, k in CHUNKS:
+        for half in HALVES:
+            if w not in SHORT:
+                ga_copy(w, k, half).wait_send()
+            gb_copy(w, k, half).wait_send()
+            gc_copy(w, k, half).wait_send()
+    for w in range(4):
+        for half in HALVES:
+            gz_beside(w, half).wait_send()
+
+    @pl.when(is_mid)
+    def _():
+        for w in range(4):
+            for half in HALVES:
+                gz_across(w, half).wait_send()
+                for k in range(3):
+                    gz_pass(w, k, half).wait_send()
+
     for t in range(count - RING, count):
         pair_copy(t).wait_send()
     for t in range(count):
@@ -1052,16 +967,23 @@
             for half in HALVES:
                 z_copy(t, half, 0, beside).wait_send()
     points_copy.wait()
-
-
-def run_backward(fulls, saved, cotangent, members, layer_norms):
+    latents_copy.wait()
+
+
+def run_step(shards, points, cotangent, members, layer_norms):
     f32, bf16 = jnp.float32, jnp.bfloat16
+    blocks = [(WIDTHS[0], BLOCK), (BLOCK, WIDTHS[1]), (WIDTHS[2], BLOCK), (3, BLOCK, 256)]
+    out_shape = [jax.ShapeDtypeStruct(blocks[w], bf16 if w in EARLY_Z else f32) for w in range(4)]
+    out_shape += [jax.ShapeDtypeStruct(s, bf16) for s in blocks]
+    out_shape += [jax.ShapeDtypeStruct(s, f32) for s in ((4, D), (ROWS, D), (ROWS, D))]
+    out_shape += [jax.ShapeDtypeStruct((PLANES,) + s, bf16) for s in SHARDS]
     rows_f32, rows_bf16 = pltpu.VMEM((ROWS, D), f32), pltpu.VMEM((ROWS, D), bf16)
-    scratch = [pltpu.VMEM(a.shape, a.dtype) for a in saved] + [rows_bf16]
-    scratch += [pltpu.VMEM((D, D), bf16)] * 2
-    scratch += [pltpu.VMEM((PLANES, 256, D), bf16), pltpu.VMEM((2, 3, D, 256), bf16)]
-    scratch += [pltpu.VMEM((4, 2, D // 2, ROWS), bf16), pltpu.VMEM((PLANES, ROWS, D), bf16)]
-    scratch += [rows_f32, rows_bf16, pltpu.VMEM((PLANES, 3, ROWS, 256), bf16), rows_f32]
+    parts = pltpu.VMEM((PLANES, 3, ROWS, 256), bf16)
+    hidden = pltpu.VMEM((PLANES, ROWS, D), bf16)
+    scratch = [rows_f32, rows_bf16, parts, pltpu.VMEM((PLANES, ROWS, 256), bf16), rows_f32, rows_bf16, hidden]
+    scratch += [pltpu.VMEM((PLANES, ROWS, D), f32), rows_f32]
+    scratch += [pltpu.VMEM((2, 2, D // 2, ROWS), bf16), hidden, rows_bf16, parts, rows_f32]
+    scratch += [pltpu.VMEM((SLOTS, D, D), bf16), pltpu.VMEM((PLANES, 256, D), bf16)]
     scratch += [pltpu.VMEM((RING, 2, 2, BLOCK, D), bf16)]
     scratch += [pltpu.VMEM((4, 2, 2, BLOCK, n), bf16) for n in WIDTHS]
     scratch += [pltpu.VMEM((4, 2, 2, HALF, n), bf16) for n in WIDTHS]
@@ -1069,24 +991,22 @@
     scratch += [pltpu.VMEM((5, 2) + ((2,) if w in EARLY_Z else ()) + (HALF, WIDTHS[w]), bf16) for w in range(4)]
     scratch += [pltpu.VMEM((n, 4, D), f32) for n in (4, 3, 4)]
     dma = pltpu.SemaphoreType.DMA
-    scratch += [dma((8,)), dma, dma((4, 4)), dma, dma((16,)), dma((16,))]
-    scratch += [dma((16, 2))] * 5 + [dma((4, 5, 2))] + [dma((6,))] * 2
+    scratch += [dma((len(LOADS), 3)), dma((4,)), dma((2,)), dma((4, 5, 2))]
+    scratch += [dma((4, 3, 2))] * 7
+    scratch += [dma((16,))] * 2 + [dma((16, 2))] * 5 + [dma((4, 5, 2))] + [dma((6,))] * 2
     anywhere, vmem = pl.BlockSpec(memory_space=pl.ANY), pl.BlockSpec(memory_space=pltpu.VMEM)
-    blocks = [(WIDTHS[0], BLOCK), (BLOCK, WIDTHS[1]), (WIDTHS[2], BLOCK), (3, BLOCK, 256)]
     result = pl.pallas_call(
-        backward_kernel,
-        out_shape=[jax.ShapeDtypeStruct(blocks[w], bf16 if w in EARLY_Z else f32) for w in range(4)]
-        + [jax.ShapeDtypeStruct(s, bf16) for s in blocks]
-        + [jax.ShapeDtypeStruct((4, D), f32), jax.ShapeDtypeStruct((ROWS, D), f32)],
-        in_specs=[anywhere] * 13 + [vmem] * 2,
-        out_specs=[vmem] * 9 + [anywhere],
+        step_kernel,
+        out_shape=out_shape,
+        in_specs=[anywhere] * 4 + [vmem] * 4,
+        out_specs=[vmem] * 9 + [anywhere] * 6,
         scratch_shapes=scratch,
-        name="backward",
+        name="step",
         compiler_params=pltpu.CompilerParams(
-            collective_id=1, has_side_effects=True, vmem_limit_bytes=60 << 20
+            collective_id=0, has_side_effects=True, vmem_limit_bytes=60 << 20
         ),
-    )(*fulls, *saved, cotangent, members, layer_norms)
-    return result[:4], result[4:8], result[8], result[9]
+    )(*shards, points, cotangent, members, layer_norms)
+    return result[:4], result[4:8], result[8], result[9], result[10]
 
 
 def on_device_cube(
@@ -1114,13 +1034,13 @@
     norm_second,
 ):
     bf16 = jnp.bfloat16
-    fulls, saved, latents = run_forward(
+    firsts, seconds, norm_summed, latents, point_gradient = run_step(
         (jnp.transpose(project_weight, (1, 0, 2)), output_weight, upward_weight, downward_weight),
         points,
+        cotangent,
         members,
         layer_norms,
     )
-    firsts, seconds, norm_summed, point_gradient = run_backward(fulls, saved, cotangent, members, layer_norms)
     data_index = lax.axis_index("dp")
     norm_columns = norm_first.shape[1]
     norm_gradient = lax.dynamic_slice_in_dim(norm_summed, data_index * norm_columns, norm_columns, 1)

time: 222 us -> 219 us (0.986)
    pallas_call x2 -> x1, Pallas kernels: 210 us -> 208 us  [run_step(): pl.pallas_call(step_kernel, out_shape=out_shape, in_specs=[anywhere] * 4...]
where the time goes in v3:
time: 219 us
  Pallas kernels  208 us (95%)
  other arithmetic  7.89 us (4%)
    pallas_call x1, Pallas kernels, run_step(): pl.pallas_call(step_kernel, out_shape=out_shape, in_specs=[anywhere] * 4...  208 us
    convert_element_type x3, other arithmetic, on_device_cube(): new = [summed, updated, one_new, two_new, updated.astype(bf16)]  5.07 us

profile of v3, /device:TPU:0, one launch (start us, length us, event | category | flops | bytes accessed | tf_op | source)
XLA Modules:
  0.0 218.7 jit_solution(1740237231685688261)
XLA Ops:
  0.7 0.0 copy-start.2
  0.7 0.0 copy-start.3
  0.7 0.0 copy-start.4
  0.7 207.8 %step.1 = (bf16[1024,128]{1,0:T(8,128)(2,1)}, bf16[128,1024]{1,0:T(8,128)(2,1)}, f32[256,128]{1,0:T(8,128)}, f32[3,128,256]{2,1,0:T(8,128)}, bf16[1024,128]{1,0:...) custom-call(bf16[3,1024,256]{2,1,0:T(8,128)(2,1)} %bitcast.34, ...), custom_call_target="tpu_custom_call" | custom-call | tf_op jit(solution)/shard_map/step/pallas_call | solution.py:998
  208.5 0.0 copy-done.2
  208.6 0.0 copy-done.3
  208.6 0.0 copy-done.4
  208.6 0.0 copy-start.5
  208.6 0.0 copy-start.6
  208.6 0.0 copy-start.7
  208.6 0.0 copy-start.12
  208.6 0.0 copy-start.13
  208.6 2.7 %fusion.11 = (bf16[1024,128]{1,0:T(8,128)(2,1)}, f32[1024,128]{1,0:T(8,128)}, f32[1024,128]{1,0:T(8,128)}, f32[1024,128]{1,0:T(8,128)}, f32[1024,128]{1,0:T(8,128)}) fusion(f32[1024,128]{1,0:T(8,128)S(1)} %copy-done.2, f32[1024,128]{1,0:T(8,128)S(1)} %copy-done.3, f32[1024,128]{1,0:T(8,128)S(1)} %copy-done.4, bf16[1024,128]{1,0:T(8,128)(2,1)} %get-tuple-element.46, ...), kind=kLoop, calls=%fused_computation.32 | loop fusion | flops 2490368 | bytes 4456448 | tf_op jit(solution)/shard_map/convert_element_type | solution.py:1059
  211.3 0.0 copy-done.5
  211.3 0.0 copy-done.6
  211.3 0.0 copy-done.7
  211.3 0.0 copy-done.12
  211.3 0.0 copy-done.13
  211.3 0.0 copy-start.15
  211.3 0.0 copy-start.16
  211.4 0.0 copy-start.17
  211.4 0.0 copy-start.18
  211.4 0.0 copy-start.19
  211.4 0.0 copy-start.8
  211.4 0.0 copy-start.9
  211.4 0.0 copy-start.10
  211.4 0.0 copy-start.11
  211.4 0.0 copy-start.14
  211.4 1.6 fusion.13
  213.0 0.0 copy-done.15
  213.0 0.0 copy-done.16
  213.0 0.0 copy-done.17
  213.0 0.0 copy-done.18
  213.0 0.0 copy-done.19
  213.0 0.0 copy-start.20
  213.1 0.0 copy-start.21
  213.1 0.8 fusion.15
  213.9 0.0 copy-done.8
  213.9 0.0 copy-done.9
  213.9 0.0 copy-done.10
  213.9 0.0 copy-done.11
  213.9 0.0 copy-done.14
  213.9 0.0 copy-start
  214.0 1.5 convert_bitcast_fusion
  215.5 1.3 multiply_subtract_fusion.3
  216.8 0.0 copy-done.1
  216.8 1.0 copy.50
  217.8 1.0 copy.51
  (4 shorter events, 0.0 us)
Async XLA Ops:
  0.7 207.9 %copy-start.2 = (f32[1024,128]{1,0:T(8,128)S(1)}, f32[1024,128]{1,0:T(8,128)}, u32[]{:S(2)}) copy-start(f32[1024,128]{1,0:T(8,128)} %param.39) | copy-start | bytes 1572868
  0.7 207.9 %copy-start.3 = (f32[1024,128]{1,0:T(8,128)S(1)}, f32[1024,128]{1,0:T(8,128)}, u32[]{:S(2)}) copy-start(f32[1024,128]{1,0:T(8,128)} %param.40) | copy-start | bytes 1572868
  0.7 207.9 %copy-start.4 = (f32[1024,128]{1,0:T(8,128)S(1)}, f32[1024,128]{1,0:T(8,128)}, u32[]{:S(2)}) copy-start(f32[1024,128]{1,0:T(8,128)} %param.41) | copy-start | bytes 1572868
  208.6 2.7 %copy-start.5 = (f32[128,1024]{1,0:T(8,128)S(1)}, f32[128,1024]{1,0:T(8,128)}, u32[]{:S(2)}) copy-start(f32[128,1024]{1,0:T(8,128)} %param.36) | copy-start | bytes 1572868
  208.6 2.7 %copy-start.6 = (f32[128,1024]{1,0:T(8,128)S(1)}, f32[128,1024]{1,0:T(8,128)}, u32[]{:S(2)}) copy-start(f32[128,1024]{1,0:T(8,128)} %param.37) | copy-start | bytes 1572868
  208.6 2.7 %copy-start.7 = (f32[128,1024]{1,0:T(8,128)S(1)}, f32[128,1024]{1,0:T(8,128)}, u32[]{:S(2)}) copy-start(f32[128,1024]{1,0:T(8,128)} %param.38) | copy-start | bytes 1572868
  208.6 2.7 %copy-start.12 = (bf16[128,1024]{1,0:T(8,128)(2,1)S(1)}, bf16[128,1024]{1,0:T(8,128)(2,1)}, u32[]{:S(2)}) copy-start(bf16[128,1024]{1,0:T(8,128)(2,1)} %get-tuple-element.43) | copy-start | bytes 786436
  208.6 2.7 %copy-start.13 = (bf16[128,1024]{1,0:T(8,128)(2,1)S(1)}, bf16[128,1024]{1,0:T(8,128)(2,1)}, u32[]{:S(2)}) copy-start(bf16[128,1024]{1,0:T(8,128)(2,1)} %get-tuple-element.44) | copy-start | bytes 786436
  211.3 1.7 copy-start.15
  211.3 1.7 copy-start.16
  211.4 1.7 copy-start.17
  211.4 1.7 copy-start.18
  211.4 1.7 copy-start.19
  211.4 2.5 %copy-start.8 = (f32[128,3,256]{2,0,1:T(8,128)S(1)}, f32[128,3,256]{2,0,1:T(8,128)}, u32[]{:S(2)}) copy-start(f32[128,3,256]{2,0,1:T(8,128)} %param.32) | copy-start | bytes 1179652
  211.4 2.5 %copy-start.9 = (f32[128,3,256]{2,0,1:T(8,128)S(1)}, f32[128,3,256]{2,0,1:T(8,128)}, u32[]{:S(2)}) copy-start(f32[128,3,256]{2,0,1:T(8,128)} %param.31) | copy-start | bytes 1179652
  211.4 2.5 %copy-start.10 = (f32[128,3,256]{2,0,1:T(8,128)S(1)}, f32[128,3,256]{2,0,1:T(8,128)}, u32[]{:S(2)}) copy-start(f32[128,3,256]{2,0,1:T(8,128)} %param.30) | copy-start | bytes 1179652
  211.4 2.5 %copy-start.11 = (f32[3,128,256]{2,1,0:T(8,128)S(1)}, f32[3,128,256]{2,1,0:T(8,128)}, u32[]{:S(2)}) copy-start(f32[3,128,256]{2,1,0:T(8,128)} %get-tuple-element.39) | copy-start | bytes 1179652
  211.4 2.5 %copy-start.14 = (bf16[3,128,256]{2,1,0:T(8,128)(2,1)S(1)}, bf16[3,128,256]{2,1,0:T(8,128)(2,1)}, u32[]{:S(2)}) copy-start(bf16[3,128,256]{2,1,0:T(8,128)(2,1)} %get-tuple-element.40) | copy-start | bytes 589828
  213.0 2.4 %copy-start.20 = (f32[4,128]{1,0:T(4,128)S(1)}, f32[4,128]{1,0:T(4,128)}, u32[]{:S(2)}) copy-start(f32[4,128]{1,0:T(4,128)} %param.42) | copy-start | bytes 6148
  213.1 2.4 %copy-start.21 = (f32[4,128]{1,0:T(4,128)S(1)}, f32[4,128]{1,0:T(4,128)}, u32[]{:S(2)}) copy-start(f32[4,128]{1,0:T(4,128)} %param.43) | copy-start | bytes 6148
  213.9 2.9 %copy-start.1 = (f32[256,1024]{1,0:T(8,128)S(1)}, f32[256,1024]{1,0:T(8,128)}, u32[]{:S(2)}) copy-start(f32[256,1024]{1,0:T(8,128)} %get-tuple-element.98) | copy-start | bytes 3145732
  213.9 3.8 %copy-start = (f32[256,1024]{1,0:T(8,128)S(1)}, f32[256,1024]{1,0:T(8,128)}, u32[]{:S(2)}) copy-start(f32[256,1024]{1,0:T(8,128)} %get-tuple-element.99) | copy-start | bytes 3145732

commit v4 on v3

--- a/solution.py
+++ b/solution.py
@@ -269,29 +269,57 @@
 ROWS = LAT
 HALVES = (0, 1)
 SHARDS = ((3, D, 256), (256, D), (D, D), (D, D))
-GATHER_ORDER = (1, 0, 2, 3)
-SHORT = (3,)
-CHUNKS = [(w, k) for w in GATHER_ORDER for k in range(3)]
-SLOTS = 3
-LOADS = [(0, None), (0, 0), (0, 1), (0, 2)]
-LOADS += [(2, None), (2, 0), (2, 1), (2, 2)]
-LOADS += [(3, None), (3, 0), (3, 1), (3, 2)]
-LOADS += [(2, 2), (2, 1), (2, 0), (2, None)]
-LOADS += [(0, 2), (0, 1), (0, 0), (0, None)]
+SHORT = ()
+CHUNKS = [(w, k) for w in (0, 1) for k in range(3)] + [(2, 0), (3, 0)]
+SLOTS = 4
+LOADS = (
+    (0, None), (0, 0), (0, 1), (0, 2), (2, None), (2, 0), (3, None), (3, 0), (0, 2), (0, 1), (0, 0), (0, None),
+)
 
 WIDTHS = (D, D, 256, 3 * 256)
 BLOCK = D // OWNERS
 HALF = BLOCK // 2
 RING = 2
 OWN = PLANES - 1
-UNITS = [(w, i) for w in (0, 1, 3, 2) for i in range(PLANES)]
-EARLY_Z = (0, 1)
+UNITS = (
+    (0, 0), (0, 3), (1, 0), (1, 3), (3, 0), (3, 1), (3, 2), (3, 3), (2, 0), (2, 1), (2, 2), (2, 3),
+)
 TURNED_AT = (0, 1, 1, 0)
-LAG_ONE, LAG_TWO, LAG_Z, TAIL = 2, 4, 6, 7
-OWN_AT = {0: 13, 1: 17}
-FINISH_AT = {0: 15, 1: 20, 3: 19, 2: 22}
-JOIN_FROM = 13
-
+(
+    SEND_OWN, TAKE, CORNER, CROSS, WHOLE, LOAD, READY, ENTER, PROJECT, BRANCH, SEND_COTANGENT, CAME, WIDEN,
+    NARROW_BACK, WIDEN_BACK, NARROW, LATENTS, RESIDUAL, ATTEND, INWARD, TURN, PRODUCE, JOIN, ONE, TWO, ALONG,
+    FINISH, INPUTS, NORM, NORMS_OUT, POINTS,
+) = range(31)
+SCHEDULE = (
+    (SEND_OWN, 1), (SEND_OWN, 0), (TAKE, 1, 0, 0), (CORNER, 1, 0, 0), (TAKE, 0, 0, 0), (TAKE, 1, 0, 1),
+    (TAKE, 0, 1, 0), (TAKE, 0, 0, 1), (TAKE, 0, 1, 1), (CORNER, 1, 0, 1), (CROSS, 1, 0, 0), (TAKE, 1, 1, 1),
+    (CORNER, 0, 0, 1), (TAKE, 1, 1, 0), (TAKE, 1, 2, 1), (TAKE, 1, 2, 0), (LOAD, 0), (CORNER, 0, 1, 0),
+    (TAKE, 0, 2, 0), (TAKE, 0, 2, 1), (SEND_OWN, 2), (CORNER, 0, 1, 1), (SEND_OWN, 3), (ENTER,), (CORNER, 0, 0, 0),
+    (SEND_COTANGENT,), (CORNER, 0, 2, 1), (CORNER, 1, 2, 1), (PROJECT, 0), (CORNER, 1, 2, 0), (CROSS, 0, 1, 1),
+    (CROSS, 0, 1, 0), (CROSS, 0, 0, 0), (CORNER, 0, 2, 0), (CROSS, 0, 0, 1), (CORNER, 1, 1, 1), (LOAD, 4),
+    (CROSS, 1, 0, 1), (WHOLE, 0, 0), (LOAD, 1), (CROSS, 0, 2, 1), (CORNER, 1, 1, 0), (TAKE, 2, 0, 0), (WHOLE, 0, 1),
+    (LOAD, 2), (TAKE, 2, 0, 1), (PROJECT, 1), (CROSS, 0, 2, 0), (CROSS, 1, 2, 1), (TAKE, 3, 0, 0), (CROSS, 1, 2, 0),
+    (CROSS, 1, 1, 0), (WHOLE, 0, 2), (LOAD, 3), (PROJECT, 2), (WHOLE, 1, 2), (READY, 4), (CROSS, 1, 1, 1),
+    (TAKE, 3, 0, 1), (CORNER, 2, 0, 1), (WHOLE, 1, 1), (WHOLE, 1, 0), (CORNER, 2, 0, 0), (PROJECT, 3), (BRANCH,),
+    (CAME, 0), (LOAD, 6), (TURN, 0), (CORNER, 3, 0, 0), (READY, 6), (CROSS, 2, 0, 1), (CORNER, 3, 0, 1),
+    (WIDEN, 0, 0), (CROSS, 2, 0, 0), (WHOLE, 2, 0), (NARROW_BACK, 0, 0), (LOAD, 5), (READY, 5), (CROSS, 3, 0, 1),
+    (CROSS, 3, 0, 0), (WIDEN, 1, 0), (WHOLE, 3, 0), (LOAD, 7), (CAME, 1), (WIDEN, 1, 1), (PRODUCE, 0), (WIDEN, 0, 1),
+    (PRODUCE, 1), (JOIN, 0), (READY, 7), (NARROW_BACK, 0, 1), (NARROW_BACK, 1, 1), (JOIN, 1), (NARROW_BACK, 1, 0),
+    (WIDEN_BACK, 1), (TURN, 1), (ONE, 0, 1), (PRODUCE, 2), (ONE, 0, 0), (PRODUCE, 3), (JOIN, 2), (TURN, 3),
+    (WIDEN_BACK, 0), (JOIN, 3), (NARROW, 1), (RESIDUAL,), (ATTEND, 4), (PRODUCE, 4), (ONE, 2, 1), (ONE, 2, 0),
+    (ATTEND, 5), (JOIN, 4), (LOAD, 8), (PRODUCE, 5), (ATTEND, 6), (TWO, 2, 1), (JOIN, 5), (ONE, 1, 1), (ONE, 4, 0),
+    (LOAD, 9), (ONE, 4, 1), (PRODUCE, 6), (TURN, 2), (ATTEND, 7), (JOIN, 6), (TWO, 2, 0), (PRODUCE, 7), (TWO, 4, 0),
+    (TWO, 0, 0), (PRODUCE, 8), (PRODUCE, 9), (ONE, 3, 0), (JOIN, 9), (ONE, 5, 1), (JOIN, 8), (ONE, 5, 0), (NARROW, 0),
+    (TWO, 4, 1), (ONE, 9, 1), (ONE, 9, 0), (PRODUCE, 10), (TWO, 0, 1), (ALONG, 4, 0), (ONE, 3, 1), (LOAD, 10),
+    (ONE, 6, 0), (PRODUCE, 11), (ALONG, 4, 1), (INWARD, 8), (TWO, 5, 1), (JOIN, 7), (LOAD, 11), (TWO, 1, 1),
+    (JOIN, 10), (TWO, 9, 1), (TWO, 5, 0), (ONE, 8, 1), (TWO, 9, 0), (ONE, 6, 1), (INWARD, 9), (INWARD, 10),
+    (INWARD, 11), (JOIN, 11), (INPUTS,), (TWO, 6, 0), (ALONG, 5, 1), (ALONG, 9, 1), (ONE, 8, 0), (NORM, 0),
+    (ALONG, 6, 0), (ONE, 10, 0), (ONE, 1, 0), (ONE, 10, 1), (TWO, 8, 1), (TWO, 8, 0), (NORM, 1), (ONE, 7, 0),
+    (ONE, 11, 1), (ALONG, 8, 1), (TWO, 10, 0), (LATENTS,), (TWO, 6, 1), (ALONG, 6, 1), (ALONG, 8, 0), (ONE, 7, 1),
+    (TWO, 10, 1), (ALONG, 5, 0), (ALONG, 10, 1), (TWO, 1, 0), (NORM, 2), (ONE, 11, 0), (TWO, 11, 1), (TWO, 3, 1),
+    (TWO, 3, 0), (FINISH, 1), (ALONG, 9, 0), (ALONG, 10, 0), (FINISH, 0), (POINTS,), (TWO, 7, 1), (TWO, 7, 0),
+    (TWO, 11, 0), (FINISH, 3), (NORMS_OUT,), (FINISH, 2),
+)
 NN = ((1,), (0,))
 NT = ((1,), (1,))
 TN = ((0,), (0,))
@@ -342,17 +370,18 @@
 
 def step_kernel(*refs):
     f32, bf16 = jnp.float32, jnp.bfloat16
-    shards, (points, cotangent, members, norms) = refs[0:4], refs[4:8]
+    shards, cotangent_in, (points, members, norms) = refs[0:4], refs[4], refs[5:8]
     outs, norm_out, latents_out, points_out, fulls = refs[8:16], refs[16], refs[17], refs[18], refs[19:23]
-    inputs, entering_one, projected, attended, residual, entering_two, activated, slope, latents = refs[23:32]
-    turned, upward_grad, branch_grad, projected_grad, normed_grad = refs[32:37]
-    slots, output_full, ring = refs[37:40]
-    acc, one_in, two_in, z_in = refs[40:44], refs[44:48], refs[48:52], refs[52:56]
-    norm_own, norm_in, norm_planes = refs[56:59]
-    load_sem, output_sem, out_sem = refs[59:62]
-    gz_send, gz_recv, ga_send, ga_recv, gb_send, gb_recv, gc_send, gc_recv = refs[62:70]
-    c_send, c_recv, one_send, one_recv, two_send, two_recv, z_send, z_recv = refs[70:78]
-    norm_send, norm_recv = refs[78:80]
+    inputs, entering_one, projected, attended, residual, latents = refs[23:29]
+    entering_two, cotangent, activated, slope, upward_grad = refs[29:34]
+    turned, branch_grad, projected_grad, normed_grad, sent, came = refs[34:40]
+    slots, output_full, ring = refs[40:43]
+    acc, one_in, two_in, z_in = refs[43:47], refs[47:51], refs[51:55], refs[55:59]
+    norm_own, norm_in, norm_planes = refs[59:62]
+    load_sem, output_sem, out_sem, swap_send, swap_recv = refs[62:67]
+    gz_send, gz_recv, ga_send, ga_recv, gb_send, gb_recv, gc_send, gc_recv = refs[67:75]
+    c_send, c_recv, one_send, one_recv, two_send, two_recv, z_send, z_recv = refs[75:83]
+    norm_send, norm_recv = refs[83:85]
     residual_grad = residual
     y, x, c, z = place()
     is_mid = jnp.logical_or(z == 1, z == 2)
@@ -360,6 +389,7 @@
     sibling = device(y, x, 1 - c, z)
     over_x, over_y = device(y, 1 - x, c, z), device(1 - y, x, c, z)
     beside, across = device(y, x, c, arrival(z, 0)), device(y, x, c, 3 - z)
+    opposite = device(y, x, c, (z + 2) % PLANES)
 
     def plane_at(k):
         return z if k is None else arrival(z, k)
@@ -376,7 +406,7 @@
         return ref.at[:, rows, :] if w == 0 else ref.at[rows, :]
 
     def view(w, plane, rows):
-        return rows_of(fulls[w].at[plane], w, rows)
+        return fulls[w].at[rows, :] if w >= 2 else rows_of(fulls[w].at[plane], w, rows)
 
     def block(w, half, first, count):
         height = SHARDS[w][-2]
@@ -394,8 +424,8 @@
         send, recv = gz_send.at[w, lane, half], gz_recv.at[w, slot, half]
         return remote(rows_of(shards[w], w, rows), view(w, z, rows), send, recv, target)
 
-    def gz_beside(w, half):
-        return gz_own(w, half, 0, 0, beside)
+    def gz_first(w, half):
+        return gz_own(w, half, 0, 0, opposite if w >= 2 else beside)
 
     def gz_across(w, half):
         return gz_own(w, half, 1, 1, across)
@@ -425,28 +455,43 @@
 
     def send_own(w):
         for half in HALVES:
-            gz_beside(w, half).start()
-
-        @pl.when(is_mid)
-        def _():
-            for half in HALVES:
-                gz_across(w, half).start()
-
-    def take(w, k):
+            gz_first(w, half).start()
+        if w < 2:
+
+            @pl.when(is_mid)
+            def _():
+                for half in HALVES:
+                    gz_across(w, half).start()
+
+    def take(w, k, half):
+        gz_arrived(w, k, half).wait_recv()
+        (gb_copy if w in SHORT else ga_copy)(w, k, half).start()
+        if w < 2:
+
+            @pl.when(is_mid)
+            def _():
+                gz_pass(w, k, half).start()
+
+    def corner(w, k, half):
+        ga_copy(w, k, half).wait_recv()
+        gb_copy(w, k, half).start()
+
+    def cross(w, k, half):
+        gb_copy(w, k, half).wait_recv()
+        gc_copy(w, k, half).start()
+
+    def whole(w, k):
         for half in HALVES:
-            gz_arrived(w, k, half).wait_recv()
-            (gb_copy if w in SHORT else ga_copy)(w, k, half).start()
-
-        @pl.when(is_mid)
-        def _():
-            for half in HALVES:
-                gz_pass(w, k, half).start()
+            gc_copy(w, k, half).wait_recv()
+        if w == 1:
+            output_load(k).start()
 
     def loads(n):
         w, k = LOADS[n]
+        if w >= 2:
+            source = shards[w] if k is None else fulls[w]
+            return [pltpu.make_async_copy(source, slots.at[n % SLOTS], load_sem.at[n, 0])]
         source = shards[w] if k is None else fulls[w].at[arrival(z, k)]
-        if w != 0:
-            return [pltpu.make_async_copy(source, slots.at[n % SLOTS], load_sem.at[n, 0])]
         return [
             pltpu.make_async_copy(
                 source.at[part], slots.at[n % SLOTS, :, part * 256 : (part + 1) * 256], load_sem.at[n, part]
@@ -465,6 +510,26 @@
     def output_load(k):
         source = shards[1] if k is None else fulls[1].at[arrival(z, k)]
         return pltpu.make_async_copy(source, output_full.at[plane_at(k)], output_sem.at[3 if k is None else k])
+
+    mine, theirs = pl.ds(0, ROWS), pl.ds(ROWS, ROWS)
+
+    def swap(n):
+        src, dst = (
+            (cotangent.at[mine], cotangent.at[theirs]),
+            (entering_two.at[mine], entering_two.at[theirs]),
+            (sent.at[0], came.at[0]),
+            (sent.at[1], came.at[1]),
+        )[n]
+        return remote(src, dst, swap_send.at[n], swap_recv.at[n], beside)
+
+    cotangent_load = pltpu.make_async_copy(cotangent_in, cotangent.at[mine], out_sem.at[2])
+
+    def send_cotangent():
+        cotangent_load.wait()
+        swap(0).start()
+
+    def swap_came(n):
+        swap(n).wait_recv()
 
     def enter():
         slot_of = lax.broadcasted_iota(jnp.int32, (ROWS, ROWS), 0) == members[...]
@@ -494,110 +559,146 @@
             probs = softmax_parts(plane, span)[2]
             attended[plane, :, span] = dot(probs.astype(bf16), projected[plane, 2, :, span], NN).astype(bf16)
 
-    def branch(k):
-        plane = plane_at(k)
-        output_load(k).wait()
+    def branches():
+        for k in (None, 0, 1, 2):
+            plane = plane_at(k)
+            output_load(k).wait()
+
+            def body(columns):
+                residual[:, columns] += dot(attended[plane], output_full[plane, :, columns], NN)
+
+            tiles(4, 256, body)
+        norm_rows(residual, entering_two, norms[2:3, :], norms[3:4, :])
+        swap(1).start()
+        latents[...] = residual[...]
+
+    def rows_at(b):
+        return theirs if b else mine
+
+    def widen(j, b):
+        rows = rows_at(b)
 
         def body(columns):
-            residual[:, columns] += dot(attended[plane], output_full[plane, :, columns], NN)
-
-        tiles(4, 256, body)
-
-    def enter_two():
-        norm_rows(residual, entering_two, norms[2:3, :], norms[3:4, :])
-        latents[...] = residual[...]
-
-    def widen(n):
-        wait_load(n)
-        plane, slot = plane_at(LOADS[n][1]), n % SLOTS
-
-        def body(columns):
-            u = dot(entering_two[...], slots[slot, :, columns], NN)
+            u = dot(entering_two[rows, :], slots[j, :, columns], NN)
             square = u * u
             bend = jnp.tanh(0.7978845608028654 * u * (1.0 + 0.044715 * square))
-            activated[plane, :, columns] = (0.5 * u * (1.0 + bend)).astype(bf16)
-            slope[plane, :, columns] = 0.5 * (1.0 + bend) + 0.5 * u * (1.0 - bend * bend) * (
+            activated[j, rows, columns] = (0.5 * u * (1.0 + bend)).astype(bf16)
+            slope[j, rows, columns] = 0.5 * (1.0 + bend) + 0.5 * u * (1.0 - bend * bend) * (
                 0.7978845608028654 * (1.0 + 3.0 * 0.044715 * square)
             )
 
         tiles(4, 256, body)
 
-    def narrow(n):
-        wait_load(n)
-        plane, slot = plane_at(LOADS[n][1]), n % SLOTS
+    def narrow_back(j, b):
+        rows = rows_at(b)
 
         def body(columns):
-            latents[:, columns] += dot(activated[plane], slots[slot, :, columns], NN)
-            product = dot(cotangent[...], slots[slot, columns, :], NT)
-            upward_grad[plane, :, columns] = (product * slope[plane, :, columns]).astype(bf16)
+            product = dot(cotangent[rows, :], slots[2 + j, columns, :], NT)
+            upward_grad[j, rows, columns] = (product * slope[j, rows, columns]).astype(bf16)
 
         tiles(4, 256, body)
 
+    def widen_back(b):
+        rows = rows_at(b)
+
+        def body(columns):
+            total = dot(upward_grad[0, rows, :], slots[0, columns, :], NT)
+            total += dot(upward_grad[1, rows, :], slots[1, columns, :], NT)
+            if b:
+                sent[1, :, columns] = total.astype(bf16)
+            else:
+                normed_grad[:, columns] = total
+
+        tiles(4, 256, body)
+        if b:
+            swap(3).start()
+
+    def narrow(b):
+        rows = rows_at(b)
+
+        def body(columns):
+            total = dot(activated[0, rows, :], slots[2, :, columns], NN)
+            total += dot(activated[1, rows, :], slots[3, :, columns], NN)
+            if b:
+                sent[0, :, columns] = total.astype(bf16)
+            else:
+                latents[:, columns] += total
+
+        tiles(4, 256, body)
+        if b:
+            swap(2).start()
+
+    latents_copy = pltpu.make_async_copy(latents, latents_out, out_sem.at[0])
+
+    def add_came(n, target):
+        swap_came(2 + n)
+
+        def strip(r, carry):
+            rows = pl.ds(pl.multiple_of(r * 32, 32), 32)
+            target[rows, :] += came[n, rows, :].astype(f32)
+            return carry
+
+        lax.fori_loop(0, ROWS // 32, strip, 0)
+
+    def latents_done():
+        add_came(0, latents)
+        latents_copy.start()
+
+    def here(t):
+        w, i = UNITS[t]
+        return acc[w].at[i if w >= 2 else i // OWN]
+
     def pair_copy(t):
-        w, i = UNITS[t]
-        return remote(
-            ring.at[t % RING, :, :, :, 0 : WIDTHS[w]], acc[w].at[i], c_send.at[t], c_recv.at[t], sibling
-        )
+        w = UNITS[t][0]
+        return remote(ring.at[t % RING, :, :, :, 0 : WIDTHS[w]], here(t), c_send.at[t], c_recv.at[t], sibling)
 
     def half_rows(half):
         return pl.ds(half * HALF, HALF)
 
+    def one_in_at(t, half):
+        w, i = UNITS[t]
+        return one_in[w].at[i if w >= 2 else i // OWN, half]
+
+    def two_in_at(t, half):
+        w, i = UNITS[t]
+        return two_in[w].at[i if w >= 2 else i // OWN, half]
+
     def one_copy(t, half):
-        w, i = UNITS[t]
         rows = half_rows(half)
-        src = acc[w].at[i, 1 - y, :, rows] if half == 0 else acc[w].at[i, :, 1 - x, rows]
-        return remote(
-            src, one_in[w].at[i, half], one_send.at[t, half], one_recv.at[t, half], (over_y, over_x)[half]
-        )
+        src = here(t).at[1 - y, :, rows] if half == 0 else here(t).at[:, 1 - x, rows]
+        send, recv = one_send.at[t, half], one_recv.at[t, half]
+        return remote(src, one_in_at(t, half), send, recv, (over_y, over_x)[half])
 
     def two_copy(t, half):
-        w, i = UNITS[t]
         rows = half_rows(half)
-        src = acc[w].at[i, y, 1 - x, rows] if half == 0 else acc[w].at[i, 1 - y, x, rows]
-        slot = 0 if w in EARLY_Z else i
-        return remote(
-            src, two_in[w].at[slot, half], two_send.at[t, half], two_recv.at[t, half], (over_x, over_y)[half]
-        )
-
-    def z_piece(t, half):
-        w, i = UNITS[t]
-        if w in EARLY_Z:
-            return acc[w].at[i, y, :, half_rows(half)] if half == 0 else acc[w].at[i, :, x, half_rows(half)]
-        return acc[w].at[i, y, x, half_rows(half)]
+        src = here(t).at[y, 1 - x, rows] if half == 0 else here(t).at[1 - y, x, rows]
+        send, recv = two_send.at[t, half], two_recv.at[t, half]
+        return remote(src, two_in_at(t, half), send, recv, (over_x, over_y)[half])
 
     def z_copy(t, half, slot, target):
         w = UNITS[t][0]
-        return remote(
-            z_piece(t, half), z_in[w].at[slot, half], z_send.at[t, half], z_recv.at[w, slot, half], target
-        )
-
-    def z_add(t, slot):
-        w = UNITS[t][0]
-        for half in HALVES:
-            z_copy(t, half, slot, beside).wait_recv()
-            piece = z_piece(t, half)
-            if w in EARLY_Z:
-                for k in (0, 1):
-                    add_rows(piece.at[k], z_in[w].at[slot, half, k])
-            else:
-                add_rows(piece, z_in[w].at[slot, half])
-
-    def z_send_end(t):
-        i = UNITS[t][1]
+        send, recv = z_send.at[t, half], z_recv.at[w, slot, half]
+        return remote(here(t).at[y, x, half_rows(half)], z_in[w].at[slot, half], send, recv, target)
+
+    def z_first(t, half):
+        w, i = UNITS[t]
+        if w < 2:
+            z_copy(t, half, 0, opposite).start()
+            return
 
         @pl.when(is_end)
         def _():
-            for half in HALVES:
-                z_copy(t, half, 2 - i, beside).start()
-
-    def z_send_mid(t):
-        i = UNITS[t][1]
+            z_copy(t, half, 2 - i, beside).start()
+
+    def z_pass(t, half):
+        w, i = UNITS[t]
 
         @pl.when(is_mid)
         def _():
-            z_add(t, (2, 1, 3)[i])
-            for half in HALVES:
-                z_copy(t, half, (3, 4, 0)[i], (across, across, beside)[i]).start()
+            slot = (2, 1, 3)[i]
+            z_copy(t, half, slot, beside).wait_recv()
+            add_rows(here(t).at[y, x, half_rows(half)], z_in[w].at[slot, half])
+            z_copy(t, half, (3, 4, 0)[i], (across, across, beside)[i]).start()
 
     def add_rows(target, source):
         def body(r, carry):
@@ -608,12 +709,12 @@
         lax.fori_loop(0, HALF // 16, body, 0)
 
     def partial(w, i, parity, columns, n):
+        if w < 2:
+            right = (activated, upward_grad)[w][1 - i // OWN, :, columns]
+            return dot(turned[w, parity], right, NN)
         plane = plane_of(i)
-        if w == 3:
-            right = projected_grad[plane, n]
-        else:
-            right = (activated, upward_grad, attended)[w][plane, :, columns]
-        return dot(turned[TURNED_AT[w], parity], right, NN)
+        right = projected_grad[plane, n] if w == 3 else attended[plane, :, columns]
+        return dot(turned[TURNED_AT[w], parity, :, 0:ROWS], right, NN)
 
     def over_tiles(w, body):
         if w == 2:
@@ -641,61 +742,38 @@
 
     def join(t):
         w, i = UNITS[t]
+        at = i if w >= 2 else i // OWN
         pair_copy(t).wait_recv()
 
         def body(columns, n):
             product = partial(w, i, c, columns, n)
             for k in range(4):
-                came = acc[w][i, k // 2, k % 2, :, columns].astype(f32)
-                acc[w][i, k // 2, k % 2, :, columns] = (product[k * BLOCK : (k + 1) * BLOCK] + came).astype(bf16)
+                other = acc[w][at, k // 2, k % 2, :, columns].astype(f32)
+                acc[w][at, k // 2, k % 2, :, columns] = (product[k * BLOCK : (k + 1) * BLOCK] + other).astype(bf16)
 
         over_tiles(w, body)
         for half in HALVES:
             one_copy(t, half).start()
 
-    def after_one(t):
-        w, i = UNITS[t]
-        for half in HALVES:
-            one_copy(t, half).wait()
-            rows = half_rows(half)
-            for k in (0, 1):
-                target = acc[w].at[i, y, k, rows] if half == 0 else acc[w].at[i, k, x, rows]
-                add_rows(target, one_in[w].at[i, half, k])
-            if w not in EARLY_Z:
-                two_copy(t, half).start()
-        if w in EARLY_Z and i < OWN:
-            z_send_end(t)
-
-    def after_two(t):
-        w, i = UNITS[t]
-        if w in EARLY_Z:
-            return
-        for half in HALVES:
-            two_copy(t, half).wait()
-            add_rows(acc[w].at[i, y, x, half_rows(half)], two_in[w].at[i, half])
-        if i < OWN:
-            z_send_end(t)
-
-    def own_hop(w):
-        t = UNITS.index((w, OWN))
-        z_add(t, 0)
-
-        @pl.when(is_mid)
-        def _():
-            z_add(t, 4)
-
-        for half in HALVES:
-            two_copy(t, half).start()
+    def after_one(t, half):
+        one_copy(t, half).wait()
+        rows = half_rows(half)
+        for k in (0, 1):
+            target = here(t).at[y, k, rows] if half == 0 else here(t).at[k, x, rows]
+            add_rows(target, one_in_at(t, half).at[k])
+        two_copy(t, half).start()
+
+    def after_two(t, half):
+        two_copy(t, half).wait()
+        add_rows(here(t).at[y, x, half_rows(half)], two_in_at(t, half))
+        if UNITS[t][1] < OWN:
+            z_first(t, half)
 
     def finish(w):
         t = UNITS.index((w, OWN))
-        mine = acc[w].at[OWN, y, x]
-        if w in EARLY_Z:
-            for half in HALVES:
-                two_copy(t, half).wait()
-        else:
-            for half in HALVES:
-                z_copy(t, half, 0, beside).wait_recv()
+        for half in HALVES:
+            z_copy(t, half, 0, beside).wait_recv()
+        if w >= 2:
 
             @pl.when(is_mid)
             def _():
@@ -704,11 +782,9 @@
 
         def body(n, carry):
             columns = pl.ds(pl.multiple_of(n * 128, 128), 128)
-            first = mine[:, columns].astype(f32)
-            if w in EARLY_Z:
-                second = [two_in[w][0, half, :, columns] for half in HALVES]
-            else:
-                second = [z_in[w][0, half, :, columns] for half in HALVES]
+            first = here(t).at[y, x][:, columns].astype(f32)
+            second = [z_in[w][0, half, :, columns] for half in HALVES]
+            if w >= 2:
                 third = [z_in[w][4, half, :, columns] for half in HALVES]
                 first += jnp.where(is_mid, jnp.concatenate(third, axis=0).astype(f32), 0.0)
             second = jnp.concatenate(second, axis=0).astype(f32)
@@ -724,26 +800,16 @@
 
         lax.fori_loop(0, WIDTHS[w] // 128, body, 0)
 
-    def turn(source, w):
+    def turn(w):
+        source = (cotangent, entering_two, branch_grad, entering_one)[w]
         for owner in range(OWNERS):
             columns = slice(owner * BLOCK, (owner + 1) * BLOCK)
             place_at = slice((owner // 2) * BLOCK, (owner // 2 + 1) * BLOCK)
-            turned[TURNED_AT[w], owner % 2, place_at, :] = source[:, columns].T
-
-    def hidden_back(i):
-        n = 12 + i
-        wait_load(n)
-        plane, slot = plane_of(i), n % SLOTS
-
-        def normed(columns):
-            product = dot(upward_grad[plane], slots[slot, columns, :], NT)
-            if i == 0:
-                normed_grad[:, columns] = product
+            flat = source[:, columns].T
+            if w < 2:
+                turned[w, owner % 2, place_at, :] = flat
             else:
-                normed_grad[:, columns] += product
-
-        tiles(4, 256, normed)
-        start_load(n + SLOTS)
+                turned[TURNED_AT[w], owner % 2, place_at, 0:ROWS] = flat
 
     def norm_back(source, gain, row, store):
         norm_own[0, row : row + 2, :] = jnp.zeros((2, D), f32)
@@ -765,6 +831,8 @@
         lax.fori_loop(0, ROWS // 32, strip, 0)
 
     def residual_back():
+        add_came(1, normed_grad)
+
         def store(rows, part):
             total = part + cotangent[rows, :].astype(f32)
             residual_grad[rows, :] = total
@@ -772,8 +840,8 @@
 
         norm_back(residual, norms[2:3, :], 2, store)
 
-    def attend_back(i):
-        plane = plane_of(i)
+    def attend_back(t):
+        plane = plane_of(UNITS[t][1])
         attended_grad = dot(branch_grad[...], output_full[plane], NT).astype(bf16)
         scale = HEAD_DIM ** (-0.5)
         for head in range(2):
@@ -787,29 +855,50 @@
             projected_grad[plane, 0, :, span] = (dot(score_grad, keys_all, NN) * scale).astype(bf16)
             projected_grad[plane, 1, :, span] = (dot(score_grad, queries, TN) * scale).astype(bf16)
 
-    def project_back(i):
-        n = 16 + i
+    def project_back(n):
         wait_load(n)
-        plane, slot = plane_of(i), n % SLOTS
+        plane, slot = plane_at(LOADS[n][1]), n % SLOTS
+        first = n == 8
 
         def normed(columns):
             total = dot(projected_grad[plane, 0], slots[slot, columns, 0:256], NT)
             for part in (1, 2):
                 total += dot(projected_grad[plane, part], slots[slot, columns, part * 256 : (part + 1) * 256], NT)
-            if i == 0:
+            if first:
                 normed_grad[:, columns] = total
             else:
                 normed_grad[:, columns] += total
 
         tiles(4, 256, normed)
-        if n + SLOTS < len(LOADS):
-            start_load(n + SLOTS)
-
-    def input_back():
+
+    def norm_step(k):
+        return remote(norm_own.at[k], norm_in.at[k], norm_send.at[k], norm_recv.at[k], (sibling, over_x, over_y)[k])
+
+    def norm_plane(d):
+        target = device(y, x, c, (z + d) % PLANES)
+        return remote(norm_own.at[3], norm_planes.at[z], norm_send.at[2 + d], norm_recv.at[2 + d], target)
+
+    def inputs_back():
         def store(rows, part):
             residual_grad[rows, :] += part
 
         norm_back(inputs, norms[0:1, :], 0, store)
+        norm_step(0).start()
+
+    def norm_hop(k):
+        norm_step(k).wait()
+        norm_own[k + 1] = norm_own[k] + norm_in[k]
+        if k < 2:
+            norm_step(k + 1).start()
+        else:
+            norm_planes[z] = norm_own[3]
+            for d in (1, 2, 3):
+                norm_plane(d).start()
+
+    def norms_out():
+        for d in (1, 2, 3):
+            norm_plane(d).wait()
+        norm_out[...] = (norm_planes[0] + norm_planes[1]) + (norm_planes[2] + norm_planes[3])
 
     points_copy = pltpu.make_async_copy(inputs, points_out, out_sem.at[1])
 
@@ -829,119 +918,16 @@
         tiles(4, 256, pick)
         points_copy.start()
 
-    def norm_step(k):
-        return remote(norm_own.at[k], norm_in.at[k], norm_send.at[k], norm_recv.at[k], (sibling, over_x, over_y)[k])
-
-    def norm_plane(d):
-        target = device(y, x, c, (z + d) % PLANES)
-        return remote(norm_own.at[3], norm_planes.at[z], norm_send.at[2 + d], norm_recv.at[2 + d], target)
-
-    def before(t):
-        w, i = UNITS[t]
-        if w == 0 and i == 0:
-            turn(cotangent, 0)
-        elif w == 1:
-            if i == 0:
-                turn(entering_two, 1)
-            hidden_back(i)
-        elif w == 3:
-            if i == 0:
-                residual_back()
-                turn(entering_one, 3)
-            attend_back(i)
-            project_back(i)
-        elif w == 2 and i == 0:
-            turn(branch_grad, 2)
-
-    count = len(UNITS)
-    input_at = 1 + UNITS.index((3, OWN))
-
-    def reduce_step(step):
-        if 0 <= step + 1 < count:
-            before(step + 1)
-            produce(step + 1)
-        if 0 <= step < count:
-            join(step)
-        if 0 <= step - LAG_ONE < count:
-            after_one(step - LAG_ONE)
-        if 0 <= step - LAG_TWO < count:
-            after_two(step - LAG_TWO)
-        if 0 <= step - LAG_Z < count and UNITS[step - LAG_Z][1] < OWN:
-            z_send_mid(step - LAG_Z)
-        if step == input_at:
-            input_back()
-            norm_step(0).start()
-        if step == count:
-            points_back()
-        at = step - input_at - 1
-        if 0 <= at < 3:
-            norm_step(at).wait()
-            norm_own[at + 1] = norm_own[at] + norm_in[at]
-            if at < 2:
-                norm_step(at + 1).start()
-            else:
-                norm_planes[z] = norm_own[3]
-                for d in (1, 2, 3):
-                    norm_plane(d).start()
-        for w in range(4):
-            if w in EARLY_Z and step == OWN_AT[w]:
-                own_hop(w)
-            if step == FINISH_AT[w]:
-                finish(w)
-
-    latents_copy = pltpu.make_async_copy(latents, latents_out, out_sem.at[0])
-    start_load(0)
+    steps = (
+        send_own, take, corner, cross, whole, start_load, wait_load, enter, project_attend, branches, send_cotangent,
+        swap_came, widen, narrow_back, widen_back, narrow, latents_done, residual_back, attend_back, project_back,
+        turn, produce, join, after_one, after_two, z_pass, finish, inputs_back, norm_hop, norms_out, points_back,
+    )
+    cotangent_load.start()
     output_load(None).start()
     greet(y, x, c, z)
-    send_own(GATHER_ORDER[0])
-    starts = {6: (1,), 7: (2,), 8: (3, 4), 9: (5,), 10: (6,), 11: (7, 8), 12: (9,), 13: (10,), 14: (11, 12), 15: (13,)}
-    uses = {7: (1,), 8: (2,), 9: (3, 4), 10: (5,), 11: (6,), 12: (7, 8), 13: (9,), 14: (10,), 15: (11,)}
-    for step in range(JOIN_FROM + count + TAIL):
-        if step < len(CHUNKS):
-            if step % 3 == 0 and step // 3 + 1 < 4:
-                send_own(GATHER_ORDER[step // 3 + 1])
-            take(*CHUNKS[step])
-        if 0 <= step - 1 < len(CHUNKS):
-            w, k = CHUNKS[step - 1]
-            if w not in SHORT:
-                for half in HALVES:
-                    ga_copy(w, k, half).wait_recv()
-                    gb_copy(w, k, half).start()
-        if 0 <= step - 2 < len(CHUNKS):
-            w, k = CHUNKS[step - 2]
-            for half in HALVES:
-                gb_copy(w, k, half).wait_recv()
-                gc_copy(w, k, half).start()
-        if 0 <= step - 3 < len(CHUNKS):
-            w, k = CHUNKS[step - 3]
-            for half in HALVES:
-                gc_copy(w, k, half).wait_recv()
-            if w == 1:
-                output_load(k).start()
-        for n in starts.get(step, ()):
-            start_load(n)
-        if step == 1:
-            enter()
-            project_attend(0)
-        for n in uses.get(step, ()):
-            w, k = LOADS[n]
-            if w == 0:
-                project_attend(n)
-                if k == 2:
-                    for at in (None, 0, 1, 2):
-                        branch(at)
-                    enter_two()
-            elif w == 2:
-                widen(n)
-            else:
-                narrow(n)
-        if step == 15:
-            latents_copy.start()
-            start_load(14)
-        reduce_step(step - JOIN_FROM)
-    for d in (1, 2, 3):
-        norm_plane(d).wait()
-    norm_out[...] = (norm_planes[0] + norm_planes[1]) + (norm_planes[2] + norm_planes[3])
+    for step, *at in SCHEDULE:
+        steps[step](*at)
     for w, k in CHUNKS:
         for half in HALVES:
             if w not in SHORT:
@@ -950,20 +936,22 @@
             gc_copy(w, k, half).wait_send()
     for w in range(4):
         for half in HALVES:
-            gz_beside(w, half).wait_send()
+            gz_first(w, half).wait_send()
 
     @pl.when(is_mid)
     def _():
-        for w in range(4):
+        for w in (0, 1):
             for half in HALVES:
                 gz_across(w, half).wait_send()
                 for k in range(3):
                     gz_pass(w, k, half).wait_send()
 
-    for t in range(count - RING, count):
+    for n in range(4):
+        swap(n).wait_send()
+    for t in range(len(UNITS) - RING, len(UNITS)):
         pair_copy(t).wait_send()
-    for t in range(count):
-        if UNITS[t][1] < OWN:
+    for t, unit in enumerate(UNITS):
+        if unit[1] < OWN:
             for half in HALVES:
                 z_copy(t, half, 0, beside).wait_send()
     points_copy.wait()
@@ -972,40 +960,43 @@
 
 def run_step(shards, points, cotangent, members, layer_norms):
     f32, bf16 = jnp.float32, jnp.bfloat16
+    vmem_of = pltpu.VMEM
     blocks = [(WIDTHS[0], BLOCK), (BLOCK, WIDTHS[1]), (WIDTHS[2], BLOCK), (3, BLOCK, 256)]
-    out_shape = [jax.ShapeDtypeStruct(blocks[w], bf16 if w in EARLY_Z else f32) for w in range(4)]
+    out_shape = [jax.ShapeDtypeStruct(blocks[w], bf16 if w < 2 else f32) for w in range(4)]
     out_shape += [jax.ShapeDtypeStruct(s, bf16) for s in blocks]
     out_shape += [jax.ShapeDtypeStruct(s, f32) for s in ((4, D), (ROWS, D), (ROWS, D))]
-    out_shape += [jax.ShapeDtypeStruct((PLANES,) + s, bf16) for s in SHARDS]
-    rows_f32, rows_bf16 = pltpu.VMEM((ROWS, D), f32), pltpu.VMEM((ROWS, D), bf16)
-    parts = pltpu.VMEM((PLANES, 3, ROWS, 256), bf16)
-    hidden = pltpu.VMEM((PLANES, ROWS, D), bf16)
-    scratch = [rows_f32, rows_bf16, parts, pltpu.VMEM((PLANES, ROWS, 256), bf16), rows_f32, rows_bf16, hidden]
-    scratch += [pltpu.VMEM((PLANES, ROWS, D), f32), rows_f32]
-    scratch += [pltpu.VMEM((2, 2, D // 2, ROWS), bf16), hidden, rows_bf16, parts, rows_f32]
-    scratch += [pltpu.VMEM((SLOTS, D, D), bf16), pltpu.VMEM((PLANES, 256, D), bf16)]
-    scratch += [pltpu.VMEM((RING, 2, 2, BLOCK, D), bf16)]
-    scratch += [pltpu.VMEM((4, 2, 2, BLOCK, n), bf16) for n in WIDTHS]
-    scratch += [pltpu.VMEM((4, 2, 2, HALF, n), bf16) for n in WIDTHS]
-    scratch += [pltpu.VMEM((1 if w in EARLY_Z else 4, 2, HALF, WIDTHS[w]), bf16) for w in range(4)]
-    scratch += [pltpu.VMEM((5, 2) + ((2,) if w in EARLY_Z else ()) + (HALF, WIDTHS[w]), bf16) for w in range(4)]
-    scratch += [pltpu.VMEM((n, 4, D), f32) for n in (4, 3, 4)]
+    out_shape += [jax.ShapeDtypeStruct(((PLANES,) if w < 2 else ()) + SHARDS[w], bf16) for w in range(4)]
+    rows_f32, rows_bf16 = vmem_of((ROWS, D), f32), vmem_of((ROWS, D), bf16)
+    both_bf16, hidden = vmem_of((2 * ROWS, D), bf16), vmem_of((2, 2 * ROWS, D), bf16)
+    parts = vmem_of((PLANES, 3, ROWS, 256), bf16)
+    scratch = [rows_f32, rows_bf16, parts, vmem_of((PLANES, ROWS, 256), bf16), rows_f32, rows_f32]
+    scratch += [both_bf16, both_bf16, hidden, vmem_of((2, 2 * ROWS, D), f32), hidden]
+    scratch += [vmem_of((2, 2, D // 2, 2 * ROWS), bf16), rows_bf16, parts, rows_f32]
+    scratch += [vmem_of((2, ROWS, D), bf16)] * 2
+    scratch += [vmem_of((SLOTS, D, D), bf16), vmem_of((PLANES, 256, D), bf16), vmem_of((RING, 2, 2, BLOCK, D), bf16)]
+    counts = (2, 2, 4, 4)
+    scratch += [vmem_of((counts[w], 2, 2, BLOCK, WIDTHS[w]), bf16) for w in range(4)]
+    scratch += [vmem_of((counts[w], 2, 2, HALF, WIDTHS[w]), bf16) for w in range(4)]
+    scratch += [vmem_of((counts[w], 2, HALF, WIDTHS[w]), bf16) for w in range(4)]
+    scratch += [vmem_of((1 if w < 2 else 5, 2, HALF, WIDTHS[w]), bf16) for w in range(4)]
+    scratch += [vmem_of((n, 4, D), f32) for n in (4, 3, 4)]
     dma = pltpu.SemaphoreType.DMA
-    scratch += [dma((len(LOADS), 3)), dma((4,)), dma((2,)), dma((4, 5, 2))]
+    units = len(UNITS)
+    scratch += [dma((len(LOADS), 3)), dma((4,)), dma((3,)), dma((4,)), dma((4,)), dma((4, 5, 2))]
     scratch += [dma((4, 3, 2))] * 7
-    scratch += [dma((16,))] * 2 + [dma((16, 2))] * 5 + [dma((4, 5, 2))] + [dma((6,))] * 2
+    scratch += [dma((units,))] * 2 + [dma((units, 2))] * 5 + [dma((4, 5, 2))] + [dma((6,))] * 2
     anywhere, vmem = pl.BlockSpec(memory_space=pl.ANY), pl.BlockSpec(memory_space=pltpu.VMEM)
     result = pl.pallas_call(
         step_kernel,
         out_shape=out_shape,
-        in_specs=[anywhere] * 4 + [vmem] * 4,
+        in_specs=[anywhere] * 5 + [vmem] * 3,
         out_specs=[vmem] * 9 + [anywhere] * 6,
         scratch_shapes=scratch,
         name="step",
         compiler_params=pltpu.CompilerParams(
             collective_id=0, has_side_effects=True, vmem_limit_bytes=60 << 20
         ),
-    )(*shards, points, cotangent, members, layer_norms)
+    )(*shards, cotangent, points, members, layer_norms)
     return result[:4], result[4:8], result[8], result[9], result[10]
 
 

time: 219 us -> 172 us (0.79)
  Pallas kernels: 208 us -> 161 us
    pallas_call x1, Pallas kernels: 208 us -> 161 us  [run_step(): pl.pallas_call(step_kernel, out_shape=out_shape, in_specs=[anywhere] * 5...]
where the time goes in v4:
time: 172 us
  Pallas kernels  161 us (94%)
  other arithmetic  7.89 us (5%)
  local copies, waits for them, and re-layouts  2.06 us (1%)
    pallas_call x1, Pallas kernels, run_step(): pl.pallas_call(step_kernel, out_shape=out_shape, in_specs=[anywhere] * 5...  161 us
    convert_element_type x3, other arithmetic, on_device_cube(): new = [summed, updated, one_new, two_new, updated.astype(bf16)]  5.07 us

profile of v4, /device:TPU:0, one launch (start us, length us, event | category | flops | bytes accessed | tf_op | source)
XLA Modules:
  0.0 172.0 jit_solution(8697390773120079643)
XLA Ops:
  0.7 0.0 copy-start.2
  0.7 0.0 copy-start.3
  0.7 0.0 copy-start.4
  0.7 161.1 %step.1 = (bf16[1024,128]{1,0:T(8,128)(2,1)}, bf16[128,1024]{1,0:T(8,128)(2,1)}, f32[256,128]{1,0:T(8,128)}, f32[3,128,256]{2,1,0:T(8,128)}, bf16[1024,128]{1,0:...) custom-call(bf16[3,1024,256]{2,1,0:T(8,128)(2,1)} %bitcast.34, ...), custom_call_target="tpu_custom_call" | custom-call | tf_op jit(solution)/shard_map/step/pallas_call | solution.py:989
  161.8 0.0 copy-done.2
  161.8 0.0 copy-done.3
  161.8 0.0 copy-done.4
  161.8 0.0 copy-start.5
  161.8 0.0 copy-start.6
  161.9 0.0 copy-start.7
  161.9 0.0 copy-start.12
  161.9 0.0 copy-start.13
  161.9 2.7 %fusion.11 = (bf16[1024,128]{1,0:T(8,128)(2,1)}, f32[1024,128]{1,0:T(8,128)}, f32[1024,128]{1,0:T(8,128)}, f32[1024,128]{1,0:T(8,128)}, f32[1024,128]{1,0:T(8,128)}) fusion(f32[1024,128]{1,0:T(8,128)S(1)} %copy-done.2, f32[1024,128]{1,0:T(8,128)S(1)} %copy-done.3, f32[1024,128]{1,0:T(8,128)S(1)} %copy-done.4, bf16[1024,128]{1,0:T(8,128)(2,1)} %get-tuple-element.46, ...), kind=kLoop, calls=%fused_computation.32 | loop fusion | flops 2490368 | bytes 4456448 | tf_op jit(solution)/shard_map/convert_element_type | solution.py:1050
  164.6 0.0 copy-done.5
  164.6 0.0 copy-done.6
  164.6 0.0 copy-done.7
  164.6 0.0 copy-done.12
  164.6 0.0 copy-done.13
  164.6 0.0 copy-start.15
  164.6 0.0 copy-start.16
  164.6 0.0 copy-start.17
  164.6 0.0 copy-start.18
  164.6 0.0 copy-start.19
  164.7 0.0 copy-start.8
  164.7 0.0 copy-start.9
  164.7 0.0 copy-start.10
  164.7 0.0 copy-start.11
  164.7 0.0 copy-start.14
  164.7 1.6 fusion.13
  166.3 0.0 copy-done.15
  166.3 0.0 copy-done.16
  166.3 0.0 copy-done.17
  166.3 0.0 copy-done.18
  166.3 0.0 copy-done.19
  166.3 0.0 copy-start.20
  166.3 0.0 copy-start.21
  166.3 0.8 fusion.15
  167.2 0.0 copy-done.8
  167.2 0.0 copy-done.9
  167.2 0.0 copy-done.10
  167.2 0.0 copy-done.11
  167.2 0.0 copy-done.14
  167.2 0.0 copy-start
  167.2 1.5 convert_bitcast_fusion
  168.7 0.0 copy-done.20
  168.7 1.3 multiply_subtract_fusion.3
  170.0 1.0 copy.50
  171.0 1.0 copy.51
  (4 shorter events, 0.0 us)
Async XLA Ops:
  0.7 161.1 %copy-start.2 = (f32[1024,128]{1,0:T(8,128)S(1)}, f32[1024,128]{1,0:T(8,128)}, u32[]{:S(2)}) copy-start(f32[1024,128]{1,0:T(8,128)} %param.39) | copy-start | bytes 1572868
  0.7 161.1 %copy-start.3 = (f32[1024,128]{1,0:T(8,128)S(1)}, f32[1024,128]{1,0:T(8,128)}, u32[]{:S(2)}) copy-start(f32[1024,128]{1,0:T(8,128)} %param.40) | copy-start | bytes 1572868
  0.7 161.1 %copy-start.4 = (f32[1024,128]{1,0:T(8,128)S(1)}, f32[1024,128]{1,0:T(8,128)}, u32[]{:S(2)}) copy-start(f32[1024,128]{1,0:T(8,128)} %param.41) | copy-start | bytes 1572868
  161.8 2.7 %copy-start.5 = (f32[128,1024]{1,0:T(8,128)S(1)}, f32[128,1024]{1,0:T(8,128)}, u32[]{:S(2)}) copy-start(f32[128,1024]{1,0:T(8,128)} %param.36) | copy-start | bytes 1572868
  161.8 2.7 %copy-start.6 = (f32[128,1024]{1,0:T(8,128)S(1)}, f32[128,1024]{1,0:T(8,128)}, u32[]{:S(2)}) copy-start(f32[128,1024]{1,0:T(8,128)} %param.37) | copy-start | bytes 1572868
  161.9 2.7 %copy-start.7 = (f32[128,1024]{1,0:T(8,128)S(1)}, f32[128,1024]{1,0:T(8,128)}, u32[]{:S(2)}) copy-start(f32[128,1024]{1,0:T(8,128)} %param.38) | copy-start | bytes 1572868
  161.9 2.7 %copy-start.12 = (bf16[128,1024]{1,0:T(8,128)(2,1)S(1)}, bf16[128,1024]{1,0:T(8,128)(2,1)}, u32[]{:S(2)}) copy-start(bf16[128,1024]{1,0:T(8,128)(2,1)} %get-tuple-element.43) | copy-start | bytes 786436
  161.9 2.7 %copy-start.13 = (bf16[128,1024]{1,0:T(8,128)(2,1)S(1)}, bf16[128,1024]{1,0:T(8,128)(2,1)}, u32[]{:S(2)}) copy-start(bf16[128,1024]{1,0:T(8,128)(2,1)} %get-tuple-element.44) | copy-start | bytes 786436
  164.6 1.7 copy-start.15
  164.6 1.7 copy-start.16
  164.6 1.7 copy-start.17
  164.6 1.7 copy-start.18
  164.6 1.7 copy-start.19
  164.7 2.5 %copy-start.8 = (f32[128,3,256]{2,0,1:T(8,128)S(1)}, f32[128,3,256]{2,0,1:T(8,128)}, u32[]{:S(2)}) copy-start(f32[128,3,256]{2,0,1:T(8,128)} %param.32) | copy-start | bytes 1179652
  164.7 2.5 %copy-start.9 = (f32[128,3,256]{2,0,1:T(8,128)S(1)}, f32[128,3,256]{2,0,1:T(8,128)}, u32[]{:S(2)}) copy-start(f32[128,3,256]{2,0,1:T(8,128)} %param.31) | copy-start | bytes 1179652
  164.7 2.5 %copy-start.10 = (f32[128,3,256]{2,0,1:T(8,128)S(1)}, f32[128,3,256]{2,0,1:T(8,128)}, u32[]{:S(2)}) copy-start(f32[128,3,256]{2,0,1:T(8,128)} %param.30) | copy-start | bytes 1179652
  164.7 2.5 %copy-start.11 = (f32[3,128,256]{2,1,0:T(8,128)S(1)}, f32[3,128,256]{2,1,0:T(8,128)}, u32[]{:S(2)}) copy-start(f32[3,128,256]{2,1,0:T(8,128)} %get-tuple-element.39) | copy-start | bytes 1179652
  164.7 2.5 %copy-start.14 = (bf16[3,128,256]{2,1,0:T(8,128)(2,1)S(1)}, bf16[3,128,256]{2,1,0:T(8,128)(2,1)}, u32[]{:S(2)}) copy-start(bf16[3,128,256]{2,1,0:T(8,128)(2,1)} %get-tuple-element.40) | copy-start | bytes 589828
  166.3 2.4 %copy-start.20 = (f32[4,128]{1,0:T(4,128)S(1)}, f32[4,128]{1,0:T(4,128)}, u32[]{:S(2)}) copy-start(f32[4,128]{1,0:T(4,128)} %param.42) | copy-start | bytes 6148
  166.3 2.4 %copy-start.21 = (f32[4,128]{1,0:T(4,128)S(1)}, f32[4,128]{1,0:T(4,128)}, u32[]{:S(2)}) copy-start(f32[4,128]{1,0:T(4,128)} %param.43) | copy-start | bytes 6148
  167.2 2.9 %copy-start.1 = (f32[256,1024]{1,0:T(8,128)S(1)}, f32[256,1024]{1,0:T(8,128)}, u32[]{:S(2)}) copy-start(f32[256,1024]{1,0:T(8,128)} %get-tuple-element.98) | copy-start | bytes 3145732
  167.2 3.8 %copy-start = (f32[256,1024]{1,0:T(8,128)S(1)}, f32[256,1024]{1,0:T(8,128)}, u32[]{:S(2)}) copy-start(f32[256,1024]{1,0:T(8,128)} %get-tuple-element.99) | copy-start | bytes 3145732

commit v5 on v4

--- a/solution.py
+++ b/solution.py
@@ -282,7 +282,7 @@
 RING = 2
 OWN = PLANES - 1
 UNITS = (
-    (0, 0), (0, 3), (1, 0), (1, 3), (3, 0), (3, 1), (3, 2), (3, 3), (2, 0), (2, 1), (2, 2), (2, 3),
+    (0, 3), (0, 0), (1, 3), (1, 0), (3, 0), (3, 1), (3, 2), (3, 3), (2, 0), (2, 1), (2, 2), (2, 3),
 )
 TURNED_AT = (0, 1, 1, 0)
 (
@@ -291,34 +291,34 @@
     FINISH, INPUTS, NORM, NORMS_OUT, POINTS,
 ) = range(31)
 SCHEDULE = (
-    (SEND_OWN, 1), (SEND_OWN, 0), (TAKE, 1, 0, 0), (CORNER, 1, 0, 0), (TAKE, 0, 0, 0), (TAKE, 1, 0, 1),
-    (TAKE, 0, 1, 0), (TAKE, 0, 0, 1), (TAKE, 0, 1, 1), (CORNER, 1, 0, 1), (CROSS, 1, 0, 0), (TAKE, 1, 1, 1),
-    (CORNER, 0, 0, 1), (TAKE, 1, 1, 0), (TAKE, 1, 2, 1), (TAKE, 1, 2, 0), (LOAD, 0), (CORNER, 0, 1, 0),
-    (TAKE, 0, 2, 0), (TAKE, 0, 2, 1), (SEND_OWN, 2), (CORNER, 0, 1, 1), (SEND_OWN, 3), (ENTER,), (CORNER, 0, 0, 0),
-    (SEND_COTANGENT,), (CORNER, 0, 2, 1), (CORNER, 1, 2, 1), (PROJECT, 0), (CORNER, 1, 2, 0), (CROSS, 0, 1, 1),
-    (CROSS, 0, 1, 0), (CROSS, 0, 0, 0), (CORNER, 0, 2, 0), (CROSS, 0, 0, 1), (CORNER, 1, 1, 1), (LOAD, 4),
-    (CROSS, 1, 0, 1), (WHOLE, 0, 0), (LOAD, 1), (CROSS, 0, 2, 1), (CORNER, 1, 1, 0), (TAKE, 2, 0, 0), (WHOLE, 0, 1),
-    (LOAD, 2), (TAKE, 2, 0, 1), (PROJECT, 1), (CROSS, 0, 2, 0), (CROSS, 1, 2, 1), (TAKE, 3, 0, 0), (CROSS, 1, 2, 0),
-    (CROSS, 1, 1, 0), (WHOLE, 0, 2), (LOAD, 3), (PROJECT, 2), (WHOLE, 1, 2), (READY, 4), (CROSS, 1, 1, 1),
-    (TAKE, 3, 0, 1), (CORNER, 2, 0, 1), (WHOLE, 1, 1), (WHOLE, 1, 0), (CORNER, 2, 0, 0), (PROJECT, 3), (BRANCH,),
-    (CAME, 0), (LOAD, 6), (TURN, 0), (CORNER, 3, 0, 0), (READY, 6), (CROSS, 2, 0, 1), (CORNER, 3, 0, 1),
-    (WIDEN, 0, 0), (CROSS, 2, 0, 0), (WHOLE, 2, 0), (NARROW_BACK, 0, 0), (LOAD, 5), (READY, 5), (CROSS, 3, 0, 1),
-    (CROSS, 3, 0, 0), (WIDEN, 1, 0), (WHOLE, 3, 0), (LOAD, 7), (CAME, 1), (WIDEN, 1, 1), (PRODUCE, 0), (WIDEN, 0, 1),
-    (PRODUCE, 1), (JOIN, 0), (READY, 7), (NARROW_BACK, 0, 1), (NARROW_BACK, 1, 1), (JOIN, 1), (NARROW_BACK, 1, 0),
-    (WIDEN_BACK, 1), (TURN, 1), (ONE, 0, 1), (PRODUCE, 2), (ONE, 0, 0), (PRODUCE, 3), (JOIN, 2), (TURN, 3),
-    (WIDEN_BACK, 0), (JOIN, 3), (NARROW, 1), (RESIDUAL,), (ATTEND, 4), (PRODUCE, 4), (ONE, 2, 1), (ONE, 2, 0),
-    (ATTEND, 5), (JOIN, 4), (LOAD, 8), (PRODUCE, 5), (ATTEND, 6), (TWO, 2, 1), (JOIN, 5), (ONE, 1, 1), (ONE, 4, 0),
-    (LOAD, 9), (ONE, 4, 1), (PRODUCE, 6), (TURN, 2), (ATTEND, 7), (JOIN, 6), (TWO, 2, 0), (PRODUCE, 7), (TWO, 4, 0),
-    (TWO, 0, 0), (PRODUCE, 8), (PRODUCE, 9), (ONE, 3, 0), (JOIN, 9), (ONE, 5, 1), (JOIN, 8), (ONE, 5, 0), (NARROW, 0),
-    (TWO, 4, 1), (ONE, 9, 1), (ONE, 9, 0), (PRODUCE, 10), (TWO, 0, 1), (ALONG, 4, 0), (ONE, 3, 1), (LOAD, 10),
-    (ONE, 6, 0), (PRODUCE, 11), (ALONG, 4, 1), (INWARD, 8), (TWO, 5, 1), (JOIN, 7), (LOAD, 11), (TWO, 1, 1),
-    (JOIN, 10), (TWO, 9, 1), (TWO, 5, 0), (ONE, 8, 1), (TWO, 9, 0), (ONE, 6, 1), (INWARD, 9), (INWARD, 10),
-    (INWARD, 11), (JOIN, 11), (INPUTS,), (TWO, 6, 0), (ALONG, 5, 1), (ALONG, 9, 1), (ONE, 8, 0), (NORM, 0),
-    (ALONG, 6, 0), (ONE, 10, 0), (ONE, 1, 0), (ONE, 10, 1), (TWO, 8, 1), (TWO, 8, 0), (NORM, 1), (ONE, 7, 0),
-    (ONE, 11, 1), (ALONG, 8, 1), (TWO, 10, 0), (LATENTS,), (TWO, 6, 1), (ALONG, 6, 1), (ALONG, 8, 0), (ONE, 7, 1),
-    (TWO, 10, 1), (ALONG, 5, 0), (ALONG, 10, 1), (TWO, 1, 0), (NORM, 2), (ONE, 11, 0), (TWO, 11, 1), (TWO, 3, 1),
-    (TWO, 3, 0), (FINISH, 1), (ALONG, 9, 0), (ALONG, 10, 0), (FINISH, 0), (POINTS,), (TWO, 7, 1), (TWO, 7, 0),
-    (TWO, 11, 0), (FINISH, 3), (NORMS_OUT,), (FINISH, 2),
+    (SEND_OWN, 0), (TAKE, 0, 0, 0), (SEND_OWN, 1), (TAKE, 0, 0, 1), (TAKE, 0, 1, 0), (CORNER, 0, 0, 0),
+    (TAKE, 0, 2, 0), (CORNER, 0, 0, 1), (TAKE, 0, 1, 1), (CORNER, 0, 1, 0), (TAKE, 1, 0, 0), (TAKE, 1, 0, 1),
+    (TAKE, 0, 2, 1), (SEND_OWN, 2), (ENTER,), (CORNER, 0, 1, 1), (TAKE, 1, 1, 0), (CROSS, 0, 0, 1), (TAKE, 1, 2, 1),
+    (TAKE, 1, 2, 0), (CROSS, 0, 0, 0), (CORNER, 1, 0, 1), (CORNER, 0, 2, 0), (TAKE, 1, 1, 1), (SEND_OWN, 3),
+    (LOAD, 0), (CORNER, 0, 2, 1), (CROSS, 0, 1, 1), (WHOLE, 0, 0), (CORNER, 1, 2, 1), (CROSS, 0, 1, 0), (LOAD, 1),
+    (CORNER, 1, 2, 0), (PROJECT, 0), (CROSS, 1, 0, 1), (SEND_COTANGENT,), (WHOLE, 0, 1), (LOAD, 4), (LOAD, 2),
+    (PROJECT, 1), (CORNER, 1, 0, 0), (CORNER, 1, 1, 1), (CORNER, 1, 1, 0), (CROSS, 0, 2, 0), (TAKE, 2, 0, 1),
+    (TAKE, 2, 0, 0), (CROSS, 0, 2, 1), (PROJECT, 2), (WHOLE, 0, 2), (LOAD, 3), (CROSS, 1, 1, 1), (LOAD, 6),
+    (TAKE, 3, 0, 1), (TAKE, 3, 0, 0), (CROSS, 1, 0, 0), (CROSS, 1, 2, 0), (CROSS, 1, 1, 0), (CROSS, 1, 2, 1),
+    (PROJECT, 3), (WHOLE, 1, 0), (READY, 4), (CORNER, 2, 0, 0), (CORNER, 2, 0, 1), (WHOLE, 1, 2), (WHOLE, 1, 1),
+    (BRANCH,), (CORNER, 3, 0, 0), (CAME, 0), (CORNER, 3, 0, 1), (CROSS, 2, 0, 1), (READY, 6), (CROSS, 2, 0, 0),
+    (TURN, 0), (WIDEN, 0, 0), (WHOLE, 2, 0), (LOAD, 5), (NARROW_BACK, 0, 0), (CROSS, 3, 0, 1), (READY, 5),
+    (CROSS, 3, 0, 0), (WIDEN, 1, 0), (CAME, 1), (WIDEN, 0, 1), (PRODUCE, 0), (WHOLE, 3, 0), (WIDEN, 1, 1),
+    (PRODUCE, 1), (JOIN, 0), (LOAD, 7), (TURN, 1), (JOIN, 1), (READY, 7), (NARROW_BACK, 0, 1), (NARROW_BACK, 1, 1),
+    (WIDEN_BACK, 1), (PRODUCE, 2), (NARROW_BACK, 1, 0), (ONE, 0, 0), (ONE, 0, 1), (PRODUCE, 3), (JOIN, 2), (TURN, 3),
+    (NARROW, 1), (JOIN, 3), (ONE, 1, 0), (WIDEN_BACK, 0), (ONE, 1, 1), (RESIDUAL,), (ATTEND, 4), (PRODUCE, 4),
+    (ATTEND, 5), (ONE, 3, 0), (ONE, 3, 1), (JOIN, 4), (PRODUCE, 5), (ATTEND, 6), (LOAD, 9), (JOIN, 5), (PRODUCE, 6),
+    (LOAD, 8), (TWO, 0, 0), (TWO, 3, 0), (ATTEND, 7), (PRODUCE, 7), (NARROW, 0), (TWO, 3, 1), (JOIN, 6), (ONE, 4, 1),
+    (TWO, 1, 1), (LOAD, 10), (LOAD, 11), (TURN, 2), (PRODUCE, 8), (INWARD, 8), (ONE, 5, 1), (ONE, 4, 0), (INWARD, 9),
+    (PRODUCE, 9), (JOIN, 8), (ONE, 2, 0), (JOIN, 9), (INWARD, 10), (TWO, 4, 1), (PRODUCE, 10), (PRODUCE, 11),
+    (ONE, 6, 1), (INWARD, 11), (TWO, 4, 0), (ONE, 8, 1), (ONE, 5, 0), (TWO, 5, 1), (TWO, 1, 0), (ONE, 8, 0),
+    (ALONG, 4, 1), (JOIN, 7), (JOIN, 10), (ONE, 9, 1), (INPUTS,), (TWO, 0, 1), (NORM, 0), (ONE, 9, 0), (TWO, 2, 0),
+    (ONE, 6, 0), (ALONG, 4, 0), (TWO, 6, 1), (POINTS,), (JOIN, 11), (ALONG, 5, 1), (TWO, 8, 0), (TWO, 8, 1),
+    (ALONG, 6, 1), (TWO, 5, 0), (ONE, 7, 1), (NORM, 1), (ONE, 10, 1), (ONE, 10, 0), (ONE, 7, 0), (ALONG, 8, 0),
+    (ONE, 2, 1), (TWO, 9, 1), (ALONG, 8, 1), (TWO, 9, 0), (TWO, 6, 0), (ALONG, 6, 0), (ONE, 11, 0), (ALONG, 5, 0),
+    (LATENTS,), (ONE, 11, 1), (TWO, 10, 1), (ALONG, 10, 1), (TWO, 7, 1), (ALONG, 9, 0), (TWO, 10, 0), (ALONG, 10, 0),
+    (NORM, 2), (ALONG, 9, 1), (TWO, 2, 1), (FINISH, 1), (TWO, 7, 0), (TWO, 11, 0), (FINISH, 3), (FINISH, 0),
+    (TWO, 11, 1), (FINISH, 2), (NORMS_OUT,),
 )
 NN = ((1,), (0,))
 NT = ((1,), (1,))
@@ -1000,6 +1000,78 @@
     return result[:4], result[4:8], result[8], result[9], result[10]
 
 
+UPDATES = ((3, D ** (-0.5)), (2, max(1, D * 4 // LAT) ** (-0.5)), (1, D ** (-0.5)), (0, FF ** (-0.5)))
+
+
+def update_kernel(*refs):
+    given, passed, (norm_sum, norms, norm_first, norm_second) = refs[0:20], refs[20:22], refs[22:26]
+    passed_out, new_out, norm_out = refs[26:28], refs[28:48], refs[48:52]
+    here, rows_here, new, in_sem, out_sem = refs[52:72], refs[72:74], refs[74:94], refs[94], refs[95]
+    loads = [pltpu.make_async_copy(a, b, in_sem.at[n]) for n, (a, b) in enumerate(zip(given, here))]
+    loads += [pltpu.make_async_copy(a, b, in_sem.at[20 + n]) for n, (a, b) in enumerate(zip(passed, rows_here))]
+    stores = [pltpu.make_async_copy(a, b, out_sem.at[n]) for n, (a, b) in enumerate(zip(new, new_out))]
+    stores += [pltpu.make_async_copy(a, b, out_sem.at[20 + n]) for n, (a, b) in enumerate(zip(rows_here, passed_out))]
+    for copy in loads:
+        copy.start()
+    columns = pl.ds(pl.multiple_of(lax.axis_index("dp") * BLOCK, BLOCK), BLOCK)
+    gradient = norm_sum[:, columns]
+    norm_out[0][...] = gradient
+    results = adamw_step(norms[:, columns], gradient, norm_first[...], norm_second[...], 0.2)
+    for n in range(3):
+        norm_out[1 + n][...] = results[n]
+    for n, (_, rate) in enumerate(UPDATES):
+        for copy in loads[5 * n : 5 * n + 5]:
+            copy.wait()
+        first, second, master, one, two = here[5 * n : 5 * n + 5]
+        targets = new[5 * n : 5 * n + 5]
+        width = first.shape[-1]
+        strip = 16 * D // width
+        strip = min(strip, first.shape[-2])
+
+        def update(at, rate=rate, first=first, second=second, master=master, one=one, two=two, targets=targets):
+            total = first[at].astype(jnp.float32) + second[at].astype(jnp.float32)
+            updated, one_new, two_new = adamw_step(master[at], total, one[at], two[at], rate)
+            for target, value in zip(targets, (total, updated, one_new, two_new, updated)):
+                target[at] = value.astype(target.dtype)
+
+        def step(r, carry, strip=strip, update=update, parts=first.shape[:-2]):
+            rows = pl.ds(pl.multiple_of(r * strip, strip), strip)
+            if parts:
+                for part in range(parts[0]):
+                    update((part, rows, slice(None)))
+            else:
+                update((rows, slice(None)))
+            return carry
+
+        lax.fori_loop(0, first.shape[-2] // strip, step, 0)
+        for copy in stores[5 * n : 5 * n + 5]:
+            copy.start()
+    for n in (20, 21):
+        loads[n].wait()
+        stores[n].start()
+    for copy in stores:
+        copy.wait()
+
+
+def run_update(given, passed, norm_sum, norms, norm_first, norm_second):
+    f32, bf16 = jnp.float32, jnp.bfloat16
+    vmem_of, dma = pltpu.VMEM, pltpu.SemaphoreType.DMA
+    new = [(a.shape, bf16 if n == 4 else f32) for a in given[2::5] for n in range(5)]
+    norm_new = [(norm_first.shape, f32)] * 4
+    rows_new = [(a.shape, a.dtype) for a in passed]
+    anywhere, vmem = pl.BlockSpec(memory_space=pl.ANY), pl.BlockSpec(memory_space=pltpu.VMEM)
+    scratch = [vmem_of(a.shape, a.dtype) for a in (*given, *passed)] + [vmem_of(*a) for a in new]
+    return pl.pallas_call(
+        update_kernel,
+        out_shape=[jax.ShapeDtypeStruct(*a) for a in rows_new + new + norm_new],
+        in_specs=[anywhere] * 22 + [vmem] * 4,
+        out_specs=[anywhere] * 22 + [vmem] * 4,
+        scratch_shapes=scratch + [dma((22,)), dma((22,))],
+        name="update",
+        compiler_params=pltpu.CompilerParams(vmem_limit_bytes=60 << 20),
+    )(*given, *passed, norm_sum, norms, norm_first, norm_second)
+
+
 def on_device_cube(
     points,
     members,
@@ -1024,7 +1096,6 @@
     norm_first,
     norm_second,
 ):
-    bf16 = jnp.bfloat16
     firsts, seconds, norm_summed, latents, point_gradient = run_step(
         (jnp.transpose(project_weight, (1, 0, 2)), output_weight, upward_weight, downward_weight),
         points,
@@ -1032,26 +1103,16 @@
         members,
         layer_norms,
     )
-    data_index = lax.axis_index("dp")
-    norm_columns = norm_first.shape[1]
-    norm_gradient = lax.dynamic_slice_in_dim(norm_summed, data_index * norm_columns, norm_columns, 1)
-    norm_current = lax.dynamic_slice_in_dim(layer_norms, data_index * norm_columns, norm_columns, 1)
-    results = [latents, point_gradient]
     swap = lambda array: jnp.transpose(array, (1, 0, 2))
-    for w, states, rate in (
-        (3, [swap(a) for a in (project_master, project_first, project_second)], D ** (-0.5)),
-        (2, [output_master, output_first, output_second], max(1, D * 4 // LAT) ** (-0.5)),
-        (1, [upward_master, upward_first, upward_second], D ** (-0.5)),
-        (0, [downward_master, downward_first, downward_second], FF ** (-0.5)),
-    ):
-        master, first, second = states
-        summed = firsts[w].astype(jnp.float32) + seconds[w].astype(jnp.float32)
-        updated, one_new, two_new = adamw_step(master, summed, first, second, rate)
-        new = [summed, updated, one_new, two_new, updated.astype(bf16)]
-        results += [swap(a) for a in new] if w == 3 else new
-    norm_new = adamw_step(norm_current, norm_gradient, norm_first, norm_second, 0.2)
-    results += [norm_gradient, *norm_new]
-    return tuple(results)
+    states = {
+        3: [swap(a) for a in (project_master, project_first, project_second)],
+        2: [output_master, output_first, output_second],
+        1: [upward_master, upward_first, upward_second],
+        0: [downward_master, downward_first, downward_second],
+    }
+    given = [array for w, _ in UPDATES for array in (firsts[w], seconds[w], *states[w])]
+    results = run_update(given, (latents, point_gradient), norm_summed, layer_norms, norm_first, norm_second)
+    return (*results[:2], *[swap(a) for a in results[2:7]], *results[7:])
 
 
 def solution(mesh):

time: 172 us -> 164 us (0.953)
  other arithmetic: 7.89 us -> 0 us
  local copies, waits for them, and re-layouts: 2.06 us -> 0 us
  Pallas kernels: 161 us -> 163 us
    pallas_call x0 -> x1, Pallas kernels: none -> 8.28 us  [run_update(): pl.pallas_call(update_kernel, out_shape=[jax.ShapeDtypeStruct(*a) for a i...]
    pallas_call x1, Pallas kernels: 161 us -> 155 us  [run_step(): pl.pallas_call(step_kernel, out_shape=out_shape, in_specs=[anywhere] * 5...]
    convert_element_type x3 -> x0, other arithmetic: 5.07 us -> none  [on_device_cube(): new = [summed, updated, one_new, two_new, updated.astype(bf16)]]
    unnamed x46 -> x0, local copies, waits for them, and re-layouts: 2.06 us -> none
where the time goes in v5:
time: 164 us
  Pallas kernels  163 us (99%)
    pallas_call x1, Pallas kernels, run_step(): pl.pallas_call(step_kernel, out_shape=out_shape, in_specs=[anywhere] * 5...  155 us
    pallas_call x1, Pallas kernels, run_update(): pl.pallas_call(update_kernel, out_shape=[jax.ShapeDtypeStruct(*a) for a i...  8.28 us

profile of v5, /device:TPU:0, one launch (start us, length us, event | category | flops | bytes accessed | tf_op | source)
XLA Modules:
  0.0 164.0 jit_solution(17624315159655387440)
XLA Ops:
  0.7 154.9 %step.1 = (bf16[1024,128]{1,0:T(8,128)(2,1)}, bf16[128,1024]{1,0:T(8,128)(2,1)}, f32[256,128]{1,0:T(8,128)}, f32[3,128,256]{2,1,0:T(8,128)}, bf16[1024,128]{1,0:...) custom-call(bf16[3,1024,256]{2,1,0:T(8,128)(2,1)} %bitcast.9, ...), custom_call_target="tpu_custom_call" | custom-call | tf_op jit(solution)/shard_map/step/pallas_call | solution.py:989
  155.6 8.3 %update.1 = (f32[256,1024]{1,0:T(8,128)}, f32[256,1024]{1,0:T(8,128)}, f32[3,128,256]{2,1,0:T(8,128)}, f32[3,128,256]{2,1,0:T(8,128)}, f32[3,128,256]{2,1,0:T(8,...) custom-call(f32[3,128,256]{2,1,0:T(8,128)} %get-tuple-element.63.ref, ...), custom_call_target="tpu_custom_call" | custom-call | tf_op jit(solution)/shard_map/update/pallas_call | solution.py:1064

commit v6 on v5

--- a/solution.py
+++ b/solution.py
@@ -282,43 +282,43 @@
 RING = 2
 OWN = PLANES - 1
 UNITS = (
-    (0, 3), (0, 0), (1, 3), (1, 0), (3, 0), (3, 1), (3, 2), (3, 3), (2, 0), (2, 1), (2, 2), (2, 3),
+    (0, 0), (0, 3), (1, 0), (1, 3), (3, 0), (3, 1), (3, 2), (3, 3), (2, 0), (2, 1), (2, 2), (2, 3),
 )
+EARLY = (3,)
 TURNED_AT = (0, 1, 1, 0)
 (
     SEND_OWN, TAKE, CORNER, CROSS, WHOLE, LOAD, READY, ENTER, PROJECT, BRANCH, SEND_COTANGENT, CAME, WIDEN,
     NARROW_BACK, WIDEN_BACK, NARROW, LATENTS, RESIDUAL, ATTEND, INWARD, TURN, PRODUCE, JOIN, ONE, TWO, ALONG,
-    FINISH, INPUTS, NORM, NORMS_OUT, POINTS,
-) = range(31)
+    LAST, FINISH, INPUTS, NORM, NORMS_OUT, POINTS,
+) = range(32)
 SCHEDULE = (
-    (SEND_OWN, 0), (TAKE, 0, 0, 0), (SEND_OWN, 1), (TAKE, 0, 0, 1), (TAKE, 0, 1, 0), (CORNER, 0, 0, 0),
-    (TAKE, 0, 2, 0), (CORNER, 0, 0, 1), (TAKE, 0, 1, 1), (CORNER, 0, 1, 0), (TAKE, 1, 0, 0), (TAKE, 1, 0, 1),
-    (TAKE, 0, 2, 1), (SEND_OWN, 2), (ENTER,), (CORNER, 0, 1, 1), (TAKE, 1, 1, 0), (CROSS, 0, 0, 1), (TAKE, 1, 2, 1),
-    (TAKE, 1, 2, 0), (CROSS, 0, 0, 0), (CORNER, 1, 0, 1), (CORNER, 0, 2, 0), (TAKE, 1, 1, 1), (SEND_OWN, 3),
-    (LOAD, 0), (CORNER, 0, 2, 1), (CROSS, 0, 1, 1), (WHOLE, 0, 0), (CORNER, 1, 2, 1), (CROSS, 0, 1, 0), (LOAD, 1),
-    (CORNER, 1, 2, 0), (PROJECT, 0), (CROSS, 1, 0, 1), (SEND_COTANGENT,), (WHOLE, 0, 1), (LOAD, 4), (LOAD, 2),
-    (PROJECT, 1), (CORNER, 1, 0, 0), (CORNER, 1, 1, 1), (CORNER, 1, 1, 0), (CROSS, 0, 2, 0), (TAKE, 2, 0, 1),
-    (TAKE, 2, 0, 0), (CROSS, 0, 2, 1), (PROJECT, 2), (WHOLE, 0, 2), (LOAD, 3), (CROSS, 1, 1, 1), (LOAD, 6),
-    (TAKE, 3, 0, 1), (TAKE, 3, 0, 0), (CROSS, 1, 0, 0), (CROSS, 1, 2, 0), (CROSS, 1, 1, 0), (CROSS, 1, 2, 1),
-    (PROJECT, 3), (WHOLE, 1, 0), (READY, 4), (CORNER, 2, 0, 0), (CORNER, 2, 0, 1), (WHOLE, 1, 2), (WHOLE, 1, 1),
-    (BRANCH,), (CORNER, 3, 0, 0), (CAME, 0), (CORNER, 3, 0, 1), (CROSS, 2, 0, 1), (READY, 6), (CROSS, 2, 0, 0),
-    (TURN, 0), (WIDEN, 0, 0), (WHOLE, 2, 0), (LOAD, 5), (NARROW_BACK, 0, 0), (CROSS, 3, 0, 1), (READY, 5),
-    (CROSS, 3, 0, 0), (WIDEN, 1, 0), (CAME, 1), (WIDEN, 0, 1), (PRODUCE, 0), (WHOLE, 3, 0), (WIDEN, 1, 1),
-    (PRODUCE, 1), (JOIN, 0), (LOAD, 7), (TURN, 1), (JOIN, 1), (READY, 7), (NARROW_BACK, 0, 1), (NARROW_BACK, 1, 1),
-    (WIDEN_BACK, 1), (PRODUCE, 2), (NARROW_BACK, 1, 0), (ONE, 0, 0), (ONE, 0, 1), (PRODUCE, 3), (JOIN, 2), (TURN, 3),
-    (NARROW, 1), (JOIN, 3), (ONE, 1, 0), (WIDEN_BACK, 0), (ONE, 1, 1), (RESIDUAL,), (ATTEND, 4), (PRODUCE, 4),
-    (ATTEND, 5), (ONE, 3, 0), (ONE, 3, 1), (JOIN, 4), (PRODUCE, 5), (ATTEND, 6), (LOAD, 9), (JOIN, 5), (PRODUCE, 6),
-    (LOAD, 8), (TWO, 0, 0), (TWO, 3, 0), (ATTEND, 7), (PRODUCE, 7), (NARROW, 0), (TWO, 3, 1), (JOIN, 6), (ONE, 4, 1),
-    (TWO, 1, 1), (LOAD, 10), (LOAD, 11), (TURN, 2), (PRODUCE, 8), (INWARD, 8), (ONE, 5, 1), (ONE, 4, 0), (INWARD, 9),
-    (PRODUCE, 9), (JOIN, 8), (ONE, 2, 0), (JOIN, 9), (INWARD, 10), (TWO, 4, 1), (PRODUCE, 10), (PRODUCE, 11),
-    (ONE, 6, 1), (INWARD, 11), (TWO, 4, 0), (ONE, 8, 1), (ONE, 5, 0), (TWO, 5, 1), (TWO, 1, 0), (ONE, 8, 0),
-    (ALONG, 4, 1), (JOIN, 7), (JOIN, 10), (ONE, 9, 1), (INPUTS,), (TWO, 0, 1), (NORM, 0), (ONE, 9, 0), (TWO, 2, 0),
-    (ONE, 6, 0), (ALONG, 4, 0), (TWO, 6, 1), (POINTS,), (JOIN, 11), (ALONG, 5, 1), (TWO, 8, 0), (TWO, 8, 1),
-    (ALONG, 6, 1), (TWO, 5, 0), (ONE, 7, 1), (NORM, 1), (ONE, 10, 1), (ONE, 10, 0), (ONE, 7, 0), (ALONG, 8, 0),
-    (ONE, 2, 1), (TWO, 9, 1), (ALONG, 8, 1), (TWO, 9, 0), (TWO, 6, 0), (ALONG, 6, 0), (ONE, 11, 0), (ALONG, 5, 0),
-    (LATENTS,), (ONE, 11, 1), (TWO, 10, 1), (ALONG, 10, 1), (TWO, 7, 1), (ALONG, 9, 0), (TWO, 10, 0), (ALONG, 10, 0),
-    (NORM, 2), (ALONG, 9, 1), (TWO, 2, 1), (FINISH, 1), (TWO, 7, 0), (TWO, 11, 0), (FINISH, 3), (FINISH, 0),
-    (TWO, 11, 1), (FINISH, 2), (NORMS_OUT,),
+    (SEND_OWN, 0), (LOAD, 0), (SEND_OWN, 1), (ENTER,), (TAKE, 0, 0, 0), (TAKE, 0, 1, 0), (TAKE, 0, 0, 1),
+    (TAKE, 0, 1, 1), (TAKE, 1, 0, 1), (TAKE, 1, 0, 0), (TAKE, 0, 2, 0), (SEND_OWN, 2), (CORNER, 0, 0, 1),
+    (CORNER, 0, 1, 0), (CORNER, 0, 2, 0), (CORNER, 1, 0, 1), (CORNER, 0, 1, 1), (TAKE, 1, 1, 0), (TAKE, 0, 2, 1),
+    (CROSS, 0, 0, 1), (CORNER, 0, 0, 0), (TAKE, 1, 1, 1), (TAKE, 1, 2, 1), (PROJECT, 0), (CORNER, 1, 0, 0),
+    (CROSS, 0, 1, 0), (TAKE, 1, 2, 0), (SEND_OWN, 3), (CORNER, 0, 2, 1), (CROSS, 0, 1, 1), (CORNER, 1, 2, 0),
+    (CORNER, 1, 1, 0), (CROSS, 1, 0, 1), (CROSS, 0, 2, 0), (LOAD, 4), (SEND_COTANGENT,), (CROSS, 0, 0, 0),
+    (CORNER, 1, 1, 1), (CORNER, 1, 2, 1), (WHOLE, 0, 0), (LOAD, 1), (CROSS, 0, 2, 1), (CROSS, 1, 0, 0),
+    (TAKE, 2, 0, 1), (TAKE, 2, 0, 0), (WHOLE, 0, 1), (TAKE, 3, 0, 0), (READY, 4), (CROSS, 1, 2, 0), (WHOLE, 0, 2),
+    (LOAD, 2), (LOAD, 3), (PROJECT, 1), (TAKE, 3, 0, 1), (CROSS, 1, 1, 1), (CROSS, 1, 1, 0), (CROSS, 1, 2, 1),
+    (PROJECT, 2), (LOAD, 6), (WHOLE, 1, 0), (WHOLE, 1, 2), (CORNER, 2, 0, 1), (WHOLE, 1, 1), (CORNER, 2, 0, 0),
+    (PROJECT, 3), (BRANCH,), (WIDEN, 0, 0), (CORNER, 3, 0, 0), (CAME, 0), (CORNER, 3, 0, 1), (READY, 6),
+    (CROSS, 2, 0, 0), (CROSS, 2, 0, 1), (NARROW_BACK, 0, 0), (WHOLE, 2, 0), (LOAD, 5), (TURN, 0), (CROSS, 3, 0, 0),
+    (CROSS, 3, 0, 1), (READY, 5), (WIDEN, 1, 0), (CAME, 1), (WIDEN, 1, 1), (PRODUCE, 0), (WIDEN, 0, 1), (WHOLE, 3, 0),
+    (LOAD, 7), (PRODUCE, 1), (JOIN, 0), (READY, 7), (NARROW_BACK, 1, 1), (NARROW_BACK, 0, 1), (WIDEN_BACK, 1),
+    (JOIN, 1), (NARROW_BACK, 1, 0), (TURN, 1), (PRODUCE, 2), (ONE, 0, 0), (PRODUCE, 3), (ONE, 0, 1), (NARROW, 1),
+    (JOIN, 2), (TURN, 3), (JOIN, 3), (WIDEN_BACK, 0), (RESIDUAL,), (TWO, 0, 1), (ATTEND, 4), (ONE, 2, 1), (ONE, 2, 0),
+    (PRODUCE, 4), (ATTEND, 5), (TWO, 0, 0), (JOIN, 4), (PRODUCE, 5), (ATTEND, 7), (TWO, 2, 1), (JOIN, 5), (TWO, 2, 0),
+    (ATTEND, 6), (PRODUCE, 6), (PRODUCE, 7), (ONE, 3, 1), (LOAD, 8), (LOAD, 9), (ONE, 4, 0), (TURN, 2), (JOIN, 6),
+    (PRODUCE, 8), (INWARD, 8), (PRODUCE, 9), (JOIN, 8), (ONE, 4, 1), (NARROW, 0), (JOIN, 9), (LOAD, 10), (ONE, 5, 0),
+    (PRODUCE, 10), (ONE, 1, 0), (ONE, 5, 1), (INWARD, 9), (LOAD, 11), (ALONG, 4, 0), (ONE, 1, 1), (TWO, 3, 1),
+    (ONE, 8, 1), (PRODUCE, 11), (INWARD, 10), (INWARD, 11), (JOIN, 11), (ONE, 6, 0), (ALONG, 4, 1), (JOIN, 10),
+    (INPUTS,), (ONE, 8, 0), (ALONG, 6, 0), (TWO, 1, 0), (ALONG, 5, 0), (ONE, 9, 0), (JOIN, 7), (ONE, 10, 0),
+    (TWO, 8, 0), (NORM, 0), (ONE, 9, 1), (TWO, 8, 1), (TWO, 1, 1), (ONE, 10, 1), (ONE, 3, 0), (ALONG, 5, 1),
+    (ONE, 6, 1), (ONE, 11, 1), (ALONG, 6, 1), (TWO, 9, 0), (POINTS,), (ONE, 7, 1), (NORM, 1), (TWO, 9, 1),
+    (FINISH, 0), (TWO, 10, 0), (ALONG, 8, 1), (ONE, 7, 0), (ONE, 11, 0), (TWO, 10, 1), (LAST, 3, 0), (ALONG, 8, 0),
+    (LATENTS,), (NORM, 2), (TWO, 3, 0), (FINISH, 1), (TWO, 11, 1), (LAST, 3, 1), (ALONG, 10, 1), (ALONG, 9, 0),
+    (ALONG, 10, 0), (ALONG, 9, 1), (NORMS_OUT,), (TWO, 11, 0), (FINISH, 2), (FINISH, 3),
 )
 NN = ((1,), (0,))
 NT = ((1,), (1,))
@@ -661,7 +661,7 @@
 
     def two_in_at(t, half):
         w, i = UNITS[t]
-        return two_in[w].at[i if w >= 2 else i // OWN, half]
+        return two_in[w].at[0 if w in EARLY else i if w >= 2 else i // OWN, half]
 
     def one_copy(t, half):
         rows = half_rows(half)
@@ -675,10 +675,26 @@
         send, recv = two_send.at[t, half], two_recv.at[t, half]
         return remote(src, two_in_at(t, half), send, recv, (over_x, over_y)[half])
 
+    def z_piece(t, half):
+        rows = half_rows(half)
+        if UNITS[t][0] in EARLY:
+            return here(t).at[y, :, rows] if half == 0 else here(t).at[:, x, rows]
+        return here(t).at[y, x, rows]
+
     def z_copy(t, half, slot, target):
         w = UNITS[t][0]
         send, recv = z_send.at[t, half], z_recv.at[w, slot, half]
-        return remote(here(t).at[y, x, half_rows(half)], z_in[w].at[slot, half], send, recv, target)
+        return remote(z_piece(t, half), z_in[w].at[slot, half], send, recv, target)
+
+    def z_add(t, half, slot):
+        w = UNITS[t][0]
+        z_copy(t, half, slot, beside).wait_recv()
+        piece = z_piece(t, half)
+        if w in EARLY:
+            for k in (0, 1):
+                add_rows(piece.at[k], z_in[w].at[slot, half, k])
+        else:
+            add_rows(piece, z_in[w].at[slot, half])
 
     def z_first(t, half):
         w, i = UNITS[t]
@@ -691,13 +707,11 @@
             z_copy(t, half, 2 - i, beside).start()
 
     def z_pass(t, half):
-        w, i = UNITS[t]
+        i = UNITS[t][1]
 
         @pl.when(is_mid)
         def _():
-            slot = (2, 1, 3)[i]
-            z_copy(t, half, slot, beside).wait_recv()
-            add_rows(here(t).at[y, x, half_rows(half)], z_in[w].at[slot, half])
+            z_add(t, half, (2, 1, 3)[i])
             z_copy(t, half, (3, 4, 0)[i], (across, across, beside)[i]).start()
 
     def add_rows(target, source):
@@ -761,7 +775,10 @@
         for k in (0, 1):
             target = here(t).at[y, k, rows] if half == 0 else here(t).at[k, x, rows]
             add_rows(target, one_in_at(t, half).at[k])
-        two_copy(t, half).start()
+        if UNITS[t][0] not in EARLY:
+            two_copy(t, half).start()
+        elif UNITS[t][1] < OWN:
+            z_first(t, half)
 
     def after_two(t, half):
         two_copy(t, half).wait()
@@ -769,11 +786,25 @@
         if UNITS[t][1] < OWN:
             z_first(t, half)
 
+    def own_hop(w, half):
+        t = UNITS.index((w, OWN))
+        z_add(t, half, 0)
+        if w >= 2:
+
+            @pl.when(is_mid)
+            def _():
+                z_add(t, half, 4)
+
+        two_copy(t, half).start()
+
     def finish(w):
         t = UNITS.index((w, OWN))
         for half in HALVES:
-            z_copy(t, half, 0, beside).wait_recv()
-        if w >= 2:
+            if w in EARLY:
+                two_copy(t, half).wait()
+            else:
+                z_copy(t, half, 0, beside).wait_recv()
+        if w >= 2 and w not in EARLY:
 
             @pl.when(is_mid)
             def _():
@@ -783,8 +814,11 @@
         def body(n, carry):
             columns = pl.ds(pl.multiple_of(n * 128, 128), 128)
             first = here(t).at[y, x][:, columns].astype(f32)
-            second = [z_in[w][0, half, :, columns] for half in HALVES]
-            if w >= 2:
+            if w in EARLY:
+                second = [two_in[w][0, half, :, columns] for half in HALVES]
+            else:
+                second = [z_in[w][0, half, :, columns] for half in HALVES]
+            if w >= 2 and w not in EARLY:
                 third = [z_in[w][4, half, :, columns] for half in HALVES]
                 first += jnp.where(is_mid, jnp.concatenate(third, axis=0).astype(f32), 0.0)
             second = jnp.concatenate(second, axis=0).astype(f32)
@@ -921,7 +955,7 @@
     steps = (
         send_own, take, corner, cross, whole, start_load, wait_load, enter, project_attend, branches, send_cotangent,
         swap_came, widen, narrow_back, widen_back, narrow, latents_done, residual_back, attend_back, project_back,
-        turn, produce, join, after_one, after_two, z_pass, finish, inputs_back, norm_hop, norms_out, points_back,
+        turn, produce, join, after_one, after_two, z_pass, own_hop, finish, inputs_back, norm_hop, norms_out, points_back,
     )
     cotangent_load.start()
     output_load(None).start()
@@ -977,8 +1011,8 @@
     counts = (2, 2, 4, 4)
     scratch += [vmem_of((counts[w], 2, 2, BLOCK, WIDTHS[w]), bf16) for w in range(4)]
     scratch += [vmem_of((counts[w], 2, 2, HALF, WIDTHS[w]), bf16) for w in range(4)]
-    scratch += [vmem_of((counts[w], 2, HALF, WIDTHS[w]), bf16) for w in range(4)]
-    scratch += [vmem_of((1 if w < 2 else 5, 2, HALF, WIDTHS[w]), bf16) for w in range(4)]
+    scratch += [vmem_of((1 if w in EARLY else counts[w], 2, HALF, WIDTHS[w]), bf16) for w in range(4)]
+    scratch += [vmem_of((1 if w < 2 else 5, 2) + ((2,) if w in EARLY else ()) + (HALF, WIDTHS[w]), bf16) for w in range(4)]
     scratch += [vmem_of((n, 4, D), f32) for n in (4, 3, 4)]
     dma = pltpu.SemaphoreType.DMA
     units = len(UNITS)

time: 164 us -> 158 us (0.963)
  Pallas kernels: 163 us -> 157 us
    pallas_call x1, Pallas kernels: 155 us -> 149 us  [run_step(): pl.pallas_call(step_kernel, out_shape=out_shape, in_specs=[anywhere] * 5...]
where the time goes in v6:
time: 158 us
  Pallas kernels  157 us (99%)
    pallas_call x1, Pallas kernels, run_step(): pl.pallas_call(step_kernel, out_shape=out_shape, in_specs=[anywhere] * 5...  149 us
    pallas_call x1, Pallas kernels, run_update(): pl.pallas_call(update_kernel, out_shape=[jax.ShapeDtypeStruct(*a) for a i...  8.28 us

profile of v6, /device:TPU:0, one launch (start us, length us, event | category | flops | bytes accessed | tf_op | source)
XLA Modules:
  0.0 158.1 jit_solution(17650068275110071414)
XLA Ops:
  0.7 148.9 %step.1 = (bf16[1024,128]{1,0:T(8,128)(2,1)}, bf16[128,1024]{1,0:T(8,128)(2,1)}, f32[256,128]{1,0:T(8,128)}, f32[3,128,256]{2,1,0:T(8,128)}, bf16[1024,128]{1,0:...) custom-call(bf16[3,1024,256]{2,1,0:T(8,128)(2,1)} %bitcast.9, ...), custom_call_target="tpu_custom_call" | custom-call | tf_op jit(solution)/shard_map/step/pallas_call | solution.py:1023
  149.6 8.3 %update.1 = (f32[256,1024]{1,0:T(8,128)}, f32[256,1024]{1,0:T(8,128)}, f32[3,128,256]{2,1,0:T(8,128)}, f32[3,128,256]{2,1,0:T(8,128)}, f32[3,128,256]{2,1,0:T(8,...) custom-call(f32[3,128,256]{2,1,0:T(8,128)} %get-tuple-element.63.ref, ...), custom_call_target="tpu_custom_call" | custom-call | tf_op jit(solution)/shard_map/update/pallas_call | solution.py:1098

commit v7 on v6

--- a/solution.py
+++ b/solution.py
@@ -292,33 +292,33 @@
     LAST, FINISH, INPUTS, NORM, NORMS_OUT, POINTS,
 ) = range(32)
 SCHEDULE = (
-    (SEND_OWN, 0), (LOAD, 0), (SEND_OWN, 1), (ENTER,), (TAKE, 0, 0, 0), (TAKE, 0, 1, 0), (TAKE, 0, 0, 1),
-    (TAKE, 0, 1, 1), (TAKE, 1, 0, 1), (TAKE, 1, 0, 0), (TAKE, 0, 2, 0), (SEND_OWN, 2), (CORNER, 0, 0, 1),
-    (CORNER, 0, 1, 0), (CORNER, 0, 2, 0), (CORNER, 1, 0, 1), (CORNER, 0, 1, 1), (TAKE, 1, 1, 0), (TAKE, 0, 2, 1),
-    (CROSS, 0, 0, 1), (CORNER, 0, 0, 0), (TAKE, 1, 1, 1), (TAKE, 1, 2, 1), (PROJECT, 0), (CORNER, 1, 0, 0),
-    (CROSS, 0, 1, 0), (TAKE, 1, 2, 0), (SEND_OWN, 3), (CORNER, 0, 2, 1), (CROSS, 0, 1, 1), (CORNER, 1, 2, 0),
-    (CORNER, 1, 1, 0), (CROSS, 1, 0, 1), (CROSS, 0, 2, 0), (LOAD, 4), (SEND_COTANGENT,), (CROSS, 0, 0, 0),
-    (CORNER, 1, 1, 1), (CORNER, 1, 2, 1), (WHOLE, 0, 0), (LOAD, 1), (CROSS, 0, 2, 1), (CROSS, 1, 0, 0),
-    (TAKE, 2, 0, 1), (TAKE, 2, 0, 0), (WHOLE, 0, 1), (TAKE, 3, 0, 0), (READY, 4), (CROSS, 1, 2, 0), (WHOLE, 0, 2),
-    (LOAD, 2), (LOAD, 3), (PROJECT, 1), (TAKE, 3, 0, 1), (CROSS, 1, 1, 1), (CROSS, 1, 1, 0), (CROSS, 1, 2, 1),
-    (PROJECT, 2), (LOAD, 6), (WHOLE, 1, 0), (WHOLE, 1, 2), (CORNER, 2, 0, 1), (WHOLE, 1, 1), (CORNER, 2, 0, 0),
-    (PROJECT, 3), (BRANCH,), (WIDEN, 0, 0), (CORNER, 3, 0, 0), (CAME, 0), (CORNER, 3, 0, 1), (READY, 6),
-    (CROSS, 2, 0, 0), (CROSS, 2, 0, 1), (NARROW_BACK, 0, 0), (WHOLE, 2, 0), (LOAD, 5), (TURN, 0), (CROSS, 3, 0, 0),
-    (CROSS, 3, 0, 1), (READY, 5), (WIDEN, 1, 0), (CAME, 1), (WIDEN, 1, 1), (PRODUCE, 0), (WIDEN, 0, 1), (WHOLE, 3, 0),
-    (LOAD, 7), (PRODUCE, 1), (JOIN, 0), (READY, 7), (NARROW_BACK, 1, 1), (NARROW_BACK, 0, 1), (WIDEN_BACK, 1),
-    (JOIN, 1), (NARROW_BACK, 1, 0), (TURN, 1), (PRODUCE, 2), (ONE, 0, 0), (PRODUCE, 3), (ONE, 0, 1), (NARROW, 1),
-    (JOIN, 2), (TURN, 3), (JOIN, 3), (WIDEN_BACK, 0), (RESIDUAL,), (TWO, 0, 1), (ATTEND, 4), (ONE, 2, 1), (ONE, 2, 0),
-    (PRODUCE, 4), (ATTEND, 5), (TWO, 0, 0), (JOIN, 4), (PRODUCE, 5), (ATTEND, 7), (TWO, 2, 1), (JOIN, 5), (TWO, 2, 0),
-    (ATTEND, 6), (PRODUCE, 6), (PRODUCE, 7), (ONE, 3, 1), (LOAD, 8), (LOAD, 9), (ONE, 4, 0), (TURN, 2), (JOIN, 6),
-    (PRODUCE, 8), (INWARD, 8), (PRODUCE, 9), (JOIN, 8), (ONE, 4, 1), (NARROW, 0), (JOIN, 9), (LOAD, 10), (ONE, 5, 0),
-    (PRODUCE, 10), (ONE, 1, 0), (ONE, 5, 1), (INWARD, 9), (LOAD, 11), (ALONG, 4, 0), (ONE, 1, 1), (TWO, 3, 1),
-    (ONE, 8, 1), (PRODUCE, 11), (INWARD, 10), (INWARD, 11), (JOIN, 11), (ONE, 6, 0), (ALONG, 4, 1), (JOIN, 10),
-    (INPUTS,), (ONE, 8, 0), (ALONG, 6, 0), (TWO, 1, 0), (ALONG, 5, 0), (ONE, 9, 0), (JOIN, 7), (ONE, 10, 0),
-    (TWO, 8, 0), (NORM, 0), (ONE, 9, 1), (TWO, 8, 1), (TWO, 1, 1), (ONE, 10, 1), (ONE, 3, 0), (ALONG, 5, 1),
-    (ONE, 6, 1), (ONE, 11, 1), (ALONG, 6, 1), (TWO, 9, 0), (POINTS,), (ONE, 7, 1), (NORM, 1), (TWO, 9, 1),
-    (FINISH, 0), (TWO, 10, 0), (ALONG, 8, 1), (ONE, 7, 0), (ONE, 11, 0), (TWO, 10, 1), (LAST, 3, 0), (ALONG, 8, 0),
-    (LATENTS,), (NORM, 2), (TWO, 3, 0), (FINISH, 1), (TWO, 11, 1), (LAST, 3, 1), (ALONG, 10, 1), (ALONG, 9, 0),
-    (ALONG, 10, 0), (ALONG, 9, 1), (NORMS_OUT,), (TWO, 11, 0), (FINISH, 2), (FINISH, 3),
+    (SEND_OWN, 0), (SEND_OWN, 1), (TAKE, 0, 1, 0), (TAKE, 0, 0, 0), (TAKE, 0, 0, 1), (TAKE, 0, 1, 1), (TAKE, 1, 0, 1),
+    (TAKE, 0, 2, 0), (TAKE, 1, 0, 0), (CORNER, 0, 0, 1), (CORNER, 0, 1, 0), (SEND_OWN, 2), (CORNER, 0, 1, 1),
+    (CORNER, 0, 2, 0), (TAKE, 0, 2, 1), (CORNER, 0, 0, 0), (TAKE, 1, 1, 1), (LOAD, 0), (TAKE, 1, 1, 0),
+    (TAKE, 1, 2, 1), (TAKE, 1, 2, 0), (SEND_OWN, 3), (CORNER, 1, 0, 1), (CORNER, 1, 0, 0), (ENTER,),
+    (CORNER, 0, 2, 1), (SEND_COTANGENT,), (CROSS, 0, 0, 1), (CROSS, 0, 1, 1), (CROSS, 0, 1, 0), (PROJECT, 0),
+    (CORNER, 1, 2, 0), (CROSS, 0, 0, 0), (CORNER, 1, 1, 1), (LOAD, 4), (CORNER, 1, 1, 0), (CROSS, 1, 0, 1),
+    (CORNER, 1, 2, 1), (CROSS, 0, 2, 0), (TAKE, 2, 0, 0), (WHOLE, 0, 0), (LOAD, 1), (TAKE, 2, 0, 1), (WHOLE, 0, 1),
+    (CROSS, 0, 2, 1), (CROSS, 1, 2, 0), (TAKE, 3, 0, 0), (LOAD, 2), (WHOLE, 0, 2), (CROSS, 1, 1, 1), (CROSS, 1, 0, 0),
+    (PROJECT, 1), (LOAD, 3), (CROSS, 1, 1, 0), (READY, 4), (TAKE, 3, 0, 1), (PROJECT, 2), (LOAD, 6), (CROSS, 1, 2, 1),
+    (CORNER, 2, 0, 1), (CORNER, 2, 0, 0), (WHOLE, 1, 0), (PROJECT, 3), (WHOLE, 1, 1), (WHOLE, 1, 2), (BRANCH,),
+    (CORNER, 3, 0, 1), (CORNER, 3, 0, 0), (WIDEN, 0, 0), (CAME, 0), (READY, 6), (CROSS, 2, 0, 1), (CROSS, 2, 0, 0),
+    (NARROW_BACK, 0, 0), (TURN, 0), (WHOLE, 2, 0), (LOAD, 5), (CROSS, 3, 0, 1), (READY, 5), (WIDEN, 1, 0),
+    (CROSS, 3, 0, 0), (CAME, 1), (WIDEN, 1, 1), (PRODUCE, 0), (WHOLE, 3, 0), (WIDEN, 0, 1), (LOAD, 7), (PRODUCE, 1),
+    (JOIN, 0), (READY, 7), (NARROW_BACK, 0, 1), (NARROW_BACK, 1, 1), (WIDEN_BACK, 1), (JOIN, 1), (TURN, 1),
+    (NARROW_BACK, 1, 0), (ONE, 0, 1), (PRODUCE, 2), (ONE, 0, 0), (PRODUCE, 3), (NARROW, 1), (JOIN, 2), (JOIN, 3),
+    (TURN, 3), (WIDEN_BACK, 0), (TWO, 0, 1), (RESIDUAL,), (TWO, 0, 0), (ATTEND, 4), (PRODUCE, 4), (ONE, 2, 0),
+    (ONE, 2, 1), (ATTEND, 5), (PRODUCE, 5), (JOIN, 4), (ATTEND, 7), (TWO, 2, 1), (JOIN, 5), (TWO, 2, 0), (ATTEND, 6),
+    (TURN, 2), (ONE, 1, 0), (PRODUCE, 6), (ONE, 4, 0), (ONE, 3, 1), (PRODUCE, 7), (PRODUCE, 8), (JOIN, 6),
+    (ONE, 4, 1), (JOIN, 8), (LOAD, 8), (LOAD, 9), (ONE, 1, 1), (PRODUCE, 9), (PRODUCE, 10), (ONE, 5, 0), (TWO, 1, 0),
+    (ALONG, 4, 0), (PRODUCE, 11), (NARROW, 0), (JOIN, 9), (INWARD, 8), (JOIN, 11), (LOAD, 10), (LOAD, 11),
+    (ONE, 5, 1), (ALONG, 4, 1), (INWARD, 9), (ONE, 8, 0), (INWARD, 10), (JOIN, 10), (ONE, 8, 1), (INWARD, 11),
+    (JOIN, 7), (ALONG, 5, 0), (ONE, 9, 0), (ONE, 6, 0), (ALONG, 6, 0), (ONE, 9, 1), (TWO, 8, 0), (INPUTS,),
+    (TWO, 8, 1), (ALONG, 5, 1), (ONE, 10, 1), (NORM, 0), (ONE, 6, 1), (TWO, 1, 1), (ONE, 10, 0), (ONE, 3, 0),
+    (ALONG, 6, 1), (NORM, 1), (TWO, 9, 0), (ONE, 7, 1), (FINISH, 0), (ONE, 11, 1), (ONE, 7, 0), (TWO, 3, 1),
+    (ALONG, 8, 0), (TWO, 9, 1), (ONE, 11, 0), (ALONG, 8, 1), (TWO, 10, 1), (LAST, 3, 0), (TWO, 3, 0), (TWO, 10, 0),
+    (TWO, 11, 1), (LATENTS,), (NORM, 2), (LAST, 3, 1), (ALONG, 10, 0), (ALONG, 10, 1), (ALONG, 9, 0), (TWO, 11, 0),
+    (ALONG, 9, 1), (FINISH, 1), (POINTS,), (FINISH, 2), (NORMS_OUT,), (FINISH, 3),
 )
 NN = ((1,), (0,))
 NT = ((1,), (1,))
@@ -1035,6 +1035,7 @@
 
 
 UPDATES = ((3, D ** (-0.5)), (2, max(1, D * 4 // LAT) ** (-0.5)), (1, D ** (-0.5)), (0, FF ** (-0.5)))
+ORDER = (2, 3, 0, 1)
 
 
 def update_kernel(*refs):
@@ -1045,15 +1046,22 @@
     loads += [pltpu.make_async_copy(a, b, in_sem.at[20 + n]) for n, (a, b) in enumerate(zip(passed, rows_here))]
     stores = [pltpu.make_async_copy(a, b, out_sem.at[n]) for n, (a, b) in enumerate(zip(new, new_out))]
     stores += [pltpu.make_async_copy(a, b, out_sem.at[20 + n]) for n, (a, b) in enumerate(zip(rows_here, passed_out))]
-    for copy in loads:
-        copy.start()
+    for n in (20, 21):
+        loads[n].start()
+    for n in ORDER:
+        for copy in loads[5 * n : 5 * n + 5]:
+            copy.start()
+    for n in (20, 21):
+        loads[n].wait()
+        stores[n].start()
     columns = pl.ds(pl.multiple_of(lax.axis_index("dp") * BLOCK, BLOCK), BLOCK)
     gradient = norm_sum[:, columns]
     norm_out[0][...] = gradient
     results = adamw_step(norms[:, columns], gradient, norm_first[...], norm_second[...], 0.2)
     for n in range(3):
         norm_out[1 + n][...] = results[n]
-    for n, (_, rate) in enumerate(UPDATES):
+    for n in ORDER:
+        rate = UPDATES[n][1]
         for copy in loads[5 * n : 5 * n + 5]:
             copy.wait()
         first, second, master, one, two = here[5 * n : 5 * n + 5]
@@ -1080,9 +1088,6 @@
         lax.fori_loop(0, first.shape[-2] // strip, step, 0)
         for copy in stores[5 * n : 5 * n + 5]:
             copy.start()
-    for n in (20, 21):
-        loads[n].wait()
-        stores[n].start()
     for copy in stores:
         copy.wait()
 

time: 158 us -> 157 us (level)
    pallas_call x1, Pallas kernels: 149 us -> 147 us  [run_step(): pl.pallas_call(step_kernel, out_shape=out_shape, in_specs=[anywhere] * 5...]
where the time goes in v7:
time: 157 us; the launch traced here: 156 us
  Pallas kernels  156 us (99%)
    pallas_call x1, Pallas kernels, run_step(): pl.pallas_call(step_kernel, out_shape=out_shape, in_specs=[anywhere] * 5...  147 us
    pallas_call x1, Pallas kernels, run_update(): pl.pallas_call(update_kernel, out_shape=[jax.ShapeDtypeStruct(*a) for a i...  8.38 us

profile of v7, /device:TPU:0, one launch (start us, length us, event | category | flops | bytes accessed | tf_op | source)
XLA Modules:
  0.0 156.4 jit_solution(18243919144211933400)
XLA Ops:
  0.7 147.2 %step.1 = (bf16[1024,128]{1,0:T(8,128)(2,1)}, bf16[128,1024]{1,0:T(8,128)(2,1)}, f32[256,128]{1,0:T(8,128)}, f32[3,128,256]{2,1,0:T(8,128)}, bf16[1024,128]{1,0:...) custom-call(bf16[3,1024,256]{2,1,0:T(8,128)(2,1)} %bitcast.9, ...), custom_call_target="tpu_custom_call" | custom-call | tf_op jit(solution)/shard_map/step/pallas_call | solution.py:1023
  147.9 8.4 %update.1 = (f32[256,1024]{1,0:T(8,128)}, f32[256,1024]{1,0:T(8,128)}, f32[3,128,256]{2,1,0:T(8,128)}, f32[3,128,256]{2,1,0:T(8,128)}, f32[3,128,256]{2,1,0:T(8,...) custom-call(f32[3,128,256]{2,1,0:T(8,128)} %get-tuple-element.63.ref, ...), custom_call_target="tpu_custom_call" | custom-call | tf_op jit(solution)/shard_map/update/pallas_call | solution.py:1103

commit v8 on v7

--- a/solution.py
+++ b/solution.py
@@ -1046,14 +1046,11 @@
     loads += [pltpu.make_async_copy(a, b, in_sem.at[20 + n]) for n, (a, b) in enumerate(zip(passed, rows_here))]
     stores = [pltpu.make_async_copy(a, b, out_sem.at[n]) for n, (a, b) in enumerate(zip(new, new_out))]
     stores += [pltpu.make_async_copy(a, b, out_sem.at[20 + n]) for n, (a, b) in enumerate(zip(rows_here, passed_out))]
-    for n in (20, 21):
-        loads[n].start()
     for n in ORDER:
         for copy in loads[5 * n : 5 * n + 5]:
             copy.start()
     for n in (20, 21):
-        loads[n].wait()
-        stores[n].start()
+        loads[n].start()
     columns = pl.ds(pl.multiple_of(lax.axis_index("dp") * BLOCK, BLOCK), BLOCK)
     gradient = norm_sum[:, columns]
     norm_out[0][...] = gradient
@@ -1088,6 +1085,9 @@
         lax.fori_loop(0, first.shape[-2] // strip, step, 0)
         for copy in stores[5 * n : 5 * n + 5]:
             copy.start()
+    for n in (20, 21):
+        loads[n].wait()
+        stores[n].start()
     for copy in stores:
         copy.wait()
 

time: 157 us -> 156 us (level)
  no operation moved by 1% of the time
where the time goes in v8:
time: 156 us
  Pallas kernels  155 us (99%)
    pallas_call x1, Pallas kernels, run_step(): pl.pallas_call(step_kernel, out_shape=out_shape, in_specs=[anywhere] * 5...  147 us
    pallas_call x1, Pallas kernels, run_update(): pl.pallas_call(update_kernel, out_shape=[jax.ShapeDtypeStruct(*a) for a i...  7.54 us

profile of v8, /device:TPU:0, one launch (start us, length us, event | category | flops | bytes accessed | tf_op | source)
XLA Modules:
  0.0 155.6 jit_solution(6575630327010882157)
XLA Ops:
  0.7 147.2 %step.1 = (bf16[1024,128]{1,0:T(8,128)(2,1)}, bf16[128,1024]{1,0:T(8,128)(2,1)}, f32[256,128]{1,0:T(8,128)}, f32[3,128,256]{2,1,0:T(8,128)}, bf16[1024,128]{1,0:...) custom-call(bf16[3,1024,256]{2,1,0:T(8,128)(2,1)} %bitcast.9, ...), custom_call_target="tpu_custom_call" | custom-call | tf_op jit(solution)/shard_map/step/pallas_call | solution.py:1023
  147.9 7.5 %update.1 = (f32[256,1024]{1,0:T(8,128)}, f32[256,1024]{1,0:T(8,128)}, f32[3,128,256]{2,1,0:T(8,128)}, f32[3,128,256]{2,1,0:T(8,128)}, f32[3,128,256]{2,1,0:T(8,...) custom-call(f32[3,128,256]{2,1,0:T(8,128)} %get-tuple-element.63.ref, ...), custom_call_target="tpu_custom_call" | custom-call | tf_op jit(solution)/shard_map/update/pallas_call | solution.py:1103
